TPU v7x, 32 devices: a whole 2x2x4 slice. The times are simulated.
32 devices in a mesh: row: 4 (over z), col: 8 (over y, x, core).
Axes of the slice: x: 2, y: 2, z: 4, core: 2. Of those that a mesh axis runs over, the one named last changes fastest.
Arguments:
- right_side: float32 [64, 16384], P(None, ('row', 'col')), may hold values from -80 to 80
- diag_vals: float32 [16384], P(('row', 'col')), may hold values from 1.05 to 1.6
- tiles: bfloat16 [64, 16, 256, 256], P(('row', 'col')), may hold values from -1 to 1, as said below
- col_ids: int32 [64, 16], P(('row', 'col')), may hold values from 0 to 63, as said below
Outputs:
- solution: float32 [64, 16384], P(None, ('row', 'col'))
- residual: float32 [64, 16384], P(None, ('row', 'col'))
Inputs may be any that keep to these rules, and one draw needn't show every extreme that they name: col_ids[i, m] = (i + o_m) mod 64 and col_ids[i, 8 + m] = (i - o_m) mod 64 for 8 distinct odd offsets o_m shared by all block-rows, each below 32. The pattern is symmetric. tiles[i, m] is the block in block-row i and block-column col_ids[i, m]; tiles[i, 8 + m] is the transpose of tiles[(i - o_m) mod 64, m], so the matrix is symmetric.
All inputs are finite; a program needn't handle non-finite values.
Results may differ from a plain program's by a relative error of at most 0.00062.
Values may be sent and summed in bfloat16 or wider, within the bound.
No kernel may reach another device: no remote copies, remote signals or barrier semaphores. Data moves between devices by JAX's collectives and lax.ppermute only.
A program may use at most 64 MiB of HBM per device.

v0:
```python
import jax
import jax.numpy as jnp
from jax import lax
from jax.sharding import PartitionSpec as P

ITERS = 4


def chol_solve(mat, rhs):
    lower = jnp.linalg.cholesky(mat)
    half = lax.linalg.triangular_solve(lower, rhs, left_side=True, lower=True)
    return lax.linalg.triangular_solve(lower, half, left_side=True, lower=True, transpose_a=True)


def gram_of(left, right):
    return jnp.dot(
        left, right.T, precision=lax.Precision.HIGHEST, preferred_element_type=jnp.float32
    )


def small_dot(left, right):
    return jnp.dot(left, right, precision=lax.Precision.HIGHEST, preferred_element_type=jnp.float32)


def apply_matrix(vec, diag_vals, tiles, col_ids):
    rhs_count = vec.shape[0]
    rows_here = tiles.shape[0]
    nbr = tiles.shape[1]
    blk = tiles.shape[2]
    rounded = vec.astype(jnp.bfloat16).reshape(rhs_count, rows_here, blk)
    whole = lax.all_gather(
        rounded.reshape(rhs_count, rows_here * blk), ("row", "col"), axis=1, tiled=True
    )
    whole = whole.reshape(rhs_count, -1, blk)
    picked = jnp.take(whole, col_ids.reshape(-1), axis=1).reshape(rhs_count, rows_here, nbr, blk)
    off = jnp.einsum("srkb,rkab->sra", picked, tiles, preferred_element_type=jnp.float32)
    coef = 1.0 / (nbr * blk)
    return diag_vals[None, :] * vec + coef * off.reshape(rhs_count, rows_here * blk)


def body(right_side, diag_vals, tiles, col_ids):
    solution = jnp.zeros_like(right_side)
    residual = right_side
    direction = right_side
    gram = lax.psum(gram_of(residual, residual), ("row", "col"))
    for step in range(ITERS):
        image = apply_matrix(direction, diag_vals, tiles, col_ids)
        curv = lax.psum(gram_of(direction, image), ("row", "col"))
        alpha = chol_solve(curv, gram)
        solution = solution + small_dot(alpha.T, direction)
        residual = residual - small_dot(alpha.T, image)
        if step + 1 < ITERS:
            gram_new = lax.psum(gram_of(residual, residual), ("row", "col"))
            beta = chol_solve(gram, gram_new)
            direction = residual + small_dot(beta.T, direction)
            gram = gram_new
    return (solution, residual)


def solution(mesh):
    placed = (
        P(None, ("row", "col")),
        P(("row", "col")),
        P(("row", "col"), None, None, None),
        P(("row", "col"), None),
    )
    return jax.shard_map(
        body,
        mesh=mesh,
        in_specs=placed,
        out_specs=(P(None, ("row", "col")), P(None, ("row", "col"))),
        check_vma=False,
    )
```

profile of v0, /device:TPU:0, one launch (start us, length us, event | category | flops | bytes accessed | tf_op | source)
XLA Modules:
  0.0 618.0 jit_solution(6379712227797717869)
XLA Ops:
  10.9 58.3 %all-gather.5.cloned.1.call-done = bf16[64,16384]{1,0:T(8,128)(2,1)} async-done(((bf16[64,512]{1,0:T(8,128)(2,1)}), bf16[64,16384]{1,0:T(8,128)(2,1)}) %all-gather.5.cloned.1.call-update) | async-done | bytes 2097168 | tf_op jit(solution)/shard_map/all_gather | solution.py:31
  75.8 40.2 %all-reduce = (f32[64,64]{0,1:T(8,128)S(1)}, f32[64,64]{0,1:T(8,128)S(1)}) all-reduce(f32[64,64]{0,1:T(8,128)S(1)} %fusion.64, f32[64,64]{0,1:T(8,128)S(1)} %convolution_bitcast_fusion.4), channel_id=1, replica_groups=mesh['row'=4,'col'=8] {'row','col'}, use_global_device_ids=true, to_apply=%region_3.6 | all-reduce | flops 8192 | bytes 65536 | tf_op jit(solution)/shard_map/psum | solution.py:45
  116.1 5.8 cholesky.119
  123.3 4.9 custom-call.21
  129.3 39.6 %psum.58 = f32[64,64]{0,1:T(8,128)S(1)} all-reduce(f32[64,64]{0,1:T(8,128)S(1)} %fusion.66), channel_id=1, replica_groups=mesh['row'=4,'col'=8] {'row','col'}, use_global_device_ids=true, to_apply=%region_4.9 | all-reduce | flops 4096 | bytes 32768 | tf_op jit(solution)/shard_map/psum | solution.py:53
  168.9 5.8 cholesky.130
  182.5 5.8 cholesky.152
  189.7 5.5 custom-call.27
  195.2 42.8 %all-gather.7.cloned.1.call-done = bf16[64,16384]{1,0:T(8,128)(2,1)} async-done(((bf16[64,512]{1,0:T(8,128)(2,1)}), bf16[64,16384]{1,0:T(8,128)(2,1)}) %all-gather.7.cloned.1.call-update) | async-done | bytes 2097168 | tf_op jit(solution)/shard_map/all_gather | solution.py:31
  244.6 40.0 %psum.59 = f32[64,64]{0,1:T(8,128)S(1)} all-reduce(f32[64,64]{0,1:T(8,128)S(1)} %fusion.8), channel_id=1, replica_groups=mesh['row'=4,'col'=8] {'row','col'}, use_global_device_ids=true, to_apply=%region_5.10 | all-reduce | flops 4096 | bytes 32768 | tf_op jit(solution)/shard_map/psum | solution.py:48
  284.7 5.8 cholesky.141
  291.9 4.9 custom-call.25
  297.8 39.6 %psum.60 = f32[64,64]{0,1:T(8,128)S(1)} all-reduce(f32[64,64]{0,1:T(8,128)S(1)} %fusion.67), channel_id=1, replica_groups=mesh['row'=4,'col'=8] {'row','col'}, use_global_device_ids=true, to_apply=%region_6.11 | all-reduce | flops 4096 | bytes 32768 | tf_op jit(solution)/shard_map/psum | solution.py:53
  339.0 5.8 cholesky.174
  346.1 5.5 custom-call.31
  351.6 42.8 %all-gather.9.cloned.1.call-done = bf16[64,16384]{1,0:T(8,128)(2,1)} async-done(((bf16[64,512]{1,0:T(8,128)(2,1)}), bf16[64,16384]{1,0:T(8,128)(2,1)}) %all-gather.9.cloned.1.call-update) | async-done | bytes 2097168 | tf_op jit(solution)/shard_map/all_gather | solution.py:31
  401.1 39.8 %psum.61 = f32[64,64]{0,1:T(8,128)S(1)} all-reduce(f32[64,64]{0,1:T(8,128)S(1)} %fusion.9), channel_id=1, replica_groups=mesh['row'=4,'col'=8] {'row','col'}, use_global_device_ids=true, to_apply=%region_7.12 | all-reduce | flops 4096 | bytes 32768 | tf_op jit(solution)/shard_map/psum | solution.py:48
  441.0 5.8 cholesky.163
  448.2 4.9 custom-call.29
  454.1 39.9 %psum.62 = f32[64,64]{1,0:T(8,128)S(1)} all-reduce(f32[64,64]{1,0:T(8,128)S(1)} %fusion.68), channel_id=1, replica_groups=mesh['row'=4,'col'=8] {'row','col'}, use_global_device_ids=true, to_apply=%region_8.13 | all-reduce | flops 4096 | bytes 32768 | tf_op jit(solution)/shard_map/psum | solution.py:53
  496.4 54.1 %all-gather.11.cloned.1.call-done = bf16[64,16384]{1,0:T(8,128)(2,1)} async-done(((bf16[64,512]{1,0:T(8,128)(2,1)}), bf16[64,16384]{1,0:T(8,128)(2,1)}) %all-gather.11.cloned.1.call-update) | async-done | bytes 2097168 | tf_op jit(solution)/shard_map/all_gather | solution.py:31
  557.1 39.8 %psum.63 = f32[64,64]{0,1:T(8,128)S(1)} all-reduce(f32[64,64]{0,1:T(8,128)S(1)} %fusion.10), channel_id=1, replica_groups=mesh['row'=4,'col'=8] {'row','col'}, use_global_device_ids=true, to_apply=%region_9.14 | all-reduce | flops 4096 | bytes 32768 | tf_op jit(solution)/shard_map/psum | solution.py:48
  597.0 5.8 cholesky.185
  604.2 4.9 custom-call.33
  (133 shorter events, 54.8 us)
Async XLA Ops:
  7.2 62.0 %all-gather.5.cloned.1.call-start = ((), (), s32[]{:S(2)}) async-start(), calls=%async_computation | async-start | bytes 2162688 | tf_op jit(solution)/shard_map/all_gather | solution.py:31
  8.8 229.2 %all-gather.7.cloned.1.call-start = ((), (), s32[]{:S(2)}) async-start(), calls=%async_computation.1 | async-start | bytes 2162688 | tf_op jit(solution)/shard_map/all_gather | solution.py:31
  71.7 3.8 copy-start
  71.7 3.8 copy-start.13
  128.6 109.4 %copy-start.9 = (f32[64,64]{1,0:T(8,128)}, f32[64,64]{1,0:T(8,128)S(1)}, u32[]{:S(2)}) copy-start(f32[64,64]{1,0:T(8,128)S(1)} %fusion.58) | copy-start | bytes 49156
  168.9 71.0 %copy-start.3 = (f32[64,64]{0,1:T(8,128)}, f32[64,64]{0,1:T(8,128)S(1)}, u32[]{:S(2)}) copy-start(f32[64,64]{0,1:T(8,128)S(1)} %psum.58) | copy-start | bytes 49156
  182.4 212.1 %all-gather.9.cloned.1.call-start = ((), (), s32[]{:S(2)}) async-start(), calls=%async_computation.2 | async-start | bytes 2162688 | tf_op jit(solution)/shard_map/all_gather | solution.py:31
  240.5 56.3 %copy-start.4 = (f32[64,64]{0,1:T(8,128)S(1)}, f32[64,64]{0,1:T(8,128)}, u32[]{:S(2)}) copy-start(f32[64,64]{0,1:T(8,128)} %copy-done.3) | copy-start | bytes 49156
  240.7 96.8 %copy-start.14 = (f32[1,64,64]{1,2,0:T(8,128)S(1)}, f32[1,64,64]{1,2,0:T(8,128)}, u32[]{:S(2)}) copy-start(f32[1,64,64]{1,2,0:T(8,128)} %custom-call.27) | copy-start | bytes 49156
  297.2 99.1 %copy-start.11 = (f32[64,64]{1,0:T(8,128)}, f32[64,64]{1,0:T(8,128)S(1)}, u32[]{:S(2)}) copy-start(f32[64,64]{1,0:T(8,128)S(1)} %fusion.48) | copy-start | bytes 49156
  297.5 98.8 %copy-start.1 = (f32[64,512]{1,0:T(8,128)}, f32[64,512]{1,0:T(8,128)S(1)}, u32[]{:S(2)}) copy-start(f32[64,512]{1,0:T(8,128)S(1)} %convolution_subtract_fusion.2) | copy-start | bytes 393220
  337.5 57.0 %copy-start.5 = (f32[64,64]{0,1:T(8,128)}, f32[64,64]{0,1:T(8,128)S(1)}, u32[]{:S(2)}) copy-start(f32[64,64]{0,1:T(8,128)S(1)} %psum.60) | copy-start | bytes 49156
  338.9 211.6 %all-gather.11.cloned.1.call-start = ((), (), s32[]{:S(2)}) async-start(), calls=%async_computation.3 | async-start | bytes 2162688 | tf_op jit(solution)/shard_map/all_gather | solution.py:31
  397.0 56.1 %copy-start.6 = (f32[64,64]{0,1:T(8,128)S(1)}, f32[64,64]{0,1:T(8,128)}, u32[]{:S(2)}) copy-start(f32[64,64]{0,1:T(8,128)} %copy-done.5) | copy-start | bytes 49156
  397.0 56.5 %copy-start.2 = (f32[64,512]{1,0:T(8,128)S(1)}, f32[64,512]{1,0:T(8,128)}, u32[]{:S(2)}) copy-start(f32[64,512]{1,0:T(8,128)} %copy-done.1) | copy-start | bytes 393220
  397.2 96.8 %copy-start.15 = (f32[1,64,64]{1,2,0:T(8,128)S(1)}, f32[1,64,64]{1,2,0:T(8,128)}, u32[]{:S(2)}) copy-start(f32[1,64,64]{1,2,0:T(8,128)} %custom-call.31) | copy-start | bytes 49156
  397.2 98.2 %copy-start.10 = (f32[64,64]{1,0:T(8,128)S(1)}, f32[64,64]{1,0:T(8,128)}, u32[]{:S(2)}) copy-start(f32[64,64]{1,0:T(8,128)} %copy-done.9) | copy-start | bytes 49156
  397.2 98.6 %copy-start.12 = (f32[64,64]{1,0:T(8,128)S(1)}, f32[64,64]{1,0:T(8,128)}, u32[]{:S(2)}) copy-start(f32[64,64]{1,0:T(8,128)} %copy-done.11) | copy-start | bytes 49156
  494.0 1.4 copy-start.7
  553.0 56.1 %copy-start.8 = (f32[64,64]{1,0:T(8,128)S(1)}, f32[64,64]{1,0:T(8,128)}, u32[]{:S(2)}) copy-start(f32[64,64]{1,0:T(8,128)} %copy-done.7) | copy-start | bytes 49156
Sparse Core Ops, SparseCore 0:
  11.5 57.6 all-gather.4
  182.5 55.4 all-gather.6
  339.0 55.4 all-gather.8
  495.5 54.9 all-gather.10
where the time goes:
time: 619 us; the launch traced here: 618 us
  blocking collectives  279 us (45%)
  waiting for transfers between devices  198 us (32%)
  other arithmetic  87.9 us (14%)
  matrix products  26.9 us (4%)
  between operations  14.6 us (2%)
  local copies, waits for them, and re-layouts  11.3 us (2%)
    all_gather x4, waiting for transfers between devices, apply_matrix(): lax.all_gather(rounded.reshape(rhs_count, rows_here * blk), ('row', 'col'...  198 us
    psum x3, blocking collectives, body(): curv = lax.psum(gram_of(direction, image), ('row', 'col'))  120 us
    psum x3, blocking collectives, body(): gram_new = lax.psum(gram_of(residual, residual), ('row', 'col'))  119 us
    another operation x21, other arithmetic, chol_solve(): lower = jnp.linalg.cholesky(mat)  45.6 us
    psum x1, blocking collectives, body(): gram = lax.psum(gram_of(residual, residual), ('row', 'col'))  40.2 us
    another operation x14, other arithmetic, chol_solve(): lax.linalg.triangular_solve(lower, half, left_side=True, lower=True, tran...  40 us
    dot_general x4, matrix products, apply_matrix(): jnp.einsum('srkb,rkab->sra', picked, tiles, preferred_element_type=jnp.fl...  14.3 us
  transfers between devices with their start and end apart: 4, of which 4 were waited for; matrix products, arithmetic and copies ran while one was open for 5% of the time, Pallas kernels for 0%

commit v1 on v0

v1 whole, which is shorter than its diff:
```python
import functools

import jax
import jax.numpy as jnp
from jax import lax
from jax.experimental import pallas as pl
from jax.experimental.pallas import tpu as pltpu
from jax.sharding import PartitionSpec as P

ITERS = 4
AXES = ("row", "col")
HIGH = lax.Precision.HIGHEST


def nn(left, right):
    return lax.dot_general(
        left, right, (((1,), (0,)), ((), ())), precision=HIGH, preferred_element_type=jnp.float32
    )


def nt(left, right):
    return lax.dot_general(
        left, right, (((1,), (1,)), ((), ())), precision=HIGH, preferred_element_type=jnp.float32
    )


def xor_permute(val, mask, count):
    return lax.ppermute(val, AXES, [(i, i ^ mask) for i in range(count)])


def total_of(val, masks, count):
    for mask in masks:
        val = val + xor_permute(val, mask, count)
    return val


def gather_of(val, masks, count):
    for mask in masks:
        val = jnp.concatenate([val, xor_permute(val, mask, count)], axis=0)
    return val


def slot_of(diff, masks):
    slot = jnp.zeros_like(diff)
    for place, mask in enumerate(masks):
        slot = slot + jnp.where((diff & mask) != 0, 1 << place, 0)
    return slot


def matrix_kernel(rows, nbr, blk, chunk, slots, whole, tiles, vec, res, diag, image, grams, held, sems):
    coef = 1.0 / (nbr * blk)
    parts = rows * nbr // chunk
    copies = []
    for part in range(parts):
        row, first = divmod(part * chunk, nbr)
        copies.append(
            pltpu.make_async_copy(
                tiles.at[row, pl.ds(first, chunk)], held.at[pl.ds(part * chunk, chunk)], sems.at[part]
            )
        )
        copies[-1].start()
    for row in range(rows):
        acc = jnp.zeros((vec.shape[0], blk), jnp.float32)
        for k in range(nbr):
            spot = row * nbr + k
            if spot % chunk == 0:
                copies[spot // chunk].wait()
            acc = acc + lax.dot_general(
                whole[slots[spot]],
                held[spot],
                (((1,), (1,)), ((), ())),
                preferred_element_type=jnp.float32,
            )
        cols = pl.ds(row * blk, blk)
        image[:, cols] = diag[:, cols] * vec[:, cols] + coef * acc
    img = image[...]
    n = vec.shape[0]
    both = nt(jnp.concatenate([res[...], img], axis=0), jnp.concatenate([res[...], img], axis=0))
    grams[:, 0:n] = both[0:n, 0:n]
    grams[:, n : 2 * n] = nt(vec[...], img)
    grams[:, 2 * n : 3 * n] = both[0:n, n : 2 * n]
    grams[:, 3 * n : 4 * n] = both[n : 2 * n, n : 2 * n]


def apply_matrix(slots, whole, tiles, vec, res, diag):
    rows, nbr, blk, _ = tiles.shape
    n = vec.shape[0]
    chunk = 4
    space = pltpu.VMEM
    return pl.pallas_call(
        functools.partial(matrix_kernel, rows, nbr, blk, chunk),
        out_shape=(
            jax.ShapeDtypeStruct(vec.shape, jnp.float32),
            jax.ShapeDtypeStruct((n, 4 * n), jnp.float32),
        ),
        in_specs=[
            pl.BlockSpec(memory_space=pltpu.SMEM),
            pl.BlockSpec(memory_space=space),
            pl.BlockSpec(memory_space=pl.ANY),
            pl.BlockSpec(memory_space=space),
            pl.BlockSpec(memory_space=space),
            pl.BlockSpec(memory_space=space),
        ],
        out_specs=(pl.BlockSpec(memory_space=space), pl.BlockSpec(memory_space=space)),
        scratch_shapes=[
            pltpu.VMEM((rows * nbr, blk, blk), tiles.dtype),
            pltpu.SemaphoreType.DMA((rows * nbr // chunk,)),
        ],
        compiler_params=pltpu.CompilerParams(vmem_limit_bytes=40 * 1024 * 1024),
        name="matrix",
    )(slots, whole, tiles, vec, res, diag)


def invert_pair(mats, n):
    rows = lax.broadcasted_iota(jnp.int32, (n, 2 * n), 0)
    lanes = lax.broadcasted_iota(jnp.int32, (n, 2 * n), 1)
    left = lanes < n
    place = jnp.where(left, lanes, lanes - n)
    for j in range(n):
        col = jnp.where(
            left,
            jnp.broadcast_to(mats[:, j : j + 1], (n, 2 * n)),
            jnp.broadcast_to(mats[:, n + j : n + j + 1], (n, 2 * n)),
        )
        pivot = col[j : j + 1, :]
        inv = 1.0 / pivot
        line = mats[j : j + 1, :]
        scaled = jnp.where(place[0:1, :] == j, inv, line * inv)
        kept = jnp.where(place == j, 0.0, mats)
        mats = jnp.where(rows == j, jnp.broadcast_to(scaled, (n, 2 * n)), kept - col * scaled)
    return mats


def solve_kernel(last, grams, other, vec, res, sol, image, *outs):
    n = vec.shape[0]
    full = grams[...] + other[...]
    gram, curv = full[:, 0:n], full[:, n : 2 * n]
    inverses = invert_pair(jnp.concatenate([curv, gram], axis=1), n)
    alpha_t = nn(gram, inverses[:, 0:n])
    old = vec[...]
    new = res[...] - nn(alpha_t, image[...])
    outs[0][...] = sol[...] + nn(alpha_t, old)
    outs[1][...] = new
    if not last:
        cross, square = full[:, 2 * n : 3 * n], full[:, 3 * n : 4 * n]
        mixed = nt(cross, alpha_t)
        gram_new = gram - mixed + nn(alpha_t, nt(square, alpha_t) - cross.T)
        beta_t = nn(gram_new, inverses[:, n : 2 * n])
        step = new + nn(beta_t, old)
        outs[2][...] = step
        blk = outs[3].shape[2]
        for row in range(outs[3].shape[0]):
            outs[3][row] = step[:, row * blk : (row + 1) * blk].astype(jnp.bfloat16)


def solve_step(last, rows, grams, other, vec, res, sol, image):
    shape = jax.ShapeDtypeStruct(vec.shape, jnp.float32)
    n, width = vec.shape
    space = pl.BlockSpec(memory_space=pltpu.VMEM)
    outs = [shape, shape]
    if not last:
        outs += [shape, jax.ShapeDtypeStruct((rows, n, width // rows), jnp.bfloat16)]
    return pl.pallas_call(
        functools.partial(solve_kernel, last),
        out_shape=tuple(outs),
        in_specs=[space] * 6,
        out_specs=tuple([space] * len(outs)),
        name="small_last" if last else "small",
    )(grams, other, vec, res, sol, image)


def body(gather_masks, sum_masks, count, cols, right_side, diag_vals, tiles, col_ids):
    rows, nbr, blk, _ = tiles.shape
    n = right_side.shape[0]
    me = lax.axis_index("row") * cols + lax.axis_index("col")
    ids = col_ids.reshape(-1)
    slots = slot_of(me ^ (ids // rows), gather_masks) * rows + ids % rows
    diag = diag_vals[None, :]
    sol = jnp.zeros_like(right_side)
    res = right_side
    vec = right_side
    rounded = right_side.astype(jnp.bfloat16).reshape(n, rows, blk).transpose(1, 0, 2)
    for step in range(ITERS):
        last = step + 1 == ITERS
        whole = gather_of(rounded, gather_masks, count)
        image, grams = apply_matrix(slots, whole, tiles, vec, res, diag)
        if last:
            grams = grams[:, : 2 * n]
        part = total_of(grams, sum_masks[:-1], count)
        outs = solve_step(last, rows, part, xor_permute(part, sum_masks[-1], count), vec, res, sol, image)
        if last:
            sol, res = outs
        else:
            sol, res, vec, rounded = outs
    return (sol, res)


def solution(mesh):
    placed = (
        P(None, ("row", "col")),
        P(("row", "col")),
        P(("row", "col"), None, None, None),
        P(("row", "col"), None),
    )
    count = mesh.shape["row"] * mesh.shape["col"]
    cols = mesh.shape["col"]
    bits = [1 << i for i in range(count.bit_length() - 1)]
    major = [b for b in bits if b >= cols]
    minor = [b for b in bits if 1 < b < cols]
    return jax.shard_map(
        functools.partial(body, major + minor + [1], bits, count, cols),
        mesh=mesh,
        in_specs=placed,
        out_specs=(P(None, ("row", "col")), P(None, ("row", "col"))),
        check_vma=False,
    )
```

time: 619 us -> 274 us (0.44)
  blocking collectives: 279 us -> 0 us
  other arithmetic: 87.9 us -> 9.01 us
  starting transfers between devices: 0.16 us -> 51.6 us
  waiting for transfers between devices: 198 us -> 147 us
  Pallas kernels: 0 us -> 49.9 us
  matrix products: 26.9 us -> 0 us
  between operations: 14.6 us -> 1.21 us
    psum x7 -> x0, blocking collectives: 279 us -> none  [the longest x3 120 us: body(): curv = lax.psum(gram_of(direction, image), ('row', 'col'))]
    all_gather x4 -> x0, waiting for transfers between devices: 198 us -> none  [apply_matrix(): lax.all_gather(rounded.reshape(rhs_count, rows_here * blk), ('row', 'col'...]
    ppermute x0 -> x40, waiting for transfers between devices: none -> 147 us  [xor_permute(): return lax.ppermute(val, AXES, [(i, i ^ mask) for i in range(count)])]
    another operation x35 -> x0, other arithmetic: 85.6 us -> none  [the longest x21 45.6 us: chol_solve(): lower = jnp.linalg.cholesky(mat)]
    ppermute x0 -> x40, starting transfers between devices: none -> 51.6 us  [xor_permute(): return lax.ppermute(val, AXES, [(i, i ^ mask) for i in range(count)])]
    pallas_call x0 -> x8, Pallas kernels: none -> 49.9 us  [the longest x4 34.5 us: solve_step(): pl.pallas_call(functools.partial(solve_kernel, last), out_shape=tuple(out...]
    dot_general x23 -> x0, matrix products: 24.1 us -> none  [the longest x4 14.3 us: apply_matrix(): jnp.einsum('srkb,rkab->sra', picked, tiles, preferred_element_type=jnp.fl...]
    unnamed x32 -> x66, local copies, waits for them, and re-layouts: 0.11 us -> 12.1 us
  transfers between devices with their start and end apart: 4 -> 40, of which waited for: 4 -> 40; matrix products, arithmetic and copies ran while one was open for 5% -> 2% of each run, Pallas kernels for 0% -> 0%
where the time goes in v1:
time: 274 us; the launch traced here: 273 us
  waiting for transfers between devices  147 us (54%)
  starting transfers between devices  51.6 us (19%)
  Pallas kernels  49.9 us (18%)
  local copies, waits for them, and re-layouts  14.3 us (5%)
  other arithmetic  9.01 us (3%)
    ppermute x40, waiting for transfers between devices, xor_permute(): return lax.ppermute(val, AXES, [(i, i ^ mask) for i in range(count)])  147 us
    ppermute x40, starting transfers between devices, xor_permute(): return lax.ppermute(val, AXES, [(i, i ^ mask) for i in range(count)])  51.6 us
    pallas_call x4, Pallas kernels, solve_step(): pl.pallas_call(functools.partial(solve_kernel, last), out_shape=tuple(out...  34.5 us
    pallas_call x4, Pallas kernels, apply_matrix(): pl.pallas_call(functools.partial(matrix_kernel, rows, nbr, blk, chunk), o...  15.4 us
    unnamed x66, local copies, waits for them, and re-layouts  12.1 us
    concatenate x12, other arithmetic, gather_of(): val = jnp.concatenate([val, xor_permute(val, mask, count)], axis=0)  7.93 us
  transfers between devices with their start and end apart: 40, of which 40 were waited for; matrix products, arithmetic and copies ran while one was open for 2% of the time, Pallas kernels for 0%

profile of v1, /device:TPU:0, one launch (start us, length us, event | category | flops | bytes accessed | tf_op | source)
XLA Modules:
  0.0 273.3 jit_solution(340548880108832565)
XLA Ops:
  10.0 5.2 %collective-permute-done.1 = bf16[4,64,256]{2,1,0:T(8,128)(2,1)S(1)} collective-permute-done((bf16[4,64,256]{2,1,0:T(8,128)(2,1)S(1)}, bf16[4,64,256]{2,1,0:T(8,128)(2,1)S(1)}, u32[]{:S(2)}, u32[]{:S(2)}) %collective-permute-start.1) | collective-permute-done | bytes 131104 | tf_op jit(solution)/shard_map/ppermute | solution.py:28
  16.8 4.8 %collective-permute-done.2 = bf16[8,64,256]{2,1,0:T(8,128)(2,1)S(1)} collective-permute-done((bf16[8,64,256]{2,1,0:T(8,128)(2,1)S(1)}, bf16[8,64,256]{2,1,0:T(8,128)(2,1)S(1)}, u32[]{:S(2)}, u32[]{:S(2)}) %collective-permute-start.2) | collective-permute-done | bytes 262176 | tf_op jit(solution)/shard_map/ppermute | solution.py:28
  26.0 5.9 %collective-permute-done.3 = bf16[16,64,256]{2,1,0:T(8,128)(2,1)S(1)} collective-permute-done((bf16[16,64,256]{2,1,0:T(8,128)(2,1)S(1)}, bf16[16,64,256]{2,1,0:T(8,128)(2,1)S(1)}, u32[]{:S(2)}, u32[]{:S(2)}) %collective-permute-start.3) | collective-permute-done | bytes 524320 | tf_op jit(solution)/shard_map/ppermute | solution.py:28
  57.9 4.1 %collective-permute-start.9 = (f32[64,256]{1,0:T(8,128)S(1)}, f32[64,256]{1,0:T(8,128)S(1)}, u32[]{:S(2)}, u32[]{:S(2)}) collective-permute-start(f32[64,256]{1,0:T(8,128)S(1)} %add.83.grams), channel_id=1, source_target_pairs={{0,16},{1,17},{2,18},{3,19},{4,20},{5,21},{6,22},{7,23},{8,24},{9,... | collective-permute-start | bytes 196616 | tf_op jit(solution)/shard_map/ppermute | solution.py:28
  65.0 8.8 %small.3 = (f32[64,512]{1,0:T(8,128)}, f32[64,512]{1,0:T(8,128)}, f32[64,512]{1,0:T(8,128)}, bf16[2,64,256]{2,1,0:T(8,128)(2,1)}) custom-call(f32[64,256]{1,0:T(8,128)} %copy-done.18, f32[64,256]{1,0:T(8,128)} %copy-done.22, f32[64,512]{1,0:T(8,128)} %res.3, f32[64,512]{1,0:T(8,128)} %res.3, f32[64,512]{1,0:T(8,128)} %broadcast_in_dim.22.sol, ...), custom_call_target="tpu_custom_call" | custom-call | tf_op jit(solution)/shard_map/small/pallas_call | solution.py:163
  75.5 4.0 %collective-permute-done.10 = bf16[2,64,256]{2,1,0:T(8,128)(2,1)S(1)} collective-permute-done((bf16[2,64,256]{2,1,0:T(8,128)(2,1)}, bf16[2,64,256]{2,1,0:T(8,128)(2,1)S(1)}, u32[]{:S(2)}, u32[]{:S(2)}) %collective-permute-start.10) | collective-permute-done | bytes 65568 | tf_op jit(solution)/shard_map/ppermute | solution.py:28
  82.5 5.2 %collective-permute-done.11 = bf16[4,64,256]{2,1,0:T(8,128)(2,1)S(1)} collective-permute-done((bf16[4,64,256]{2,1,0:T(8,128)(2,1)S(1)}, bf16[4,64,256]{2,1,0:T(8,128)(2,1)S(1)}, u32[]{:S(2)}, u32[]{:S(2)}) %collective-permute-start.11) | collective-permute-done | bytes 131104 | tf_op jit(solution)/shard_map/ppermute | solution.py:28
  90.1 4.9 %collective-permute-done.12 = bf16[8,64,256]{2,1,0:T(8,128)(2,1)S(1)} collective-permute-done((bf16[8,64,256]{2,1,0:T(8,128)(2,1)S(1)}, bf16[8,64,256]{2,1,0:T(8,128)(2,1)S(1)}, u32[]{:S(2)}, u32[]{:S(2)}) %collective-permute-start.12) | collective-permute-done | bytes 262176 | tf_op jit(solution)/shard_map/ppermute | solution.py:28
  98.5 6.7 %collective-permute-done.13 = bf16[16,64,256]{2,1,0:T(8,128)(2,1)S(1)} collective-permute-done((bf16[16,64,256]{2,1,0:T(8,128)(2,1)S(1)}, bf16[16,64,256]{2,1,0:T(8,128)(2,1)S(1)}, u32[]{:S(2)}, u32[]{:S(2)}) %collective-permute-start.13) | collective-permute-done | bytes 524320 | tf_op jit(solution)/shard_map/ppermute | solution.py:28
  122.7 4.1 %collective-permute-done.18 = f32[64,256]{1,0:T(8,128)S(1)} collective-permute-done((f32[64,256]{1,0:T(8,128)S(1)}, f32[64,256]{1,0:T(8,128)S(1)}, u32[]{:S(2)}, u32[]{:S(2)}) %collective-permute-start.18) | collective-permute-done | bytes 65568 | tf_op jit(solution)/shard_map/ppermute | solution.py:28
  133.4 8.8 %small.4 = (f32[64,512]{1,0:T(8,128)}, f32[64,512]{1,0:T(8,128)}, f32[64,512]{1,0:T(8,128)}, bf16[2,64,256]{2,1,0:T(8,128)(2,1)}) custom-call(f32[64,256]{1,0:T(8,128)} %copy-done.16, f32[64,256]{1,0:T(8,128)} %copy-done.20, f32[64,512]{1,0:T(8,128)} %get-tuple-element.25.vec, f32[64,512]{1,0:T(8,128)} %get-tuple-element.26.res, ...), custom_call_target="tpu_custom_call" | custom-call | tf_op jit(solution)/shard_map/small/pallas_call | solution.py:163
  142.2 4.5 %collective-permute-done.20 = bf16[2,64,256]{2,1,0:T(8,128)(2,1)S(1)} collective-permute-done((bf16[2,64,256]{2,1,0:T(8,128)(2,1)}, bf16[2,64,256]{2,1,0:T(8,128)(2,1)S(1)}, u32[]{:S(2)}, u32[]{:S(2)}) %collective-permute-start.20) | collective-permute-done | bytes 65568 | tf_op jit(solution)/shard_map/ppermute | solution.py:28
  149.2 5.7 %collective-permute-done.21 = bf16[4,64,256]{2,1,0:T(8,128)(2,1)S(1)} collective-permute-done((bf16[4,64,256]{2,1,0:T(8,128)(2,1)S(1)}, bf16[4,64,256]{2,1,0:T(8,128)(2,1)S(1)}, u32[]{:S(2)}, u32[]{:S(2)}) %collective-permute-start.21) | collective-permute-done | bytes 131104 | tf_op jit(solution)/shard_map/ppermute | solution.py:28
  157.3 4.9 %collective-permute-done.22 = bf16[8,64,256]{2,1,0:T(8,128)(2,1)S(1)} collective-permute-done((bf16[8,64,256]{2,1,0:T(8,128)(2,1)S(1)}, bf16[8,64,256]{2,1,0:T(8,128)(2,1)S(1)}, u32[]{:S(2)}, u32[]{:S(2)}) %collective-permute-start.22) | collective-permute-done | bytes 262176 | tf_op jit(solution)/shard_map/ppermute | solution.py:28
  165.6 6.7 %collective-permute-done.23 = bf16[16,64,256]{2,1,0:T(8,128)(2,1)S(1)} collective-permute-done((bf16[16,64,256]{2,1,0:T(8,128)(2,1)S(1)}, bf16[16,64,256]{2,1,0:T(8,128)(2,1)S(1)}, u32[]{:S(2)}, u32[]{:S(2)}) %collective-permute-start.23) | collective-permute-done | bytes 524320 | tf_op jit(solution)/shard_map/ppermute | solution.py:28
  175.2 4.0 %matrix.6 = (f32[64,512]{1,0:T(8,128)S(1)}, f32[64,256]{1,0:T(8,128)S(1)}) custom-call(s32[32]{0:T(128)S(1)} %fusion.slots, bf16[64,64,256]{2,1,0:T(8,128)(2,1)S(1)} %constant_dynamic-update-slice_fusion.27.whole, bf16[2,16,256,256]{3,2,1,0:T(8,128)(2,1)S(1)} %copy-done.2, f32[64,512]{1,0:T(8,128)S(1)} %copy-done.6, f32[64,512]{1,0:T(8,128)S(1)} %copy-done.5, ...), custom_call_target="tpu_custom_call" | custom-call | tf_op jit(solution)/shard_map/matrix/pallas_call | solution.py:90
  189.9 4.3 %collective-permute-done.28 = f32[64,256]{1,0:T(8,128)S(1)} collective-permute-done((f32[64,256]{1,0:T(8,128)S(1)}, f32[64,256]{1,0:T(8,128)S(1)}, u32[]{:S(2)}, u32[]{:S(2)}) %collective-permute-start.28) | collective-permute-done | bytes 65568 | tf_op jit(solution)/shard_map/ppermute | solution.py:28
  195.7 4.0 %collective-permute-done.29.other = f32[64,256]{1,0:T(8,128)S(1)} collective-permute-done((f32[64,256]{1,0:T(8,128)S(1)}, f32[64,256]{1,0:T(8,128)S(1)}, u32[]{:S(2)}, u32[]{:S(2)}) %collective-permute-start.29) | collective-permute-done | bytes 65568 | tf_op jit(solution)/shard_map/ppermute | solution.py:28
  200.3 8.8 %small.5 = (f32[64,512]{1,0:T(8,128)}, f32[64,512]{1,0:T(8,128)}, f32[64,512]{1,0:T(8,128)}, bf16[2,64,256]{2,1,0:T(8,128)(2,1)}) custom-call(f32[64,256]{1,0:T(8,128)} %copy-done.17, f32[64,256]{1,0:T(8,128)} %copy-done.21, f32[64,512]{1,0:T(8,128)} %get-tuple-element.31.vec, f32[64,512]{1,0:T(8,128)} %get-tuple-element.32.res, ...), custom_call_target="tpu_custom_call" | custom-call | tf_op jit(solution)/shard_map/small/pallas_call | solution.py:163
  209.1 4.5 %collective-permute-done.30 = bf16[2,64,256]{2,1,0:T(8,128)(2,1)S(1)} collective-permute-done((bf16[2,64,256]{2,1,0:T(8,128)(2,1)}, bf16[2,64,256]{2,1,0:T(8,128)(2,1)S(1)}, u32[]{:S(2)}, u32[]{:S(2)}) %collective-permute-start.30) | collective-permute-done | bytes 65568 | tf_op jit(solution)/shard_map/ppermute | solution.py:28
  216.0 5.8 %collective-permute-done.31 = bf16[4,64,256]{2,1,0:T(8,128)(2,1)S(1)} collective-permute-done((bf16[4,64,256]{2,1,0:T(8,128)(2,1)S(1)}, bf16[4,64,256]{2,1,0:T(8,128)(2,1)S(1)}, u32[]{:S(2)}, u32[]{:S(2)}) %collective-permute-start.31) | collective-permute-done | bytes 131104 | tf_op jit(solution)/shard_map/ppermute | solution.py:28
  224.3 4.9 %collective-permute-done.32 = bf16[8,64,256]{2,1,0:T(8,128)(2,1)S(1)} collective-permute-done((bf16[8,64,256]{2,1,0:T(8,128)(2,1)S(1)}, bf16[8,64,256]{2,1,0:T(8,128)(2,1)S(1)}, u32[]{:S(2)}, u32[]{:S(2)}) %collective-permute-start.32) | collective-permute-done | bytes 262176 | tf_op jit(solution)/shard_map/ppermute | solution.py:28
  232.6 6.7 %collective-permute-done.33 = bf16[16,64,256]{2,1,0:T(8,128)(2,1)S(1)} collective-permute-done((bf16[16,64,256]{2,1,0:T(8,128)(2,1)S(1)}, bf16[16,64,256]{2,1,0:T(8,128)(2,1)S(1)}, u32[]{:S(2)}, u32[]{:S(2)}) %collective-permute-start.33) | collective-permute-done | bytes 524320 | tf_op jit(solution)/shard_map/ppermute | solution.py:28
  265.2 8.1 %small_last.1 = (f32[64,512]{1,0:T(8,128)}, f32[64,512]{1,0:T(8,128)}) custom-call(f32[64,128]{1,0:T(8,128)} %copy-done.19, f32[64,128]{1,0:T(8,128)} %copy-done.23, f32[64,512]{1,0:T(8,128)} %get-tuple-element.37.vec, f32[64,512]{1,0:T(8,128)} %get-tuple-element.38.res, f32[64,512]{1,0:T(8,128)} %get-tuple-element.40.sol, f32[64,512]{1,0:T(8,128)} %copy-done.14), custom_call_target="tpu_custom_call" | custom-call | tf_op jit(solution)/shard_map/small_last/pallas_call | solution.py:163
  (172 shorter events, 136.7 us)
Async XLA Ops:
  1.6 5.3 %collective-permute-start = (bf16[2,64,256]{2,1,0:T(8,128)(2,1)S(1)}, bf16[2,64,256]{2,1,0:T(8,128)(2,1)S(1)}, u32[]{:S(2)}, u32[]{:S(2)}) collective-permute-start(bf16[2,64,256]{2,1,0:T(8,128)(2,1)S(1)} %bitcast.20), channel_id=1, source_target_pairs={{0,8},{1,9},{2,10},{3,11},{4,12},{5,13},{6,14},{7,15},{8,0},{9,1},... | collective-permute-start | bytes 196616 | tf_op jit(solution)/shard_map/ppermute | solution.py:28
  6.9 8.3 %collective-permute-start.1 = (bf16[4,64,256]{2,1,0:T(8,128)(2,1)S(1)}, bf16[4,64,256]{2,1,0:T(8,128)(2,1)S(1)}, u32[]{:S(2)}, u32[]{:S(2)}) collective-permute-start(bf16[4,64,256]{2,1,0:T(8,128)(2,1)S(1)} %pad_maximum_fusion.8), channel_id=1, source_target_pairs={{0,16},{1,17},{2,18},{3,19},{4,20},{5,21},{6,22},{7,23},{8,24},{9,... | collective-permute-start | bytes 393224 | tf_op jit(solution)/shard_map/ppermute | solution.py:28
  15.2 6.4 %collective-permute-start.2 = (bf16[8,64,256]{2,1,0:T(8,128)(2,1)S(1)}, bf16[8,64,256]{2,1,0:T(8,128)(2,1)S(1)}, u32[]{:S(2)}, u32[]{:S(2)}) collective-permute-start(bf16[8,64,256]{2,1,0:T(8,128)(2,1)S(1)} %pad_maximum_fusion.4), channel_id=1, source_target_pairs={{0,2},{1,3},{2,0},{3,1},{4,6},{5,7},{6,4},{7,5},{8,10},{9,11},{10,... | collective-permute-start | bytes 786440 | tf_op jit(solution)/shard_map/ppermute | solution.py:28
  21.7 10.2 %collective-permute-start.3 = (bf16[16,64,256]{2,1,0:T(8,128)(2,1)S(1)}, bf16[16,64,256]{2,1,0:T(8,128)(2,1)S(1)}, u32[]{:S(2)}, u32[]{:S(2)}) collective-permute-start(bf16[16,64,256]{2,1,0:T(8,128)(2,1)S(1)} %pad_maximum_fusion), channel_id=1, source_target_pairs={{0,4},{1,5},{2,6},{3,7},{4,0},{5,1},{6,2},{7,3},{8,12},{9,13},{10,... | collective-permute-start | bytes 1572872 | tf_op jit(solution)/shard_map/ppermute | solution.py:28
  43.7 4.3 %collective-permute-start.6 = (f32[64,256]{1,0:T(8,128)S(1)}, f32[64,256]{1,0:T(8,128)S(1)}, u32[]{:S(2)}, u32[]{:S(2)}) collective-permute-start(f32[64,256]{1,0:T(8,128)S(1)} %add.80), channel_id=1, source_target_pairs={{0,2},{1,3},{2,0},{3,1},{4,6},{5,7},{6,4},{7,5},{8,10},{9,11},{10,... | collective-permute-start | bytes 196616 | tf_op jit(solution)/shard_map/ppermute | solution.py:28
  52.4 5.5 %collective-permute-start.8 = (f32[64,256]{1,0:T(8,128)S(1)}, f32[64,256]{1,0:T(8,128)S(1)}, u32[]{:S(2)}, u32[]{:S(2)}) collective-permute-start(f32[64,256]{1,0:T(8,128)S(1)} %add.82), channel_id=1, source_target_pairs={{0,8},{1,9},{2,10},{3,11},{4,12},{5,13},{6,14},{7,15},{8,0},{9,1},... | collective-permute-start | bytes 196616 | tf_op jit(solution)/shard_map/ppermute | solution.py:28
  57.9 6.4 %collective-permute-start.9 = (f32[64,256]{1,0:T(8,128)S(1)}, f32[64,256]{1,0:T(8,128)S(1)}, u32[]{:S(2)}, u32[]{:S(2)}) collective-permute-start(f32[64,256]{1,0:T(8,128)S(1)} %add.83.grams), channel_id=1, source_target_pairs={{0,16},{1,17},{2,18},{3,19},{4,20},{5,21},{6,22},{7,23},{8,24},{9,... | collective-permute-start | bytes 196616 | tf_op jit(solution)/shard_map/ppermute | solution.py:28
  73.8 5.7 %collective-permute-start.10 = (bf16[2,64,256]{2,1,0:T(8,128)(2,1)}, bf16[2,64,256]{2,1,0:T(8,128)(2,1)S(1)}, u32[]{:S(2)}, u32[]{:S(2)}) collective-permute-start(bf16[2,64,256]{2,1,0:T(8,128)(2,1)} %get-tuple-element.24), channel_id=1, source_target_pairs={{0,8},{1,9},{2,10},{3,11},{4,12},{5,13},{6,14},{7,15},{8,0},{9,1},... | collective-permute-start | bytes 196616 | tf_op jit(solution)/shard_map/ppermute | solution.py:28
  80.4 7.3 %collective-permute-start.11 = (bf16[4,64,256]{2,1,0:T(8,128)(2,1)S(1)}, bf16[4,64,256]{2,1,0:T(8,128)(2,1)S(1)}, u32[]{:S(2)}, u32[]{:S(2)}) collective-permute-start(bf16[4,64,256]{2,1,0:T(8,128)(2,1)S(1)} %pad_maximum_fusion.9), channel_id=1, source_target_pairs={{0,16},{1,17},{2,18},{3,19},{4,20},{5,21},{6,22},{7,23},{8,24},{9,... | collective-permute-start | bytes 393224 | tf_op jit(solution)/shard_map/ppermute | solution.py:28
  88.6 6.4 %collective-permute-start.12 = (bf16[8,64,256]{2,1,0:T(8,128)(2,1)S(1)}, bf16[8,64,256]{2,1,0:T(8,128)(2,1)S(1)}, u32[]{:S(2)}, u32[]{:S(2)}) collective-permute-start(bf16[8,64,256]{2,1,0:T(8,128)(2,1)S(1)} %pad_maximum_fusion.5), channel_id=1, source_target_pairs={{0,2},{1,3},{2,0},{3,1},{4,6},{5,7},{6,4},{7,5},{8,10},{9,11},{10,... | collective-permute-start | bytes 786440 | tf_op jit(solution)/shard_map/ppermute | solution.py:28
  95.9 9.2 %collective-permute-start.13 = (bf16[16,64,256]{2,1,0:T(8,128)(2,1)S(1)}, bf16[16,64,256]{2,1,0:T(8,128)(2,1)S(1)}, u32[]{:S(2)}, u32[]{:S(2)}) collective-permute-start(bf16[16,64,256]{2,1,0:T(8,128)(2,1)S(1)} %pad_maximum_fusion.1), channel_id=1, source_target_pairs={{0,4},{1,5},{2,6},{3,7},{4,0},{5,1},{6,2},{7,3},{8,12},{9,13},{10,... | collective-permute-start | bytes 1572872 | tf_op jit(solution)/shard_map/ppermute | solution.py:28
  113.8 4.3 %collective-permute-start.16 = (f32[64,256]{1,0:T(8,128)S(1)}, f32[64,256]{1,0:T(8,128)S(1)}, u32[]{:S(2)}, u32[]{:S(2)}) collective-permute-start(f32[64,256]{1,0:T(8,128)S(1)} %add.84), channel_id=1, source_target_pairs={{0,2},{1,3},{2,0},{3,1},{4,6},{5,7},{6,4},{7,5},{8,10},{9,11},{10,... | collective-permute-start | bytes 196616 | tf_op jit(solution)/shard_map/ppermute | solution.py:28
  122.5 4.3 %collective-permute-start.18 = (f32[64,256]{1,0:T(8,128)S(1)}, f32[64,256]{1,0:T(8,128)S(1)}, u32[]{:S(2)}, u32[]{:S(2)}) collective-permute-start(f32[64,256]{1,0:T(8,128)S(1)} %add.86), channel_id=1, source_target_pairs={{0,8},{1,9},{2,10},{3,11},{4,12},{5,13},{6,14},{7,15},{8,0},{9,1},... | collective-permute-start | bytes 196616 | tf_op jit(solution)/shard_map/ppermute | solution.py:28
  126.9 5.9 %collective-permute-start.19 = (f32[64,256]{1,0:T(8,128)S(1)}, f32[64,256]{1,0:T(8,128)S(1)}, u32[]{:S(2)}, u32[]{:S(2)}) collective-permute-start(f32[64,256]{1,0:T(8,128)S(1)} %add.87.grams), channel_id=1, source_target_pairs={{0,16},{1,17},{2,18},{3,19},{4,20},{5,21},{6,22},{7,23},{8,24},{9,... | collective-permute-start | bytes 196616 | tf_op jit(solution)/shard_map/ppermute | solution.py:28
  142.2 4.5 %collective-permute-start.20 = (bf16[2,64,256]{2,1,0:T(8,128)(2,1)}, bf16[2,64,256]{2,1,0:T(8,128)(2,1)S(1)}, u32[]{:S(2)}, u32[]{:S(2)}) collective-permute-start(bf16[2,64,256]{2,1,0:T(8,128)(2,1)} %get-tuple-element.30), channel_id=1, source_target_pairs={{0,8},{1,9},{2,10},{3,11},{4,12},{5,13},{6,14},{7,15},{8,0},{9,1},... | collective-permute-start | bytes 196616 | tf_op jit(solution)/shard_map/ppermute | solution.py:28
  147.5 7.3 %collective-permute-start.21 = (bf16[4,64,256]{2,1,0:T(8,128)(2,1)S(1)}, bf16[4,64,256]{2,1,0:T(8,128)(2,1)S(1)}, u32[]{:S(2)}, u32[]{:S(2)}) collective-permute-start(bf16[4,64,256]{2,1,0:T(8,128)(2,1)S(1)} %pad_maximum_fusion.10), channel_id=1, source_target_pairs={{0,16},{1,17},{2,18},{3,19},{4,20},{5,21},{6,22},{7,23},{8,24},{9,... | collective-permute-start | bytes 393224 | tf_op jit(solution)/shard_map/ppermute | solution.py:28
  155.7 6.4 %collective-permute-start.22 = (bf16[8,64,256]{2,1,0:T(8,128)(2,1)S(1)}, bf16[8,64,256]{2,1,0:T(8,128)(2,1)S(1)}, u32[]{:S(2)}, u32[]{:S(2)}) collective-permute-start(bf16[8,64,256]{2,1,0:T(8,128)(2,1)S(1)} %pad_maximum_fusion.6), channel_id=1, source_target_pairs={{0,2},{1,3},{2,0},{3,1},{4,6},{5,7},{6,4},{7,5},{8,10},{9,11},{10,... | collective-permute-start | bytes 786440 | tf_op jit(solution)/shard_map/ppermute | solution.py:28
  163.1 9.2 %collective-permute-start.23 = (bf16[16,64,256]{2,1,0:T(8,128)(2,1)S(1)}, bf16[16,64,256]{2,1,0:T(8,128)(2,1)S(1)}, u32[]{:S(2)}, u32[]{:S(2)}) collective-permute-start(bf16[16,64,256]{2,1,0:T(8,128)(2,1)S(1)} %pad_maximum_fusion.2), channel_id=1, source_target_pairs={{0,4},{1,5},{2,6},{3,7},{4,0},{5,1},{6,2},{7,3},{8,12},{9,13},{10,... | collective-permute-start | bytes 1572872 | tf_op jit(solution)/shard_map/ppermute | solution.py:28
  194.2 5.5 %collective-permute-start.29 = (f32[64,256]{1,0:T(8,128)S(1)}, f32[64,256]{1,0:T(8,128)S(1)}, u32[]{:S(2)}, u32[]{:S(2)}) collective-permute-start(f32[64,256]{1,0:T(8,128)S(1)} %add.91.grams), channel_id=1, source_target_pairs={{0,16},{1,17},{2,18},{3,19},{4,20},{5,21},{6,22},{7,23},{8,24},{9,... | collective-permute-start | bytes 196616 | tf_op jit(solution)/shard_map/ppermute | solution.py:28
  209.1 4.6 %collective-permute-start.30 = (bf16[2,64,256]{2,1,0:T(8,128)(2,1)}, bf16[2,64,256]{2,1,0:T(8,128)(2,1)S(1)}, u32[]{:S(2)}, u32[]{:S(2)}) collective-permute-start(bf16[2,64,256]{2,1,0:T(8,128)(2,1)} %get-tuple-element.36), channel_id=1, source_target_pairs={{0,8},{1,9},{2,10},{3,11},{4,12},{5,13},{6,14},{7,15},{8,0},{9,1},... | collective-permute-start | bytes 196616 | tf_op jit(solution)/shard_map/ppermute | solution.py:28
  214.5 7.3 %collective-permute-start.31 = (bf16[4,64,256]{2,1,0:T(8,128)(2,1)S(1)}, bf16[4,64,256]{2,1,0:T(8,128)(2,1)S(1)}, u32[]{:S(2)}, u32[]{:S(2)}) collective-permute-start(bf16[4,64,256]{2,1,0:T(8,128)(2,1)S(1)} %pad_maximum_fusion.11), channel_id=1, source_target_pairs={{0,16},{1,17},{2,18},{3,19},{4,20},{5,21},{6,22},{7,23},{8,24},{9,... | collective-permute-start | bytes 393224 | tf_op jit(solution)/shard_map/ppermute | solution.py:28
  222.7 6.4 %collective-permute-start.32 = (bf16[8,64,256]{2,1,0:T(8,128)(2,1)S(1)}, bf16[8,64,256]{2,1,0:T(8,128)(2,1)S(1)}, u32[]{:S(2)}, u32[]{:S(2)}) collective-permute-start(bf16[8,64,256]{2,1,0:T(8,128)(2,1)S(1)} %pad_maximum_fusion.7), channel_id=1, source_target_pairs={{0,2},{1,3},{2,0},{3,1},{4,6},{5,7},{6,4},{7,5},{8,10},{9,11},{10,... | collective-permute-start | bytes 786440 | tf_op jit(solution)/shard_map/ppermute | solution.py:28
  230.1 9.2 %collective-permute-start.33 = (bf16[16,64,256]{2,1,0:T(8,128)(2,1)S(1)}, bf16[16,64,256]{2,1,0:T(8,128)(2,1)S(1)}, u32[]{:S(2)}, u32[]{:S(2)}) collective-permute-start(bf16[16,64,256]{2,1,0:T(8,128)(2,1)S(1)} %pad_maximum_fusion.3), channel_id=1, source_target_pairs={{0,4},{1,5},{2,6},{3,7},{4,0},{5,1},{6,2},{7,3},{8,12},{9,13},{10,... | collective-permute-start | bytes 1572872 | tf_op jit(solution)/shard_map/ppermute | solution.py:28
  259.7 4.9 %collective-permute-start.39 = (f32[64,128]{1,0:T(8,128)S(1)}, f32[64,128]{1,0:T(8,128)S(1)}, u32[]{:S(2)}, u32[]{:S(2)}) collective-permute-start(f32[64,128]{1,0:T(8,128)S(1)} %add.95.grams), channel_id=1, source_target_pairs={{0,16},{1,17},{2,18},{3,19},{4,20},{5,21},{6,22},{7,23},{8,24},{9,... | collective-permute-start | bytes 98312 | tf_op jit(solution)/shard_map/ppermute | solution.py:28
  (41 other events, 205.7 us)

commit v2 on v1

v2 whole, which is shorter than its diff:
```python
import functools

import jax
import jax.numpy as jnp
from jax import lax
from jax.experimental import pallas as pl
from jax.experimental.pallas import tpu as pltpu
from jax.sharding import PartitionSpec as P

ITERS = 4
AXES = ("row", "col")
HIGH = lax.Precision.HIGHEST


def nn(left, right):
    return lax.dot_general(
        left, right, (((1,), (0,)), ((), ())), precision=HIGH, preferred_element_type=jnp.float32
    )


def nt(left, right):
    return lax.dot_general(
        left, right, (((1,), (1,)), ((), ())), precision=HIGH, preferred_element_type=jnp.float32
    )


def xor_permute(val, mask, count):
    return lax.ppermute(val, AXES, [(i, i ^ mask) for i in range(count)])


def spread(val, masks, count):
    partners = [0]
    for mask in masks:
        partners = partners + [p ^ mask for p in partners]
    return [val] + [xor_permute(val, p, count) for p in partners[1:]]


def gather_of(val, groups, core, count):
    for masks in groups[:-1]:
        val = jnp.concatenate(spread(val, masks, count), axis=0)
    pieces = spread(val, groups[-1], count)
    return pieces + [xor_permute(piece, core, count) for piece in pieces]


def slot_of(diff, masks):
    slot = jnp.zeros_like(diff)
    for place, mask in enumerate(masks):
        slot = slot + jnp.where((diff & mask) != 0, 1 << place, 0)
    return slot


def matrix_kernel(rows, nbr, blk, chunk, count, slots, tiles, vec, res, diag, *refs):
    pieces, (image, keep, give, held, whole, sems, piece_sems) = refs[:count], refs[count:]
    coef = 1.0 / (nbr * blk)
    parts = rows * nbr // chunk
    each = whole.shape[0] // count
    arrivals = [
        pltpu.make_async_copy(piece, whole.at[pl.ds(i * each, each)], piece_sems.at[i])
        for i, piece in enumerate(pieces)
    ]
    copies = []
    for part in range(parts):
        row, first = divmod(part * chunk, nbr)
        copies.append(
            pltpu.make_async_copy(
                tiles.at[row, pl.ds(first, chunk)], held.at[pl.ds(part * chunk, chunk)], sems.at[part]
            )
        )
    for copy in arrivals + copies:
        copy.start()
    for copy in arrivals:
        copy.wait()
    n = vec.shape[0]
    for row in range(rows):
        acc = jnp.zeros((n, blk), jnp.float32)
        for k in range(nbr):
            spot = row * nbr + k
            if spot % chunk == 0:
                copies[spot // chunk].wait()
            acc = acc + lax.dot_general(
                whole[slots[spot]],
                held[spot],
                (((1,), (1,)), ((), ())),
                preferred_element_type=jnp.float32,
            )
        cols = pl.ds(row * blk, blk)
        image[:, cols] = diag[:, cols] * vec[:, cols] + coef * acc
    img = image[...]
    old = res[...]
    both = nt(jnp.concatenate([old, img], axis=0), jnp.concatenate([old, img], axis=0))
    curv = nt(vec[...], img)
    first = jnp.concatenate([both[0:n, 0:n], curv], axis=1)
    second = both[:, n : 2 * n]
    second = jnp.concatenate([second[0:n], second[n : 2 * n]], axis=1)
    core = slots[rows * nbr]
    keep[...] = jnp.where(core == 0, first, second)
    give[...] = jnp.where(core == 0, second, first)


def apply_matrix(slots, pieces, tiles, vec, res, diag):
    rows, nbr, blk, _ = tiles.shape
    n = vec.shape[0]
    chunk = 4
    vmem = pl.BlockSpec(memory_space=pltpu.VMEM)
    anywhere = pl.BlockSpec(memory_space=pl.ANY)
    half = jax.ShapeDtypeStruct((n, 2 * n), jnp.float32)
    blocks = sum(piece.shape[0] for piece in pieces)
    return pl.pallas_call(
        functools.partial(matrix_kernel, rows, nbr, blk, chunk, len(pieces)),
        out_shape=(jax.ShapeDtypeStruct(vec.shape, jnp.float32), half, half),
        in_specs=[pl.BlockSpec(memory_space=pltpu.SMEM), anywhere, vmem, vmem, vmem]
        + [anywhere] * len(pieces),
        out_specs=(vmem, vmem, vmem),
        scratch_shapes=[
            pltpu.VMEM((rows * nbr, blk, blk), tiles.dtype),
            pltpu.VMEM((blocks, n, blk), tiles.dtype),
            pltpu.SemaphoreType.DMA((rows * nbr // chunk,)),
            pltpu.SemaphoreType.DMA((len(pieces),)),
        ],
        compiler_params=pltpu.CompilerParams(vmem_limit_bytes=40 * 1024 * 1024),
        name="matrix",
    )(slots, tiles, vec, res, diag, *pieces)


def invert_pair(mats, n):
    rows = lax.broadcasted_iota(jnp.int32, (n, 2 * n), 0)
    lanes = lax.broadcasted_iota(jnp.int32, (n, 2 * n), 1)
    left = lanes < n
    place = jnp.where(left, lanes, lanes - n)
    for j in range(n):
        col = jnp.where(
            left,
            jnp.broadcast_to(mats[:, j : j + 1], (n, 2 * n)),
            jnp.broadcast_to(mats[:, n + j : n + j + 1], (n, 2 * n)),
        )
        pivot = col[j : j + 1, :]
        inv = 1.0 / pivot
        line = mats[j : j + 1, :]
        scaled = jnp.where(place[0:1, :] == j, inv, line * inv)
        kept = jnp.where(place == j, 0.0, mats)
        mats = jnp.where(rows == j, jnp.broadcast_to(scaled, (n, 2 * n)), kept - col * scaled)
    return mats


def solve_kernel(last, core, mine, other, vec, res, sol, image, *outs):
    n = vec.shape[0]
    at_zero = core[0] == 0
    first = jnp.where(at_zero, mine[...], other[...])
    gram, curv = first[:, 0:n], first[:, n : 2 * n]
    inverses = invert_pair(jnp.concatenate([curv, gram], axis=1), n)
    alpha_t = nn(gram, inverses[:, 0:n])
    old = vec[...]
    new = res[...] - nn(alpha_t, image[...])
    outs[0][...] = sol[...] + nn(alpha_t, old)
    outs[1][...] = new
    if not last:
        second = jnp.where(at_zero, other[...], mine[...])
        cross, square = second[:, 0:n], second[:, n : 2 * n]
        mixed = nt(cross, alpha_t)
        gram_new = gram - mixed + nn(alpha_t, nt(square, alpha_t) - cross.T)
        beta_t = nn(gram_new, inverses[:, n : 2 * n])
        step = new + nn(beta_t, old)
        outs[2][...] = step
        blk = outs[3].shape[2]
        for row in range(outs[3].shape[0]):
            outs[3][row] = step[:, row * blk : (row + 1) * blk].astype(jnp.bfloat16)


def solve_step(last, rows, core, mine, other, vec, res, sol, image):
    shape = jax.ShapeDtypeStruct(vec.shape, jnp.float32)
    n, width = vec.shape
    space = pl.BlockSpec(memory_space=pltpu.VMEM)
    outs = [shape, shape]
    if not last:
        outs += [shape, jax.ShapeDtypeStruct((rows, n, width // rows), jnp.bfloat16)]
    return pl.pallas_call(
        functools.partial(solve_kernel, last),
        out_shape=tuple(outs),
        in_specs=[pl.BlockSpec(memory_space=pltpu.SMEM)] + [space] * 6,
        out_specs=tuple([space] * len(outs)),
        name="small_last" if last else "small",
    )(core, mine, other, vec, res, sol, image)


def body(groups, bits, core_bit, count, cols, right_side, diag_vals, tiles, col_ids):
    rows, nbr, blk, _ = tiles.shape
    n = right_side.shape[0]
    me = lax.axis_index("row") * cols + lax.axis_index("col")
    core = ((me & core_bit) != 0).astype(jnp.int32)[None]
    ids = col_ids.reshape(-1)
    order = [mask for masks in groups for mask in masks] + [core_bit]
    slots = slot_of(me ^ (ids // rows), order) * rows + ids % rows
    slots = jnp.concatenate([slots, core])
    diag = diag_vals[None, :]
    sol = jnp.zeros_like(right_side)
    res = right_side
    vec = right_side
    rounded = right_side.astype(jnp.bfloat16).reshape(n, rows, blk).transpose(1, 0, 2)
    for step in range(ITERS):
        last = step + 1 == ITERS
        pieces = gather_of(rounded, groups, core_bit, count)
        image, keep, give = apply_matrix(slots, pieces, tiles, vec, res, diag)
        mine = keep + xor_permute(give, core_bit, count)
        for mask in bits:
            mine = mine + xor_permute(mine, mask, count)
        other = xor_permute(mine, core_bit, count)
        outs = solve_step(last, rows, core, mine, other, vec, res, sol, image)
        if last:
            sol, res = outs
        else:
            sol, res, vec, rounded = outs
    return (sol, res)


def solution(mesh):
    placed = (
        P(None, ("row", "col")),
        P(("row", "col")),
        P(("row", "col"), None, None, None),
        P(("row", "col"), None),
    )
    count = mesh.shape["row"] * mesh.shape["col"]
    cols = mesh.shape["col"]
    bits = [1 << i for i in range(1, count.bit_length() - 1)]
    major = [b for b in bits if b >= cols]
    minor = [b for b in bits if b < cols]
    groups = [part[i : i + 2] for part in (major, minor) for i in range(0, len(part), 2)]
    return jax.shard_map(
        functools.partial(body, groups, bits, 1, count, cols),
        mesh=mesh,
        in_specs=placed,
        out_specs=(P(None, ("row", "col")), P(None, ("row", "col"))),
        check_vma=False,
    )
```

time: 274 us -> 255 us (0.931)
  waiting for transfers between devices: 147 us -> 129 us
  local copies, waits for them, and re-layouts: 14.3 us -> 24.3 us
  other arithmetic: 9.01 us -> 1.15 us
  starting transfers between devices: 51.6 us -> 48.5 us
    ppermute x40 -> x64, waiting for transfers between devices: 147 us -> 129 us  [xor_permute(): return lax.ppermute(val, AXES, [(i, i ^ mask) for i in range(count)])]
    unnamed x66 -> x59, local copies, waits for them, and re-layouts: 12.1 us -> 22.8 us
    concatenate x12 -> x2, other arithmetic: 7.93 us -> 0.11 us  [the longest x1 0.08 us: body(): slots = jnp.concatenate([slots, core])]
    ppermute x40 -> x64, starting transfers between devices: 51.6 us -> 48.5 us  [xor_permute(): return lax.ppermute(val, AXES, [(i, i ^ mask) for i in range(count)])]
  transfers between devices with their start and end apart: 40 -> 64, of which waited for: 40 -> 52; matrix products, arithmetic and copies ran while one was open for 2% -> 1% of each run, Pallas kernels for 0% -> 0%
where the time goes in v2:
time: 255 us; the launch traced here: 254 us
  waiting for transfers between devices  129 us (51%)
  Pallas kernels  50.7 us (20%)
  starting transfers between devices  48.5 us (19%)
  local copies, waits for them, and re-layouts  24.3 us (10%)
    ppermute x64, waiting for transfers between devices, xor_permute(): return lax.ppermute(val, AXES, [(i, i ^ mask) for i in range(count)])  129 us
    ppermute x64, starting transfers between devices, xor_permute(): return lax.ppermute(val, AXES, [(i, i ^ mask) for i in range(count)])  48.5 us
    pallas_call x4, Pallas kernels, solve_step(): pl.pallas_call(functools.partial(solve_kernel, last), out_shape=tuple(out...  34.4 us
    unnamed x59, local copies, waits for them, and re-layouts  22.8 us
    pallas_call x4, Pallas kernels, apply_matrix(): pl.pallas_call(functools.partial(matrix_kernel, rows, nbr, blk, chunk, le...  16.2 us
  transfers between devices with their start and end apart: 64, of which 52 were waited for; matrix products, arithmetic and copies ran while one was open for 1% of the time, Pallas kernels for 0%

profile of v2, /device:TPU:0, one launch (start us, length us, event | category | flops | bytes accessed | tf_op | source)
XLA Modules:
  0.0 254.3 jit_solution(12018414440846559676)
XLA Ops:
  1.6 5.1 %collective-permute-start.2 = (bf16[2,64,256]{2,1,0:T(8,128)(2,1)S(1)}, bf16[2,64,256]{2,1,0:T(8,128)(2,1)S(1)}, u32[]{:S(2)}, u32[]{:S(2)}) collective-permute-start(bf16[2,64,256]{2,1,0:T(8,128)(2,1)S(1)} %bitcast.14), channel_id=1, source_target_pairs={{0,24},{1,25},{2,26},{3,27},{4,28},{5,29},{6,30},{7,31},{8,16},{9,... | collective-permute-start | bytes 196616 | tf_op jit(solution)/shard_map/ppermute | solution.py:28
  16.7 5.9 %collective-permute-done.5.refs_3_ = bf16[8,64,256]{2,1,0:T(8,128)(2,1)S(1)} collective-permute-done((bf16[8,64,256]{2,1,0:T(8,128)(2,1)S(1)}, bf16[8,64,256]{2,1,0:T(8,128)(2,1)S(1)}, u32[]{:S(2)}, u32[]{:S(2)}) %collective-permute-start.5) | collective-permute-done | bytes 262176 | tf_op jit(solution)/shard_map/ppermute | solution.py:28
  22.6 4.2 %collective-permute-done.4.refs_2_ = bf16[8,64,256]{2,1,0:T(8,128)(2,1)S(1)} collective-permute-done((bf16[8,64,256]{2,1,0:T(8,128)(2,1)S(1)}, bf16[8,64,256]{2,1,0:T(8,128)(2,1)S(1)}, u32[]{:S(2)}, u32[]{:S(2)}) %collective-permute-start.4) | collective-permute-done | bytes 262176 | tf_op jit(solution)/shard_map/ppermute | solution.py:28
  32.5 4.0 %matrix.4 = (f32[64,512]{1,0:T(8,128)S(1)}, f32[64,128]{1,0:T(8,128)S(1)}, f32[64,128]{1,0:T(8,128)S(1)}) custom-call(s32[33]{0:T(128)S(1)} %pad_add_fusion.slots, bf16[2,16,256,256]{3,2,1,0:T(8,128)(2,1)S(1)} %copy-done, f32[64,512]{1,0:T(8,128)S(1)} %copy-done.4, f32[64,512]{1,0:T(8,128)S(1)} %copy-done.4, f32[1,512]{1,0:T(1,128)S(1)} %bitcast.9, ...), custom_call_target="tpu_custom_call" | custom-call | tf_op jit(solution)/shard_map/matrix/pallas_call | solution.py:108
  50.5 4.7 %collective-permute-done.14 = f32[64,128]{1,0:T(8,128)S(1)} collective-permute-done((f32[64,128]{1,0:T(8,128)S(1)}, f32[64,128]{1,0:T(8,128)S(1)}, u32[]{:S(2)}, u32[]{:S(2)}) %collective-permute-start.14) | collective-permute-done | bytes 32800 | tf_op jit(solution)/shard_map/ppermute | solution.py:28
  57.2 8.8 %small.3 = (f32[64,512]{1,0:T(8,128)}, f32[64,512]{1,0:T(8,128)}, f32[64,512]{1,0:T(8,128)}, bf16[2,64,256]{2,1,0:T(8,128)(2,1)}) custom-call(s32[1]{0:T(128)} %bitcast.core, f32[64,128]{1,0:T(8,128)} %copy-done.20, f32[64,128]{1,0:T(8,128)} %copy-done.24, f32[64,512]{1,0:T(8,128)} %res.3, f32[64,512]{1,0:T(8,128)} %res.3, f32[64,512]{1,0:T(8,128)} %broadcast_in_dim.29.sol, ...), custom_call_target="tpu_custom_call" | custom-call | tf_op jit(solution)/shard_map/small/pallas_call | solution.py:176
  78.5 6.6 %collective-permute-done.21.refs_3_ = bf16[8,64,256]{2,1,0:T(8,128)(2,1)S(1)} collective-permute-done((bf16[8,64,256]{2,1,0:T(8,128)(2,1)S(1)}, bf16[8,64,256]{2,1,0:T(8,128)(2,1)S(1)}, u32[]{:S(2)}, u32[]{:S(2)}) %collective-permute-start.21) | collective-permute-done | bytes 262176 | tf_op jit(solution)/shard_map/ppermute | solution.py:28
  85.1 4.6 %collective-permute-done.20.refs_2_ = bf16[8,64,256]{2,1,0:T(8,128)(2,1)S(1)} collective-permute-done((bf16[8,64,256]{2,1,0:T(8,128)(2,1)S(1)}, bf16[8,64,256]{2,1,0:T(8,128)(2,1)S(1)}, u32[]{:S(2)}, u32[]{:S(2)}) %collective-permute-start.20) | collective-permute-done | bytes 262176 | tf_op jit(solution)/shard_map/ppermute | solution.py:28
  95.7 4.0 %matrix.5 = (f32[64,512]{1,0:T(8,128)S(1)}, f32[64,128]{1,0:T(8,128)S(1)}, f32[64,128]{1,0:T(8,128)S(1)}) custom-call(s32[33]{0:T(128)S(1)} %pad_add_fusion.slots, bf16[2,16,256,256]{3,2,1,0:T(8,128)(2,1)S(1)} %copy-done.1, f32[64,512]{1,0:T(8,128)S(1)} %copy-done.10, f32[64,512]{1,0:T(8,128)S(1)} %copy-done.9, f32[1,512]{1,0:T(1,128)S(1)} %bitcast.10, ...), custom_call_target="tpu_custom_call" | custom-call | tf_op jit(solution)/shard_map/matrix/pallas_call | solution.py:108
  109.4 3.9 %collective-permute-done.29 = f32[64,128]{1,0:T(8,128)S(1)} collective-permute-done((f32[64,128]{1,0:T(8,128)S(1)}, f32[64,128]{1,0:T(8,128)S(1)}, u32[]{:S(2)}, u32[]{:S(2)}) %collective-permute-start.29) | collective-permute-done | bytes 32800 | tf_op jit(solution)/shard_map/ppermute | solution.py:28
  113.3 4.9 %collective-permute-done.30 = f32[64,128]{1,0:T(8,128)S(1)} collective-permute-done((f32[64,128]{1,0:T(8,128)S(1)}, f32[64,128]{1,0:T(8,128)S(1)}, u32[]{:S(2)}, u32[]{:S(2)}) %collective-permute-start.30) | collective-permute-done | bytes 32800 | tf_op jit(solution)/shard_map/ppermute | solution.py:28
  120.1 8.7 %small.4 = (f32[64,512]{1,0:T(8,128)}, f32[64,512]{1,0:T(8,128)}, f32[64,512]{1,0:T(8,128)}, bf16[2,64,256]{2,1,0:T(8,128)(2,1)}) custom-call(s32[1]{0:T(128)} %bitcast.core, f32[64,128]{1,0:T(8,128)} %copy-done.17, f32[64,128]{1,0:T(8,128)} %copy-done.21, f32[64,512]{1,0:T(8,128)} %get-tuple-element.29.vec, f32[64,512]{1,0:T(8,128)} %get-tuple-element.30.res, ...), custom_call_target="tpu_custom_call" | custom-call | tf_op jit(solution)/shard_map/small/pallas_call | solution.py:176
  141.4 6.6 %collective-permute-done.37.refs_3_ = bf16[8,64,256]{2,1,0:T(8,128)(2,1)S(1)} collective-permute-done((bf16[8,64,256]{2,1,0:T(8,128)(2,1)S(1)}, bf16[8,64,256]{2,1,0:T(8,128)(2,1)S(1)}, u32[]{:S(2)}, u32[]{:S(2)}) %collective-permute-start.37) | collective-permute-done | bytes 262176 | tf_op jit(solution)/shard_map/ppermute | solution.py:28
  148.1 4.6 %collective-permute-done.36.refs_2_ = bf16[8,64,256]{2,1,0:T(8,128)(2,1)S(1)} collective-permute-done((bf16[8,64,256]{2,1,0:T(8,128)(2,1)S(1)}, bf16[8,64,256]{2,1,0:T(8,128)(2,1)S(1)}, u32[]{:S(2)}, u32[]{:S(2)}) %collective-permute-start.36) | collective-permute-done | bytes 262176 | tf_op jit(solution)/shard_map/ppermute | solution.py:28
  158.6 4.2 %matrix.6 = (f32[64,512]{1,0:T(8,128)S(1)}, f32[64,128]{1,0:T(8,128)S(1)}, f32[64,128]{1,0:T(8,128)S(1)}) custom-call(s32[33]{0:T(128)S(1)} %pad_add_fusion.slots, bf16[2,16,256,256]{3,2,1,0:T(8,128)(2,1)S(1)} %copy-done.2, f32[64,512]{1,0:T(8,128)S(1)} %copy-done.6, f32[64,512]{1,0:T(8,128)S(1)} %copy-done.5, f32[1,512]{1,0:T(1,128)S(1)} %bitcast.11, ...), custom_call_target="tpu_custom_call" | custom-call | tf_op jit(solution)/shard_map/matrix/pallas_call | solution.py:108
  172.5 3.9 %collective-permute-done.45 = f32[64,128]{1,0:T(8,128)S(1)} collective-permute-done((f32[64,128]{1,0:T(8,128)S(1)}, f32[64,128]{1,0:T(8,128)S(1)}, u32[]{:S(2)}, u32[]{:S(2)}) %collective-permute-start.45) | collective-permute-done | bytes 32800 | tf_op jit(solution)/shard_map/ppermute | solution.py:28
  176.4 4.9 %collective-permute-done.46 = f32[64,128]{1,0:T(8,128)S(1)} collective-permute-done((f32[64,128]{1,0:T(8,128)S(1)}, f32[64,128]{1,0:T(8,128)S(1)}, u32[]{:S(2)}, u32[]{:S(2)}) %collective-permute-start.46) | collective-permute-done | bytes 32800 | tf_op jit(solution)/shard_map/ppermute | solution.py:28
  183.2 8.8 %small.5 = (f32[64,512]{1,0:T(8,128)}, f32[64,512]{1,0:T(8,128)}, f32[64,512]{1,0:T(8,128)}, bf16[2,64,256]{2,1,0:T(8,128)(2,1)}) custom-call(s32[1]{0:T(128)} %bitcast.core, f32[64,128]{1,0:T(8,128)} %copy-done.18, f32[64,128]{1,0:T(8,128)} %copy-done.22, f32[64,512]{1,0:T(8,128)} %get-tuple-element.36.vec, f32[64,512]{1,0:T(8,128)} %get-tuple-element.37.res, ...), custom_call_target="tpu_custom_call" | custom-call | tf_op jit(solution)/shard_map/small/pallas_call | solution.py:176
  204.6 6.6 %collective-permute-done.53.refs_3_ = bf16[8,64,256]{2,1,0:T(8,128)(2,1)S(1)} collective-permute-done((bf16[8,64,256]{2,1,0:T(8,128)(2,1)S(1)}, bf16[8,64,256]{2,1,0:T(8,128)(2,1)S(1)}, u32[]{:S(2)}, u32[]{:S(2)}) %collective-permute-start.53) | collective-permute-done | bytes 262176 | tf_op jit(solution)/shard_map/ppermute | solution.py:28
  211.2 4.6 %collective-permute-done.52.refs_2_ = bf16[8,64,256]{2,1,0:T(8,128)(2,1)S(1)} collective-permute-done((bf16[8,64,256]{2,1,0:T(8,128)(2,1)S(1)}, bf16[8,64,256]{2,1,0:T(8,128)(2,1)S(1)}, u32[]{:S(2)}, u32[]{:S(2)}) %collective-permute-start.52) | collective-permute-done | bytes 262176 | tf_op jit(solution)/shard_map/ppermute | solution.py:28
  221.7 4.0 %matrix.7 = (f32[64,512]{1,0:T(8,128)S(1)}, f32[64,128]{1,0:T(8,128)S(1)}, f32[64,128]{1,0:T(8,128)S(1)}) custom-call(s32[33]{0:T(128)S(1)} %pad_add_fusion.slots, bf16[2,16,256,256]{3,2,1,0:T(8,128)(2,1)S(1)} %copy-done.3, f32[64,512]{1,0:T(8,128)S(1)} %copy-done.8, f32[64,512]{1,0:T(8,128)S(1)} %copy-done.7, f32[1,512]{1,0:T(1,128)S(1)} %bitcast.12, ...), custom_call_target="tpu_custom_call" | custom-call | tf_op jit(solution)/shard_map/matrix/pallas_call | solution.py:108
  235.5 3.9 %collective-permute-done.61 = f32[64,128]{1,0:T(8,128)S(1)} collective-permute-done((f32[64,128]{1,0:T(8,128)S(1)}, f32[64,128]{1,0:T(8,128)S(1)}, u32[]{:S(2)}, u32[]{:S(2)}) %collective-permute-start.61) | collective-permute-done | bytes 32800 | tf_op jit(solution)/shard_map/ppermute | solution.py:28
  239.4 4.9 %collective-permute-done.62 = f32[64,128]{1,0:T(8,128)S(1)} collective-permute-done((f32[64,128]{1,0:T(8,128)S(1)}, f32[64,128]{1,0:T(8,128)S(1)}, u32[]{:S(2)}, u32[]{:S(2)}) %collective-permute-start.62) | collective-permute-done | bytes 32800 | tf_op jit(solution)/shard_map/ppermute | solution.py:28
  246.2 8.1 %small_last.1 = (f32[64,512]{1,0:T(8,128)}, f32[64,512]{1,0:T(8,128)}) custom-call(s32[1]{0:T(128)} %bitcast.core, f32[64,128]{1,0:T(8,128)} %copy-done.19, f32[64,128]{1,0:T(8,128)} %copy-done.23, f32[64,512]{1,0:T(8,128)} %get-tuple-element.43.vec, f32[64,512]{1,0:T(8,128)} %get-tuple-element.44.res, f32[64,512]{1,0:T(8,128)} %get-tuple-element.48.sol, ...), custom_call_target="tpu_custom_call" | custom-call | tf_op jit(solution)/shard_map/small_last/pallas_call | solution.py:176
  (201 shorter events, 122.6 us)
Async XLA Ops:
  1.6 7.7 %collective-permute-start.2 = (bf16[2,64,256]{2,1,0:T(8,128)(2,1)S(1)}, bf16[2,64,256]{2,1,0:T(8,128)(2,1)S(1)}, u32[]{:S(2)}, u32[]{:S(2)}) collective-permute-start(bf16[2,64,256]{2,1,0:T(8,128)(2,1)S(1)} %bitcast.14), channel_id=1, source_target_pairs={{0,24},{1,25},{2,26},{3,27},{4,28},{5,29},{6,30},{7,31},{8,16},{9,... | collective-permute-start | bytes 196616 | tf_op jit(solution)/shard_map/ppermute | solution.py:28
  12.3 10.2 %collective-permute-start.5 = (bf16[8,64,256]{2,1,0:T(8,128)(2,1)S(1)}, bf16[8,64,256]{2,1,0:T(8,128)(2,1)S(1)}, u32[]{:S(2)}, u32[]{:S(2)}) collective-permute-start(bf16[8,64,256]{2,1,0:T(8,128)(2,1)S(1)} %pad_maximum_fusion.refs_0_), channel_id=1, source_target_pairs={{0,6},{1,7},{2,4},{3,5},{4,2},{5,3},{6,0},{7,1},{8,14},{9,15},{10,... | collective-permute-start | bytes 786440 | tf_op jit(solution)/shard_map/ppermute | solution.py:28
  14.8 11.9 %collective-permute-start.4 = (bf16[8,64,256]{2,1,0:T(8,128)(2,1)S(1)}, bf16[8,64,256]{2,1,0:T(8,128)(2,1)S(1)}, u32[]{:S(2)}, u32[]{:S(2)}) collective-permute-start(bf16[8,64,256]{2,1,0:T(8,128)(2,1)S(1)} %pad_maximum_fusion.refs_0_), channel_id=1, source_target_pairs={{0,4},{1,5},{2,6},{3,7},{4,0},{5,1},{6,2},{7,3},{8,12},{9,13},{10,... | collective-permute-start | bytes 786440 | tf_op jit(solution)/shard_map/ppermute | solution.py:28
  15.4 11.7 %collective-permute-start.3 = (bf16[8,64,256]{2,1,0:T(8,128)(2,1)S(1)}, bf16[8,64,256]{2,1,0:T(8,128)(2,1)S(1)}, u32[]{:S(2)}, u32[]{:S(2)}) collective-permute-start(bf16[8,64,256]{2,1,0:T(8,128)(2,1)S(1)} %pad_maximum_fusion.refs_0_), channel_id=1, source_target_pairs={{0,2},{1,3},{2,0},{3,1},{4,6},{5,7},{6,4},{7,5},{8,10},{9,11},{10,... | collective-permute-start | bytes 786440 | tf_op jit(solution)/shard_map/ppermute | solution.py:28
  16.7 10.8 %collective-permute-start.6 = (bf16[8,64,256]{2,1,0:T(8,128)(2,1)S(1)}, bf16[8,64,256]{2,1,0:T(8,128)(2,1)S(1)}, u32[]{:S(2)}, u32[]{:S(2)}) collective-permute-start(bf16[8,64,256]{2,1,0:T(8,128)(2,1)S(1)} %pad_maximum_fusion.refs_0_), channel_id=1, source_target_pairs={{0,1},{1,0},{2,3},{3,2},{4,5},{5,4},{6,7},{7,6},{8,9},{9,8},{10,11... | collective-permute-start | bytes 786440 | tf_op jit(solution)/shard_map/ppermute | solution.py:28
  65.9 9.0 %collective-permute-start.18 = (bf16[2,64,256]{2,1,0:T(8,128)(2,1)}, bf16[2,64,256]{2,1,0:T(8,128)(2,1)S(1)}, u32[]{:S(2)}, u32[]{:S(2)}) collective-permute-start(bf16[2,64,256]{2,1,0:T(8,128)(2,1)} %get-tuple-element.31), channel_id=1, source_target_pairs={{0,24},{1,25},{2,26},{3,27},{4,28},{5,29},{6,30},{7,31},{8,16},{9,... | collective-permute-start | bytes 196616 | tf_op jit(solution)/shard_map/ppermute | solution.py:28
  67.3 7.6 %collective-permute-start.17 = (bf16[2,64,256]{2,1,0:T(8,128)(2,1)}, bf16[2,64,256]{2,1,0:T(8,128)(2,1)S(1)}, u32[]{:S(2)}, u32[]{:S(2)}) collective-permute-start(bf16[2,64,256]{2,1,0:T(8,128)(2,1)} %get-tuple-element.31), channel_id=1, source_target_pairs={{0,16},{1,17},{2,18},{3,19},{4,20},{5,21},{6,22},{7,23},{8,24},{9,... | collective-permute-start | bytes 196616 | tf_op jit(solution)/shard_map/ppermute | solution.py:28
  74.9 10.2 %collective-permute-start.21 = (bf16[8,64,256]{2,1,0:T(8,128)(2,1)S(1)}, bf16[8,64,256]{2,1,0:T(8,128)(2,1)S(1)}, u32[]{:S(2)}, u32[]{:S(2)}) collective-permute-start(bf16[8,64,256]{2,1,0:T(8,128)(2,1)S(1)} %constant_dynamic-update-slice_fusion.refs_0_), channel_id=1, source_target_pairs={{0,6},{1,7},{2,4},{3,5},{4,2},{5,3},{6,0},{7,1},{8,14},{9,15},{10,... | collective-permute-start | bytes 786440 | tf_op jit(solution)/shard_map/ppermute | solution.py:28
  76.8 13.0 %collective-permute-start.20 = (bf16[8,64,256]{2,1,0:T(8,128)(2,1)S(1)}, bf16[8,64,256]{2,1,0:T(8,128)(2,1)S(1)}, u32[]{:S(2)}, u32[]{:S(2)}) collective-permute-start(bf16[8,64,256]{2,1,0:T(8,128)(2,1)S(1)} %constant_dynamic-update-slice_fusion.refs_0_), channel_id=1, source_target_pairs={{0,4},{1,5},{2,6},{3,7},{4,0},{5,1},{6,2},{7,3},{8,12},{9,13},{10,... | collective-permute-start | bytes 786440 | tf_op jit(solution)/shard_map/ppermute | solution.py:28
  78.0 11.9 %collective-permute-start.19 = (bf16[8,64,256]{2,1,0:T(8,128)(2,1)S(1)}, bf16[8,64,256]{2,1,0:T(8,128)(2,1)S(1)}, u32[]{:S(2)}, u32[]{:S(2)}) collective-permute-start(bf16[8,64,256]{2,1,0:T(8,128)(2,1)S(1)} %constant_dynamic-update-slice_fusion.refs_0_), channel_id=1, source_target_pairs={{0,2},{1,3},{2,0},{3,1},{4,6},{5,7},{6,4},{7,5},{8,10},{9,11},{10,... | collective-permute-start | bytes 786440 | tf_op jit(solution)/shard_map/ppermute | solution.py:28
  78.5 11.8 %collective-permute-start.22 = (bf16[8,64,256]{2,1,0:T(8,128)(2,1)S(1)}, bf16[8,64,256]{2,1,0:T(8,128)(2,1)S(1)}, u32[]{:S(2)}, u32[]{:S(2)}) collective-permute-start(bf16[8,64,256]{2,1,0:T(8,128)(2,1)S(1)} %constant_dynamic-update-slice_fusion.refs_0_), channel_id=1, source_target_pairs={{0,1},{1,0},{2,3},{3,2},{4,5},{5,4},{6,7},{7,6},{8,9},{9,8},{10,11... | collective-permute-start | bytes 786440 | tf_op jit(solution)/shard_map/ppermute | solution.py:28
  128.9 9.0 %collective-permute-start.34 = (bf16[2,64,256]{2,1,0:T(8,128)(2,1)}, bf16[2,64,256]{2,1,0:T(8,128)(2,1)S(1)}, u32[]{:S(2)}, u32[]{:S(2)}) collective-permute-start(bf16[2,64,256]{2,1,0:T(8,128)(2,1)} %get-tuple-element.38), channel_id=1, source_target_pairs={{0,24},{1,25},{2,26},{3,27},{4,28},{5,29},{6,30},{7,31},{8,16},{9,... | collective-permute-start | bytes 196616 | tf_op jit(solution)/shard_map/ppermute | solution.py:28
  130.2 7.7 %collective-permute-start.33 = (bf16[2,64,256]{2,1,0:T(8,128)(2,1)}, bf16[2,64,256]{2,1,0:T(8,128)(2,1)S(1)}, u32[]{:S(2)}, u32[]{:S(2)}) collective-permute-start(bf16[2,64,256]{2,1,0:T(8,128)(2,1)} %get-tuple-element.38), channel_id=1, source_target_pairs={{0,16},{1,17},{2,18},{3,19},{4,20},{5,21},{6,22},{7,23},{8,24},{9,... | collective-permute-start | bytes 196616 | tf_op jit(solution)/shard_map/ppermute | solution.py:28
  130.6 6.6 %collective-permute-start.32 = (bf16[2,64,256]{2,1,0:T(8,128)(2,1)}, bf16[2,64,256]{2,1,0:T(8,128)(2,1)S(1)}, u32[]{:S(2)}, u32[]{:S(2)}) collective-permute-start(bf16[2,64,256]{2,1,0:T(8,128)(2,1)} %get-tuple-element.38), channel_id=1, source_target_pairs={{0,8},{1,9},{2,10},{3,11},{4,12},{5,13},{6,14},{7,15},{8,0},{9,1},... | collective-permute-start | bytes 196616 | tf_op jit(solution)/shard_map/ppermute | solution.py:28
  137.9 10.2 %collective-permute-start.37 = (bf16[8,64,256]{2,1,0:T(8,128)(2,1)S(1)}, bf16[8,64,256]{2,1,0:T(8,128)(2,1)S(1)}, u32[]{:S(2)}, u32[]{:S(2)}) collective-permute-start(bf16[8,64,256]{2,1,0:T(8,128)(2,1)S(1)} %constant_dynamic-update-slice_fusion.4.refs_0_), channel_id=1, source_target_pairs={{0,6},{1,7},{2,4},{3,5},{4,2},{5,3},{6,0},{7,1},{8,14},{9,15},{10,... | collective-permute-start | bytes 786440 | tf_op jit(solution)/shard_map/ppermute | solution.py:28
  139.7 13.0 %collective-permute-start.36 = (bf16[8,64,256]{2,1,0:T(8,128)(2,1)S(1)}, bf16[8,64,256]{2,1,0:T(8,128)(2,1)S(1)}, u32[]{:S(2)}, u32[]{:S(2)}) collective-permute-start(bf16[8,64,256]{2,1,0:T(8,128)(2,1)S(1)} %constant_dynamic-update-slice_fusion.4.refs_0_), channel_id=1, source_target_pairs={{0,4},{1,5},{2,6},{3,7},{4,0},{5,1},{6,2},{7,3},{8,12},{9,13},{10,... | collective-permute-start | bytes 786440 | tf_op jit(solution)/shard_map/ppermute | solution.py:28
  140.9 11.9 %collective-permute-start.35 = (bf16[8,64,256]{2,1,0:T(8,128)(2,1)S(1)}, bf16[8,64,256]{2,1,0:T(8,128)(2,1)S(1)}, u32[]{:S(2)}, u32[]{:S(2)}) collective-permute-start(bf16[8,64,256]{2,1,0:T(8,128)(2,1)S(1)} %constant_dynamic-update-slice_fusion.4.refs_0_), channel_id=1, source_target_pairs={{0,2},{1,3},{2,0},{3,1},{4,6},{5,7},{6,4},{7,5},{8,10},{9,11},{10,... | collective-permute-start | bytes 786440 | tf_op jit(solution)/shard_map/ppermute | solution.py:28
  141.4 11.8 %collective-permute-start.38 = (bf16[8,64,256]{2,1,0:T(8,128)(2,1)S(1)}, bf16[8,64,256]{2,1,0:T(8,128)(2,1)S(1)}, u32[]{:S(2)}, u32[]{:S(2)}) collective-permute-start(bf16[8,64,256]{2,1,0:T(8,128)(2,1)S(1)} %constant_dynamic-update-slice_fusion.4.refs_0_), channel_id=1, source_target_pairs={{0,1},{1,0},{2,3},{3,2},{4,5},{5,4},{6,7},{7,6},{8,9},{9,8},{10,11... | collective-permute-start | bytes 786440 | tf_op jit(solution)/shard_map/ppermute | solution.py:28
  192.0 9.0 %collective-permute-start.50 = (bf16[2,64,256]{2,1,0:T(8,128)(2,1)}, bf16[2,64,256]{2,1,0:T(8,128)(2,1)S(1)}, u32[]{:S(2)}, u32[]{:S(2)}) collective-permute-start(bf16[2,64,256]{2,1,0:T(8,128)(2,1)} %get-tuple-element.45), channel_id=1, source_target_pairs={{0,24},{1,25},{2,26},{3,27},{4,28},{5,29},{6,30},{7,31},{8,16},{9,... | collective-permute-start | bytes 196616 | tf_op jit(solution)/shard_map/ppermute | solution.py:28
  193.2 7.8 %collective-permute-start.49 = (bf16[2,64,256]{2,1,0:T(8,128)(2,1)}, bf16[2,64,256]{2,1,0:T(8,128)(2,1)S(1)}, u32[]{:S(2)}, u32[]{:S(2)}) collective-permute-start(bf16[2,64,256]{2,1,0:T(8,128)(2,1)} %get-tuple-element.45), channel_id=1, source_target_pairs={{0,16},{1,17},{2,18},{3,19},{4,20},{5,21},{6,22},{7,23},{8,24},{9,... | collective-permute-start | bytes 196616 | tf_op jit(solution)/shard_map/ppermute | solution.py:28
  201.0 10.2 %collective-permute-start.53 = (bf16[8,64,256]{2,1,0:T(8,128)(2,1)S(1)}, bf16[8,64,256]{2,1,0:T(8,128)(2,1)S(1)}, u32[]{:S(2)}, u32[]{:S(2)}) collective-permute-start(bf16[8,64,256]{2,1,0:T(8,128)(2,1)S(1)} %constant_dynamic-update-slice_fusion.8.refs_0_), channel_id=1, source_target_pairs={{0,6},{1,7},{2,4},{3,5},{4,2},{5,3},{6,0},{7,1},{8,14},{9,15},{10,... | collective-permute-start | bytes 786440 | tf_op jit(solution)/shard_map/ppermute | solution.py:28
  202.8 13.0 %collective-permute-start.52 = (bf16[8,64,256]{2,1,0:T(8,128)(2,1)S(1)}, bf16[8,64,256]{2,1,0:T(8,128)(2,1)S(1)}, u32[]{:S(2)}, u32[]{:S(2)}) collective-permute-start(bf16[8,64,256]{2,1,0:T(8,128)(2,1)S(1)} %constant_dynamic-update-slice_fusion.8.refs_0_), channel_id=1, source_target_pairs={{0,4},{1,5},{2,6},{3,7},{4,0},{5,1},{6,2},{7,3},{8,12},{9,13},{10,... | collective-permute-start | bytes 786440 | tf_op jit(solution)/shard_map/ppermute | solution.py:28
  204.1 11.9 %collective-permute-start.51 = (bf16[8,64,256]{2,1,0:T(8,128)(2,1)S(1)}, bf16[8,64,256]{2,1,0:T(8,128)(2,1)S(1)}, u32[]{:S(2)}, u32[]{:S(2)}) collective-permute-start(bf16[8,64,256]{2,1,0:T(8,128)(2,1)S(1)} %constant_dynamic-update-slice_fusion.8.refs_0_), channel_id=1, source_target_pairs={{0,2},{1,3},{2,0},{3,1},{4,6},{5,7},{6,4},{7,5},{8,10},{9,11},{10,... | collective-permute-start | bytes 786440 | tf_op jit(solution)/shard_map/ppermute | solution.py:28
  204.6 11.8 %collective-permute-start.54 = (bf16[8,64,256]{2,1,0:T(8,128)(2,1)S(1)}, bf16[8,64,256]{2,1,0:T(8,128)(2,1)S(1)}, u32[]{:S(2)}, u32[]{:S(2)}) collective-permute-start(bf16[8,64,256]{2,1,0:T(8,128)(2,1)S(1)} %constant_dynamic-update-slice_fusion.8.refs_0_), channel_id=1, source_target_pairs={{0,1},{1,0},{2,3},{3,2},{4,5},{5,4},{6,7},{7,6},{8,9},{9,8},{10,11... | collective-permute-start | bytes 786440 | tf_op jit(solution)/shard_map/ppermute | solution.py:28
  (65 other events, 240.6 us)

commit v3 on v2

--- a/solution.py
+++ b/solution.py
@@ -35,38 +35,46 @@
     return [val] + [xor_permute(val, p, count) for p in partners[1:]]
 
 
-def gather_of(val, groups, core, count):
-    for masks in groups[:-1]:
+def crossed_permute(val, even, odd, core, count):
+    return lax.ppermute(val, AXES, [(i, i ^ (odd if i & core else even)) for i in range(count)])
+
+
+def gather_of(val, groups, crossed, core, count):
+    for masks in groups:
         val = jnp.concatenate(spread(val, masks, count), axis=0)
-    pieces = spread(val, groups[-1], count)
+    one, two = crossed
+    near = crossed_permute(val, one, two, core, count)
+    far = crossed_permute(val, two, one, core, count)
+    both = crossed_permute(near, two, one, core, count)
+    pieces = [val, near, far, both]
     return pieces + [xor_permute(piece, core, count) for piece in pieces]
 
 
-def slot_of(diff, masks):
+def slot_of(me, other, groups, crossed, core):
+    diff = me ^ other
     slot = jnp.zeros_like(diff)
-    for place, mask in enumerate(masks):
-        slot = slot + jnp.where((diff & mask) != 0, 1 << place, 0)
-    return slot
-
-
-def matrix_kernel(rows, nbr, blk, chunk, count, slots, tiles, vec, res, diag, *refs):
-    pieces, (image, keep, give, held, whole, sems, piece_sems) = refs[:count], refs[count:]
+    place = 1
+    for masks in groups:
+        for mask in masks:
+            slot = slot + jnp.where((diff & mask) != 0, place, 0)
+            place *= 2
+    one, two = crossed
+    at_one = (other & core) != 0
+    first = jnp.where(at_one, diff & two, diff & one) != 0
+    second = jnp.where(at_one, diff & one, diff & two) != 0
+    slot = slot + jnp.where(first, place, 0) + jnp.where(second, 2 * place, 0)
+    return slot + jnp.where((diff & core) != 0, 4 * place, 0)
+
+
+def matrix_kernel(rows, nbr, blk, count, slots, tiles, vec, res, diag, *refs):
+    pieces, (image, keep, give, whole, piece_sems) = refs[:count], refs[count:]
     coef = 1.0 / (nbr * blk)
-    parts = rows * nbr // chunk
     each = whole.shape[0] // count
     arrivals = [
         pltpu.make_async_copy(piece, whole.at[pl.ds(i * each, each)], piece_sems.at[i])
         for i, piece in enumerate(pieces)
     ]
-    copies = []
-    for part in range(parts):
-        row, first = divmod(part * chunk, nbr)
-        copies.append(
-            pltpu.make_async_copy(
-                tiles.at[row, pl.ds(first, chunk)], held.at[pl.ds(part * chunk, chunk)], sems.at[part]
-            )
-        )
-    for copy in arrivals + copies:
+    for copy in arrivals:
         copy.start()
     for copy in arrivals:
         copy.wait()
@@ -75,11 +83,9 @@
         acc = jnp.zeros((n, blk), jnp.float32)
         for k in range(nbr):
             spot = row * nbr + k
-            if spot % chunk == 0:
-                copies[spot // chunk].wait()
             acc = acc + lax.dot_general(
                 whole[slots[spot]],
-                held[spot],
+                tiles[row, k],
                 (((1,), (1,)), ((), ())),
                 preferred_element_type=jnp.float32,
             )
@@ -100,24 +106,21 @@
 def apply_matrix(slots, pieces, tiles, vec, res, diag):
     rows, nbr, blk, _ = tiles.shape
     n = vec.shape[0]
-    chunk = 4
     vmem = pl.BlockSpec(memory_space=pltpu.VMEM)
     anywhere = pl.BlockSpec(memory_space=pl.ANY)
     half = jax.ShapeDtypeStruct((n, 2 * n), jnp.float32)
     blocks = sum(piece.shape[0] for piece in pieces)
     return pl.pallas_call(
-        functools.partial(matrix_kernel, rows, nbr, blk, chunk, len(pieces)),
+        functools.partial(matrix_kernel, rows, nbr, blk, len(pieces)),
         out_shape=(jax.ShapeDtypeStruct(vec.shape, jnp.float32), half, half),
-        in_specs=[pl.BlockSpec(memory_space=pltpu.SMEM), anywhere, vmem, vmem, vmem]
+        in_specs=[pl.BlockSpec(memory_space=pltpu.SMEM), vmem, vmem, vmem, vmem]
         + [anywhere] * len(pieces),
         out_specs=(vmem, vmem, vmem),
         scratch_shapes=[
-            pltpu.VMEM((rows * nbr, blk, blk), tiles.dtype),
             pltpu.VMEM((blocks, n, blk), tiles.dtype),
-            pltpu.SemaphoreType.DMA((rows * nbr // chunk,)),
             pltpu.SemaphoreType.DMA((len(pieces),)),
         ],
-        compiler_params=pltpu.CompilerParams(vmem_limit_bytes=40 * 1024 * 1024),
+        compiler_params=pltpu.CompilerParams(vmem_limit_bytes=12 * 1024 * 1024),
         name="matrix",
     )(slots, tiles, vec, res, diag, *pieces)
 
@@ -178,18 +181,18 @@
         out_shape=tuple(outs),
         in_specs=[pl.BlockSpec(memory_space=pltpu.SMEM)] + [space] * 6,
         out_specs=tuple([space] * len(outs)),
+        compiler_params=pltpu.CompilerParams(vmem_limit_bytes=8 * 1024 * 1024),
         name="small_last" if last else "small",
     )(core, mine, other, vec, res, sol, image)
 
 
-def body(groups, bits, core_bit, count, cols, right_side, diag_vals, tiles, col_ids):
+def body(groups, crossed, bits, core_bit, count, cols, right_side, diag_vals, tiles, col_ids):
     rows, nbr, blk, _ = tiles.shape
     n = right_side.shape[0]
     me = lax.axis_index("row") * cols + lax.axis_index("col")
     core = ((me & core_bit) != 0).astype(jnp.int32)[None]
     ids = col_ids.reshape(-1)
-    order = [mask for masks in groups for mask in masks] + [core_bit]
-    slots = slot_of(me ^ (ids // rows), order) * rows + ids % rows
+    slots = slot_of(me, ids // rows, groups, crossed, core_bit) * rows + ids % rows
     slots = jnp.concatenate([slots, core])
     diag = diag_vals[None, :]
     sol = jnp.zeros_like(right_side)
@@ -198,7 +201,7 @@
     rounded = right_side.astype(jnp.bfloat16).reshape(n, rows, blk).transpose(1, 0, 2)
     for step in range(ITERS):
         last = step + 1 == ITERS
-        pieces = gather_of(rounded, groups, core_bit, count)
+        pieces = gather_of(rounded, groups, crossed, core_bit, count)
         image, keep, give = apply_matrix(slots, pieces, tiles, vec, res, diag)
         mine = keep + xor_permute(give, core_bit, count)
         for mask in bits:
@@ -222,11 +225,12 @@
     count = mesh.shape["row"] * mesh.shape["col"]
     cols = mesh.shape["col"]
     bits = [1 << i for i in range(1, count.bit_length() - 1)]
-    major = [b for b in bits if b >= cols]
-    minor = [b for b in bits if b < cols]
+    crossed, rest = bits[:2], bits[2:]
+    major = [b for b in rest if b >= cols]
+    minor = [b for b in rest if b < cols]
     groups = [part[i : i + 2] for part in (major, minor) for i in range(0, len(part), 2)]
     return jax.shard_map(
-        functools.partial(body, groups, bits, 1, count, cols),
+        functools.partial(body, groups, crossed, bits, 1, count, cols),
         mesh=mesh,
         in_specs=placed,
         out_specs=(P(None, ("row", "col")), P(None, ("row", "col"))),

time: 255 us -> 226 us (0.89)
  local copies, waits for them, and re-layouts: 24.3 us -> 4.62 us
  Pallas kernels: 50.7 us -> 38.6 us
  starting transfers between devices: 48.5 us -> 52.2 us
    ppermute x64 -> x52, waiting for transfers between devices: 129 us -> 84 us  [xor_permute(): return lax.ppermute(val, AXES, [(i, i ^ mask) for i in range(count)])]
    ppermute x0 -> x12, waiting for transfers between devices: none -> 44.1 us  [crossed_permute(): lax.ppermute(val, AXES, [(i, i ^ (odd if i & core else even)) for i in ra...]
    unnamed x59 -> x17, local copies, waits for them, and re-layouts: 22.8 us -> 3.83 us
    ppermute x0 -> x12, starting transfers between devices: none -> 14.1 us  [crossed_permute(): lax.ppermute(val, AXES, [(i, i ^ (odd if i & core else even)) for i in ra...]
    ppermute x64 -> x52, starting transfers between devices: 48.5 us -> 38.1 us  [xor_permute(): return lax.ppermute(val, AXES, [(i, i ^ mask) for i in range(count)])]
    pallas_call x4, Pallas kernels: 34.4 us -> 27.9 us  [solve_step(): pl.pallas_call(functools.partial(solve_kernel, last), out_shape=tuple(out...]
    pallas_call x4, Pallas kernels: 16.2 us -> 10.8 us  [apply_matrix(): pl.pallas_call(functools.partial(matrix_kernel, rows, nbr, blk, len(piece...]
  transfers between devices with their start and end apart: 64 -> 64, of which waited for: 52 -> 44; matrix products, arithmetic and copies ran while one was open for 1% -> 0% of each run, Pallas kernels for 0% -> 0%
where the time goes in v3:
time: 226 us
  waiting for transfers between devices  128 us (57%)
  starting transfers between devices  52.2 us (23%)
  Pallas kernels  38.6 us (17%)
  local copies, waits for them, and re-layouts  4.62 us (2%)
    ppermute x52, waiting for transfers between devices, xor_permute(): return lax.ppermute(val, AXES, [(i, i ^ mask) for i in range(count)])  84 us
    ppermute x12, waiting for transfers between devices, crossed_permute(): lax.ppermute(val, AXES, [(i, i ^ (odd if i & core else even)) for i in ra...  44.1 us
    ppermute x52, starting transfers between devices, xor_permute(): return lax.ppermute(val, AXES, [(i, i ^ mask) for i in range(count)])  38.1 us
    pallas_call x4, Pallas kernels, solve_step(): pl.pallas_call(functools.partial(solve_kernel, last), out_shape=tuple(out...  27.9 us
    ppermute x12, starting transfers between devices, crossed_permute(): lax.ppermute(val, AXES, [(i, i ^ (odd if i & core else even)) for i in ra...  14.1 us
    pallas_call x4, Pallas kernels, apply_matrix(): pl.pallas_call(functools.partial(matrix_kernel, rows, nbr, blk, len(piece...  10.8 us
  transfers between devices with their start and end apart: 64, of which 44 were waited for; matrix products, arithmetic and copies ran while one was open for 0% of the time, Pallas kernels for 0%

profile of v3, /device:TPU:0, one launch (start us, length us, event | category | flops | bytes accessed | tf_op | source)
XLA Modules:
  0.0 225.7 jit_solution(1284991377214032774)
XLA Ops:
  1.6 5.1 %collective-permute-start.2 = (bf16[2,64,256]{2,1,0:T(8,128)(2,1)S(1)}, bf16[2,64,256]{2,1,0:T(8,128)(2,1)S(1)}, u32[]{:S(2)}, u32[]{:S(2)}) collective-permute-start(bf16[2,64,256]{2,1,0:T(8,128)(2,1)S(1)} %bitcast.14), channel_id=1, source_target_pairs={{0,24},{1,25},{2,26},{3,27},{4,28},{5,29},{6,30},{7,31},{8,16},{9,... | collective-permute-start | bytes 196616 | tf_op jit(solution)/shard_map/ppermute | solution.py:28
  15.4 6.0 %collective-permute-done.3.refs_1_ = bf16[8,64,256]{2,1,0:T(8,128)(2,1)S(1)} collective-permute-done((bf16[8,64,256]{2,1,0:T(8,128)(2,1)S(1)}, bf16[8,64,256]{2,1,0:T(8,128)(2,1)S(1)}, u32[]{:S(2)}, u32[]{:S(2)}) %collective-permute-start.3) | collective-permute-done | bytes 262176 | tf_op jit(solution)/shard_map/ppermute | solution.py:39
  23.3 4.5 %collective-permute-done.5.refs_3_ = bf16[8,64,256]{2,1,0:T(8,128)(2,1)S(1)} collective-permute-done((bf16[8,64,256]{2,1,0:T(8,128)(2,1)S(1)}, bf16[8,64,256]{2,1,0:T(8,128)(2,1)S(1)}, u32[]{:S(2)}, u32[]{:S(2)}) %collective-permute-start.5) | collective-permute-done | bytes 262176 | tf_op jit(solution)/shard_map/ppermute | solution.py:39
  41.6 3.3 %collective-permute-done.12 = f32[64,128]{1,0:T(8,128)S(1)} collective-permute-done((f32[64,128]{1,0:T(8,128)S(1)}, f32[64,128]{1,0:T(8,128)S(1)}, u32[]{:S(2)}, u32[]{:S(2)}) %collective-permute-start.12) | collective-permute-done | bytes 32800 | tf_op jit(solution)/shard_map/ppermute | solution.py:28
  54.9 7.0 %small.3 = (f32[64,512]{1,0:T(8,128)S(1)}, f32[64,512]{1,0:T(8,128)S(1)}, f32[64,512]{1,0:T(8,128)S(1)}, bf16[2,64,256]{2,1,0:T(8,128)(2,1)S(1)}) custom-call(s32[1]{0:T(128)} %bitcast.core, f32[64,128]{1,0:T(8,128)S(1)} %add.96.mine, f32[64,128]{1,0:T(8,128)S(1)} %collective-permute-done.15.other, f32[64,512]{1,0:T(8,128)S(1)} %copy-done.1, ...), custom_call_target="tpu_custom_call" | custom-call | tf_op jit(solution)/shard_map/small/pallas_call | solution.py:179
  61.9 3.2 %collective-permute-start.18 = (bf16[2,64,256]{2,1,0:T(8,128)(2,1)S(1)}, bf16[2,64,256]{2,1,0:T(8,128)(2,1)S(1)}, u32[]{:S(2)}, u32[]{:S(2)}) collective-permute-start(bf16[2,64,256]{2,1,0:T(8,128)(2,1)S(1)} %get-tuple-element.31), channel_id=1, source_target_pairs={{0,24},{1,25},{2,26},{3,27},{4,28},{5,29},{6,30},{7,31},{8,16},{9,... | collective-permute-start | bytes 196616 | tf_op jit(solution)/shard_map/ppermute | solution.py:28
  66.3 3.4 %collective-permute-done.16 = bf16[2,64,256]{2,1,0:T(8,128)(2,1)S(1)} collective-permute-done((bf16[2,64,256]{2,1,0:T(8,128)(2,1)S(1)}, bf16[2,64,256]{2,1,0:T(8,128)(2,1)S(1)}, u32[]{:S(2)}, u32[]{:S(2)}) %collective-permute-start.16) | collective-permute-done | bytes 65568 | tf_op jit(solution)/shard_map/ppermute | solution.py:28
  73.3 6.4 %collective-permute-done.19.refs_1_ = bf16[8,64,256]{2,1,0:T(8,128)(2,1)S(1)} collective-permute-done((bf16[8,64,256]{2,1,0:T(8,128)(2,1)S(1)}, bf16[8,64,256]{2,1,0:T(8,128)(2,1)S(1)}, u32[]{:S(2)}, u32[]{:S(2)}) %collective-permute-start.19) | collective-permute-done | bytes 262176 | tf_op jit(solution)/shard_map/ppermute | solution.py:39
  81.4 4.7 %collective-permute-done.21.refs_3_ = bf16[8,64,256]{2,1,0:T(8,128)(2,1)S(1)} collective-permute-done((bf16[8,64,256]{2,1,0:T(8,128)(2,1)S(1)}, bf16[8,64,256]{2,1,0:T(8,128)(2,1)S(1)}, u32[]{:S(2)}, u32[]{:S(2)}) %collective-permute-start.21) | collective-permute-done | bytes 262176 | tf_op jit(solution)/shard_map/ppermute | solution.py:39
  99.4 3.9 %collective-permute-done.29 = f32[64,128]{1,0:T(8,128)S(1)} collective-permute-done((f32[64,128]{1,0:T(8,128)S(1)}, f32[64,128]{1,0:T(8,128)S(1)}, u32[]{:S(2)}, u32[]{:S(2)}) %collective-permute-start.29) | collective-permute-done | bytes 32800 | tf_op jit(solution)/shard_map/ppermute | solution.py:28
  104.2 3.9 %collective-permute-done.30 = f32[64,128]{1,0:T(8,128)S(1)} collective-permute-done((f32[64,128]{1,0:T(8,128)S(1)}, f32[64,128]{1,0:T(8,128)S(1)}, u32[]{:S(2)}, u32[]{:S(2)}) %collective-permute-start.30) | collective-permute-done | bytes 32800 | tf_op jit(solution)/shard_map/ppermute | solution.py:28
  109.3 7.0 %small.4 = (f32[64,512]{1,0:T(8,128)S(1)}, f32[64,512]{1,0:T(8,128)S(1)}, f32[64,512]{1,0:T(8,128)S(1)}, bf16[2,64,256]{2,1,0:T(8,128)(2,1)S(1)}) custom-call(s32[1]{0:T(128)} %bitcast.core, f32[64,128]{1,0:T(8,128)S(1)} %add.101.mine, f32[64,128]{1,0:T(8,128)S(1)} %collective-permute-done.31.other, f32[64,512]{1,0:T(8,128)S(1)} %get-tuple-element.29.vec, ...), custom_call_target="tpu_custom_call" | custom-call | tf_op jit(solution)/shard_map/small/pallas_call | solution.py:179
  120.8 3.5 %collective-permute-done.32 = bf16[2,64,256]{2,1,0:T(8,128)(2,1)S(1)} collective-permute-done((bf16[2,64,256]{2,1,0:T(8,128)(2,1)S(1)}, bf16[2,64,256]{2,1,0:T(8,128)(2,1)S(1)}, u32[]{:S(2)}, u32[]{:S(2)}) %collective-permute-start.32) | collective-permute-done | bytes 65568 | tf_op jit(solution)/shard_map/ppermute | solution.py:28
  127.9 6.4 %collective-permute-done.35.refs_1_ = bf16[8,64,256]{2,1,0:T(8,128)(2,1)S(1)} collective-permute-done((bf16[8,64,256]{2,1,0:T(8,128)(2,1)S(1)}, bf16[8,64,256]{2,1,0:T(8,128)(2,1)S(1)}, u32[]{:S(2)}, u32[]{:S(2)}) %collective-permute-start.35) | collective-permute-done | bytes 262176 | tf_op jit(solution)/shard_map/ppermute | solution.py:39
  135.7 5.0 %collective-permute-done.37.refs_3_ = bf16[8,64,256]{2,1,0:T(8,128)(2,1)S(1)} collective-permute-done((bf16[8,64,256]{2,1,0:T(8,128)(2,1)S(1)}, bf16[8,64,256]{2,1,0:T(8,128)(2,1)S(1)}, u32[]{:S(2)}, u32[]{:S(2)}) %collective-permute-start.37) | collective-permute-done | bytes 262176 | tf_op jit(solution)/shard_map/ppermute | solution.py:39
  154.4 3.7 %collective-permute-done.45 = f32[64,128]{1,0:T(8,128)S(1)} collective-permute-done((f32[64,128]{1,0:T(8,128)S(1)}, f32[64,128]{1,0:T(8,128)S(1)}, u32[]{:S(2)}, u32[]{:S(2)}) %collective-permute-start.45) | collective-permute-done | bytes 32800 | tf_op jit(solution)/shard_map/ppermute | solution.py:28
  158.9 4.1 %collective-permute-done.46 = f32[64,128]{1,0:T(8,128)S(1)} collective-permute-done((f32[64,128]{1,0:T(8,128)S(1)}, f32[64,128]{1,0:T(8,128)S(1)}, u32[]{:S(2)}, u32[]{:S(2)}) %collective-permute-start.46) | collective-permute-done | bytes 32800 | tf_op jit(solution)/shard_map/ppermute | solution.py:28
  164.2 7.0 %small.5 = (f32[64,512]{1,0:T(8,128)S(1)}, f32[64,512]{1,0:T(8,128)S(1)}, f32[64,512]{1,0:T(8,128)S(1)}, bf16[2,64,256]{2,1,0:T(8,128)(2,1)S(1)}) custom-call(s32[1]{0:T(128)} %bitcast.core, f32[64,128]{1,0:T(8,128)S(1)} %add.106.mine, f32[64,128]{1,0:T(8,128)S(1)} %collective-permute-done.47.other, f32[64,512]{1,0:T(8,128)S(1)} %get-tuple-element.36.vec, ...), custom_call_target="tpu_custom_call" | custom-call | tf_op jit(solution)/shard_map/small/pallas_call | solution.py:179
  175.6 3.7 %collective-permute-done.48 = bf16[2,64,256]{2,1,0:T(8,128)(2,1)S(1)} collective-permute-done((bf16[2,64,256]{2,1,0:T(8,128)(2,1)S(1)}, bf16[2,64,256]{2,1,0:T(8,128)(2,1)S(1)}, u32[]{:S(2)}, u32[]{:S(2)}) %collective-permute-start.48) | collective-permute-done | bytes 65568 | tf_op jit(solution)/shard_map/ppermute | solution.py:28
  182.4 6.4 %collective-permute-done.51.refs_1_ = bf16[8,64,256]{2,1,0:T(8,128)(2,1)S(1)} collective-permute-done((bf16[8,64,256]{2,1,0:T(8,128)(2,1)S(1)}, bf16[8,64,256]{2,1,0:T(8,128)(2,1)S(1)}, u32[]{:S(2)}, u32[]{:S(2)}) %collective-permute-start.51) | collective-permute-done | bytes 262176 | tf_op jit(solution)/shard_map/ppermute | solution.py:39
  190.6 4.7 %collective-permute-done.53.refs_3_ = bf16[8,64,256]{2,1,0:T(8,128)(2,1)S(1)} collective-permute-done((bf16[8,64,256]{2,1,0:T(8,128)(2,1)S(1)}, bf16[8,64,256]{2,1,0:T(8,128)(2,1)S(1)}, u32[]{:S(2)}, u32[]{:S(2)}) %collective-permute-start.53) | collective-permute-done | bytes 262176 | tf_op jit(solution)/shard_map/ppermute | solution.py:39
  208.9 3.6 %collective-permute-done.61 = f32[64,128]{1,0:T(8,128)S(1)} collective-permute-done((f32[64,128]{1,0:T(8,128)S(1)}, f32[64,128]{1,0:T(8,128)S(1)}, u32[]{:S(2)}, u32[]{:S(2)}) %collective-permute-start.61) | collective-permute-done | bytes 32800 | tf_op jit(solution)/shard_map/ppermute | solution.py:28
  213.3 4.2 %collective-permute-done.62 = f32[64,128]{1,0:T(8,128)S(1)} collective-permute-done((f32[64,128]{1,0:T(8,128)S(1)}, f32[64,128]{1,0:T(8,128)S(1)}, u32[]{:S(2)}, u32[]{:S(2)}) %collective-permute-start.62) | collective-permute-done | bytes 32800 | tf_op jit(solution)/shard_map/ppermute | solution.py:28
  218.7 7.0 %small_last.1 = (f32[64,512]{1,0:T(8,128)}, f32[64,512]{1,0:T(8,128)}) custom-call(s32[1]{0:T(128)} %bitcast.core, f32[64,128]{1,0:T(8,128)S(1)} %add.111.mine, f32[64,128]{1,0:T(8,128)S(1)} %collective-permute-done.63.other, f32[64,512]{1,0:T(8,128)S(1)} %get-tuple-element.43.vec, f32[64,512]{1,0:T(8,128)S(1)} %get-tuple-element.44.res, ...), custom_call_target="tpu_custom_call" | custom-call | tf_op jit(solution)/shard_map/small_last/pallas_call | solution.py:179
  (159 shorter events, 107.2 us)
Async XLA Ops:
  1.6 7.7 %collective-permute-start.2 = (bf16[2,64,256]{2,1,0:T(8,128)(2,1)S(1)}, bf16[2,64,256]{2,1,0:T(8,128)(2,1)S(1)}, u32[]{:S(2)}, u32[]{:S(2)}) collective-permute-start(bf16[2,64,256]{2,1,0:T(8,128)(2,1)S(1)} %bitcast.14), channel_id=1, source_target_pairs={{0,24},{1,25},{2,26},{3,27},{4,28},{5,29},{6,30},{7,31},{8,16},{9,... | collective-permute-start | bytes 196616 | tf_op jit(solution)/shard_map/ppermute | solution.py:28
  6.7 5.6 %collective-permute-start.1 = (bf16[2,64,256]{2,1,0:T(8,128)(2,1)S(1)}, bf16[2,64,256]{2,1,0:T(8,128)(2,1)S(1)}, u32[]{:S(2)}, u32[]{:S(2)}) collective-permute-start(bf16[2,64,256]{2,1,0:T(8,128)(2,1)S(1)} %bitcast.15), channel_id=1, source_target_pairs={{0,16},{1,17},{2,18},{3,19},{4,20},{5,21},{6,22},{7,23},{8,24},{9,... | collective-permute-start | bytes 196616 | tf_op jit(solution)/shard_map/ppermute | solution.py:28
  6.7 5.6 %collective-permute-start = (bf16[2,64,256]{2,1,0:T(8,128)(2,1)S(1)}, bf16[2,64,256]{2,1,0:T(8,128)(2,1)S(1)}, u32[]{:S(2)}, u32[]{:S(2)}) collective-permute-start(bf16[2,64,256]{2,1,0:T(8,128)(2,1)S(1)} %bitcast.16), channel_id=1, source_target_pairs={{0,8},{1,9},{2,10},{3,11},{4,12},{5,13},{6,14},{7,15},{8,0},{9,1},... | collective-permute-start | bytes 196616 | tf_op jit(solution)/shard_map/ppermute | solution.py:28
  12.3 9.1 %collective-permute-start.3 = (bf16[8,64,256]{2,1,0:T(8,128)(2,1)S(1)}, bf16[8,64,256]{2,1,0:T(8,128)(2,1)S(1)}, u32[]{:S(2)}, u32[]{:S(2)}) collective-permute-start(bf16[8,64,256]{2,1,0:T(8,128)(2,1)S(1)} %pad_maximum_fusion.refs_0_), channel_id=1, source_target_pairs={{0,2},{1,5},{2,0},{3,7},{4,6},{5,1},{6,4},{7,3},{8,10},{9,13},{10,... | collective-permute-start | bytes 786440 | tf_op jit(solution)/shard_map/ppermute | solution.py:39
  13.9 9.4 %collective-permute-start.4 = (bf16[8,64,256]{2,1,0:T(8,128)(2,1)S(1)}, bf16[8,64,256]{2,1,0:T(8,128)(2,1)S(1)}, u32[]{:S(2)}, u32[]{:S(2)}) collective-permute-start(bf16[8,64,256]{2,1,0:T(8,128)(2,1)S(1)} %pad_maximum_fusion.refs_0_), channel_id=1, source_target_pairs={{0,4},{1,3},{2,6},{3,1},{4,0},{5,7},{6,2},{7,5},{8,12},{9,11},{10,... | collective-permute-start | bytes 786440 | tf_op jit(solution)/shard_map/ppermute | solution.py:39
  21.5 6.4 %collective-permute-start.5 = (bf16[8,64,256]{2,1,0:T(8,128)(2,1)S(1)}, bf16[8,64,256]{2,1,0:T(8,128)(2,1)S(1)}, u32[]{:S(2)}, u32[]{:S(2)}) collective-permute-start(bf16[8,64,256]{2,1,0:T(8,128)(2,1)S(1)} %collective-permute-done.3.refs_1_), channel_id=1, source_target_pairs={{0,4},{1,3},{2,6},{3,1},{4,0},{5,7},{6,2},{7,5},{8,12},{9,11},{10,... | collective-permute-start | bytes 786440 | tf_op jit(solution)/shard_map/ppermute | solution.py:39
  61.9 9.4 %collective-permute-start.18 = (bf16[2,64,256]{2,1,0:T(8,128)(2,1)S(1)}, bf16[2,64,256]{2,1,0:T(8,128)(2,1)S(1)}, u32[]{:S(2)}, u32[]{:S(2)}) collective-permute-start(bf16[2,64,256]{2,1,0:T(8,128)(2,1)S(1)} %get-tuple-element.31), channel_id=1, source_target_pairs={{0,24},{1,25},{2,26},{3,27},{4,28},{5,29},{6,30},{7,31},{8,16},{9,... | collective-permute-start | bytes 196616 | tf_op jit(solution)/shard_map/ppermute | solution.py:28
  65.1 6.1 %collective-permute-start.17 = (bf16[2,64,256]{2,1,0:T(8,128)(2,1)S(1)}, bf16[2,64,256]{2,1,0:T(8,128)(2,1)S(1)}, u32[]{:S(2)}, u32[]{:S(2)}) collective-permute-start(bf16[2,64,256]{2,1,0:T(8,128)(2,1)S(1)} %get-tuple-element.31), channel_id=1, source_target_pairs={{0,16},{1,17},{2,18},{3,19},{4,20},{5,21},{6,22},{7,23},{8,24},{9,... | collective-permute-start | bytes 196616 | tf_op jit(solution)/shard_map/ppermute | solution.py:28
  71.3 8.4 %collective-permute-start.19 = (bf16[8,64,256]{2,1,0:T(8,128)(2,1)S(1)}, bf16[8,64,256]{2,1,0:T(8,128)(2,1)S(1)}, u32[]{:S(2)}, u32[]{:S(2)}) collective-permute-start(bf16[8,64,256]{2,1,0:T(8,128)(2,1)S(1)} %constant_dynamic-update-slice_fusion.refs_0_), channel_id=1, source_target_pairs={{0,2},{1,5},{2,0},{3,7},{4,6},{5,1},{6,4},{7,3},{8,10},{9,13},{10,... | collective-permute-start | bytes 786440 | tf_op jit(solution)/shard_map/ppermute | solution.py:39
  72.8 8.5 %collective-permute-start.20 = (bf16[8,64,256]{2,1,0:T(8,128)(2,1)S(1)}, bf16[8,64,256]{2,1,0:T(8,128)(2,1)S(1)}, u32[]{:S(2)}, u32[]{:S(2)}) collective-permute-start(bf16[8,64,256]{2,1,0:T(8,128)(2,1)S(1)} %constant_dynamic-update-slice_fusion.refs_0_), channel_id=1, source_target_pairs={{0,4},{1,3},{2,6},{3,1},{4,0},{5,7},{6,2},{7,5},{8,12},{9,11},{10,... | collective-permute-start | bytes 786440 | tf_op jit(solution)/shard_map/ppermute | solution.py:39
  79.7 6.4 %collective-permute-start.21 = (bf16[8,64,256]{2,1,0:T(8,128)(2,1)S(1)}, bf16[8,64,256]{2,1,0:T(8,128)(2,1)S(1)}, u32[]{:S(2)}, u32[]{:S(2)}) collective-permute-start(bf16[8,64,256]{2,1,0:T(8,128)(2,1)S(1)} %collective-permute-done.19.refs_1_), channel_id=1, source_target_pairs={{0,4},{1,3},{2,6},{3,1},{4,0},{5,7},{6,2},{7,5},{8,12},{9,11},{10,... | collective-permute-start | bytes 786440 | tf_op jit(solution)/shard_map/ppermute | solution.py:39
  116.3 8.8 %collective-permute-start.34 = (bf16[2,64,256]{2,1,0:T(8,128)(2,1)S(1)}, bf16[2,64,256]{2,1,0:T(8,128)(2,1)S(1)}, u32[]{:S(2)}, u32[]{:S(2)}) collective-permute-start(bf16[2,64,256]{2,1,0:T(8,128)(2,1)S(1)} %get-tuple-element.38), channel_id=1, source_target_pairs={{0,24},{1,25},{2,26},{3,27},{4,28},{5,29},{6,30},{7,31},{8,16},{9,... | collective-permute-start | bytes 196616 | tf_op jit(solution)/shard_map/ppermute | solution.py:28
  118.5 6.6 %collective-permute-start.33 = (bf16[2,64,256]{2,1,0:T(8,128)(2,1)S(1)}, bf16[2,64,256]{2,1,0:T(8,128)(2,1)S(1)}, u32[]{:S(2)}, u32[]{:S(2)}) collective-permute-start(bf16[2,64,256]{2,1,0:T(8,128)(2,1)S(1)} %get-tuple-element.38), channel_id=1, source_target_pairs={{0,16},{1,17},{2,18},{3,19},{4,20},{5,21},{6,22},{7,23},{8,24},{9,... | collective-permute-start | bytes 196616 | tf_op jit(solution)/shard_map/ppermute | solution.py:28
  118.5 5.8 %collective-permute-start.32 = (bf16[2,64,256]{2,1,0:T(8,128)(2,1)S(1)}, bf16[2,64,256]{2,1,0:T(8,128)(2,1)S(1)}, u32[]{:S(2)}, u32[]{:S(2)}) collective-permute-start(bf16[2,64,256]{2,1,0:T(8,128)(2,1)S(1)} %get-tuple-element.38), channel_id=1, source_target_pairs={{0,8},{1,9},{2,10},{3,11},{4,12},{5,13},{6,14},{7,15},{8,0},{9,1},... | collective-permute-start | bytes 196616 | tf_op jit(solution)/shard_map/ppermute | solution.py:28
  125.1 9.2 %collective-permute-start.35 = (bf16[8,64,256]{2,1,0:T(8,128)(2,1)S(1)}, bf16[8,64,256]{2,1,0:T(8,128)(2,1)S(1)}, u32[]{:S(2)}, u32[]{:S(2)}) collective-permute-start(bf16[8,64,256]{2,1,0:T(8,128)(2,1)S(1)} %constant_dynamic-update-slice_fusion.4.refs_0_), channel_id=1, source_target_pairs={{0,2},{1,5},{2,0},{3,7},{4,6},{5,1},{6,4},{7,3},{8,10},{9,13},{10,... | collective-permute-start | bytes 786440 | tf_op jit(solution)/shard_map/ppermute | solution.py:39
  126.7 9.0 %collective-permute-start.36 = (bf16[8,64,256]{2,1,0:T(8,128)(2,1)S(1)}, bf16[8,64,256]{2,1,0:T(8,128)(2,1)S(1)}, u32[]{:S(2)}, u32[]{:S(2)}) collective-permute-start(bf16[8,64,256]{2,1,0:T(8,128)(2,1)S(1)} %constant_dynamic-update-slice_fusion.4.refs_0_), channel_id=1, source_target_pairs={{0,4},{1,3},{2,6},{3,1},{4,0},{5,7},{6,2},{7,5},{8,12},{9,11},{10,... | collective-permute-start | bytes 786440 | tf_op jit(solution)/shard_map/ppermute | solution.py:39
  134.3 6.4 %collective-permute-start.37 = (bf16[8,64,256]{2,1,0:T(8,128)(2,1)S(1)}, bf16[8,64,256]{2,1,0:T(8,128)(2,1)S(1)}, u32[]{:S(2)}, u32[]{:S(2)}) collective-permute-start(bf16[8,64,256]{2,1,0:T(8,128)(2,1)S(1)} %collective-permute-done.35.refs_1_), channel_id=1, source_target_pairs={{0,4},{1,3},{2,6},{3,1},{4,0},{5,7},{6,2},{7,5},{8,12},{9,11},{10,... | collective-permute-start | bytes 786440 | tf_op jit(solution)/shard_map/ppermute | solution.py:39
  135.2 5.5 %collective-permute-start.39 = (bf16[8,64,256]{2,1,0:T(8,128)(2,1)S(1)}, bf16[8,64,256]{2,1,0:T(8,128)(2,1)S(1)}, u32[]{:S(2)}, u32[]{:S(2)}) collective-permute-start(bf16[8,64,256]{2,1,0:T(8,128)(2,1)S(1)} %collective-permute-done.35.refs_1_), channel_id=1, source_target_pairs={{0,1},{1,0},{2,3},{3,2},{4,5},{5,4},{6,7},{7,6},{8,9},{9,8},{10,11... | collective-permute-start | bytes 786440 | tf_op jit(solution)/shard_map/ppermute | solution.py:28
  171.1 8.8 %collective-permute-start.50 = (bf16[2,64,256]{2,1,0:T(8,128)(2,1)S(1)}, bf16[2,64,256]{2,1,0:T(8,128)(2,1)S(1)}, u32[]{:S(2)}, u32[]{:S(2)}) collective-permute-start(bf16[2,64,256]{2,1,0:T(8,128)(2,1)S(1)} %get-tuple-element.45), channel_id=1, source_target_pairs={{0,24},{1,25},{2,26},{3,27},{4,28},{5,29},{6,30},{7,31},{8,16},{9,... | collective-permute-start | bytes 196616 | tf_op jit(solution)/shard_map/ppermute | solution.py:28
  173.3 6.7 %collective-permute-start.49 = (bf16[2,64,256]{2,1,0:T(8,128)(2,1)S(1)}, bf16[2,64,256]{2,1,0:T(8,128)(2,1)S(1)}, u32[]{:S(2)}, u32[]{:S(2)}) collective-permute-start(bf16[2,64,256]{2,1,0:T(8,128)(2,1)S(1)} %get-tuple-element.45), channel_id=1, source_target_pairs={{0,16},{1,17},{2,18},{3,19},{4,20},{5,21},{6,22},{7,23},{8,24},{9,... | collective-permute-start | bytes 196616 | tf_op jit(solution)/shard_map/ppermute | solution.py:28
  173.3 6.0 %collective-permute-start.48 = (bf16[2,64,256]{2,1,0:T(8,128)(2,1)S(1)}, bf16[2,64,256]{2,1,0:T(8,128)(2,1)S(1)}, u32[]{:S(2)}, u32[]{:S(2)}) collective-permute-start(bf16[2,64,256]{2,1,0:T(8,128)(2,1)S(1)} %get-tuple-element.45), channel_id=1, source_target_pairs={{0,8},{1,9},{2,10},{3,11},{4,12},{5,13},{6,14},{7,15},{8,0},{9,1},... | collective-permute-start | bytes 196616 | tf_op jit(solution)/shard_map/ppermute | solution.py:28
  180.0 8.8 %collective-permute-start.51 = (bf16[8,64,256]{2,1,0:T(8,128)(2,1)S(1)}, bf16[8,64,256]{2,1,0:T(8,128)(2,1)S(1)}, u32[]{:S(2)}, u32[]{:S(2)}) collective-permute-start(bf16[8,64,256]{2,1,0:T(8,128)(2,1)S(1)} %constant_dynamic-update-slice_fusion.8.refs_0_), channel_id=1, source_target_pairs={{0,2},{1,5},{2,0},{3,7},{4,6},{5,1},{6,4},{7,3},{8,10},{9,13},{10,... | collective-permute-start | bytes 786440 | tf_op jit(solution)/shard_map/ppermute | solution.py:39
  181.6 9.0 %collective-permute-start.52 = (bf16[8,64,256]{2,1,0:T(8,128)(2,1)S(1)}, bf16[8,64,256]{2,1,0:T(8,128)(2,1)S(1)}, u32[]{:S(2)}, u32[]{:S(2)}) collective-permute-start(bf16[8,64,256]{2,1,0:T(8,128)(2,1)S(1)} %constant_dynamic-update-slice_fusion.8.refs_0_), channel_id=1, source_target_pairs={{0,4},{1,3},{2,6},{3,1},{4,0},{5,7},{6,2},{7,5},{8,12},{9,11},{10,... | collective-permute-start | bytes 786440 | tf_op jit(solution)/shard_map/ppermute | solution.py:39
  188.8 6.4 %collective-permute-start.53 = (bf16[8,64,256]{2,1,0:T(8,128)(2,1)S(1)}, bf16[8,64,256]{2,1,0:T(8,128)(2,1)S(1)}, u32[]{:S(2)}, u32[]{:S(2)}) collective-permute-start(bf16[8,64,256]{2,1,0:T(8,128)(2,1)S(1)} %collective-permute-done.51.refs_1_), channel_id=1, source_target_pairs={{0,4},{1,3},{2,6},{3,1},{4,0},{5,7},{6,2},{7,5},{8,12},{9,11},{10,... | collective-permute-start | bytes 786440 | tf_op jit(solution)/shard_map/ppermute | solution.py:39
  (44 other events, 221.7 us)

commit v4 on v3

--- a/solution.py
+++ b/solution.py
@@ -40,13 +40,16 @@
 
 
 def gather_of(val, groups, crossed, core, count):
-    for masks in groups:
+    for masks in groups[:-1]:
         val = jnp.concatenate(spread(val, masks, count), axis=0)
+    parts = spread(val, groups[-1], count)
+    half = len(parts) // 2
+    halves = [jnp.concatenate(parts[:half], axis=0), jnp.concatenate(parts[half:], axis=0)]
     one, two = crossed
-    near = crossed_permute(val, one, two, core, count)
-    far = crossed_permute(val, two, one, core, count)
-    both = crossed_permute(near, two, one, core, count)
-    pieces = [val, near, far, both]
+    near = [crossed_permute(part, one, two, core, count) for part in halves]
+    far = [crossed_permute(part, two, one, core, count) for part in halves]
+    both = [crossed_permute(part, two, one, core, count) for part in near]
+    pieces = halves + near + far + both
     return pieces + [xor_permute(piece, core, count) for piece in pieces]
 
 
@@ -103,6 +106,29 @@
     give[...] = jnp.where(core == 0, second, first)
 
 
+def round_kernel(source, target, same):
+    blk = target.shape[2]
+    for row in range(target.shape[0]):
+        target[row] = source[:, row * blk : (row + 1) * blk].astype(jnp.bfloat16)
+    same[...] = source[...]
+
+
+def round_blocks(source, rows):
+    n, width = source.shape
+    vmem = pl.BlockSpec(memory_space=pltpu.VMEM)
+    return pl.pallas_call(
+        round_kernel,
+        out_shape=(
+            jax.ShapeDtypeStruct((rows, n, width // rows), jnp.bfloat16),
+            jax.ShapeDtypeStruct(source.shape, source.dtype),
+        ),
+        in_specs=[vmem],
+        out_specs=(vmem, vmem),
+        compiler_params=pltpu.CompilerParams(vmem_limit_bytes=4 * 1024 * 1024),
+        name="round",
+    )(source)
+
+
 def apply_matrix(slots, pieces, tiles, vec, res, diag):
     rows, nbr, blk, _ = tiles.shape
     n = vec.shape[0]
@@ -126,23 +152,59 @@
 
 
 def invert_pair(mats, n):
-    rows = lax.broadcasted_iota(jnp.int32, (n, 2 * n), 0)
-    lanes = lax.broadcasted_iota(jnp.int32, (n, 2 * n), 1)
+    size = 8
+    width = 2 * n
+    lanes = lax.broadcasted_iota(jnp.int32, (size, width), 1)
+    rows = lax.broadcasted_iota(jnp.int32, (size, width), 0)
     left = lanes < n
     place = jnp.where(left, lanes, lanes - n)
-    for j in range(n):
-        col = jnp.where(
-            left,
-            jnp.broadcast_to(mats[:, j : j + 1], (n, 2 * n)),
-            jnp.broadcast_to(mats[:, n + j : n + j + 1], (n, 2 * n)),
-        )
-        pivot = col[j : j + 1, :]
-        inv = 1.0 / pivot
-        line = mats[j : j + 1, :]
-        scaled = jnp.where(place[0:1, :] == j, inv, line * inv)
-        kept = jnp.where(place == j, 0.0, mats)
-        mats = jnp.where(rows == j, jnp.broadcast_to(scaled, (n, 2 * n)), kept - col * scaled)
-    return mats
+    line_place = place[0:1, :]
+    blocks = [mats[i : i + size, :] for i in range(0, n, size)]
+    for at in range(n // size):
+        base = at * size
+        spread_cols = [
+            [
+                jnp.where(
+                    left,
+                    jnp.broadcast_to(block[:, base + i : base + i + 1], (size, width)),
+                    jnp.broadcast_to(block[:, n + base + i : n + base + i + 1], (size, width)),
+                )
+                for i in range(size)
+            ]
+            for block in blocks
+        ]
+        own = spread_cols[at]
+        inside = (line_place >= base) & (line_place < base + size)
+        lines = [
+            jnp.where(line_place == base + i, 1.0, jnp.where(inside, 0.0, blocks[at][i : i + 1, :]))
+            for i in range(size)
+        ]
+        upper = [[own[k][i : i + 1, :] if k >= i else None for k in range(size)] for i in range(size)]
+        for i in range(size):
+            inv = 1.0 / upper[i][i]
+            for m in range(i + 1, size):
+                factor = upper[i][m] * inv
+                for k in range(m, size):
+                    upper[m][k] = upper[m][k] - factor * upper[i][k]
+                lines[m] = lines[m] - factor * lines[i]
+            upper[i][i] = inv
+        for i in reversed(range(size)):
+            for k in range(i + 1, size):
+                lines[i] = lines[i] - upper[i][k] * lines[k]
+            lines[i] = lines[i] * upper[i][i]
+        within = (place >= base) & (place < base + size)
+        solved = jnp.broadcast_to(lines[0], (size, width))
+        for i in range(1, size):
+            solved = jnp.where(rows == i, jnp.broadcast_to(lines[i], (size, width)), solved)
+        for q, block in enumerate(blocks):
+            if q == at:
+                continue
+            kept = jnp.where(within, 0.0, block)
+            for i in range(size):
+                kept = kept - spread_cols[q][i] * lines[i]
+            blocks[q] = kept
+        blocks[at] = solved
+    return jnp.concatenate(blocks, axis=0)
 
 
 def solve_kernel(last, core, mine, other, vec, res, sol, image, *outs):
@@ -188,7 +250,6 @@
 
 def body(groups, crossed, bits, core_bit, count, cols, right_side, diag_vals, tiles, col_ids):
     rows, nbr, blk, _ = tiles.shape
-    n = right_side.shape[0]
     me = lax.axis_index("row") * cols + lax.axis_index("col")
     core = ((me & core_bit) != 0).astype(jnp.int32)[None]
     ids = col_ids.reshape(-1)
@@ -196,9 +257,8 @@
     slots = jnp.concatenate([slots, core])
     diag = diag_vals[None, :]
     sol = jnp.zeros_like(right_side)
-    res = right_side
-    vec = right_side
-    rounded = right_side.astype(jnp.bfloat16).reshape(n, rows, blk).transpose(1, 0, 2)
+    rounded, res = round_blocks(right_side, rows)
+    vec = res
     for step in range(ITERS):
         last = step + 1 == ITERS
         pieces = gather_of(rounded, groups, crossed, core_bit, count)

time: 226 us -> 211 us (0.934)
  waiting for transfers between devices: 128 us -> 95.3 us
  starting transfers between devices: 52.2 us -> 74.1 us
  Pallas kernels: 38.6 us -> 35.9 us
    ppermute x12 -> x24, waiting for transfers between devices: 44.1 us -> 26 us  [crossed_permute(): lax.ppermute(val, AXES, [(i, i ^ (odd if i & core else even)) for i in ra...]
    ppermute x52 -> x68, waiting for transfers between devices: 84 us -> 69.3 us  [xor_permute(): return lax.ppermute(val, AXES, [(i, i ^ mask) for i in range(count)])]
    pallas_call x4, Pallas kernels: 27.9 us -> 14.1 us  [solve_step(): pl.pallas_call(functools.partial(solve_kernel, last), out_shape=tuple(out...]
    ppermute x52 -> x68, starting transfers between devices: 38.1 us -> 49.3 us  [xor_permute(): return lax.ppermute(val, AXES, [(i, i ^ mask) for i in range(count)])]
    pallas_call x4, Pallas kernels: 10.8 us -> 21.7 us  [apply_matrix(): pl.pallas_call(functools.partial(matrix_kernel, rows, nbr, blk, len(piece...]
    ppermute x12 -> x24, starting transfers between devices: 14.1 us -> 24.8 us  [crossed_permute(): lax.ppermute(val, AXES, [(i, i ^ (odd if i & core else even)) for i in ra...]
  transfers between devices with their start and end apart: 64 -> 92, of which waited for: 44 -> 49; matrix products, arithmetic and copies ran while one was open for 0% -> 0% of each run, Pallas kernels for 0% -> 0%
where the time goes in v4:
time: 211 us
  waiting for transfers between devices  95.3 us (45%)
  starting transfers between devices  74.1 us (35%)
  Pallas kernels  35.9 us (17%)
  local copies, waits for them, and re-layouts  4.63 us (2%)
    ppermute x68, waiting for transfers between devices, xor_permute(): return lax.ppermute(val, AXES, [(i, i ^ mask) for i in range(count)])  69.3 us
    ppermute x68, starting transfers between devices, xor_permute(): return lax.ppermute(val, AXES, [(i, i ^ mask) for i in range(count)])  49.3 us
    ppermute x24, waiting for transfers between devices, crossed_permute(): lax.ppermute(val, AXES, [(i, i ^ (odd if i & core else even)) for i in ra...  26 us
    ppermute x24, starting transfers between devices, crossed_permute(): lax.ppermute(val, AXES, [(i, i ^ (odd if i & core else even)) for i in ra...  24.8 us
    pallas_call x4, Pallas kernels, apply_matrix(): pl.pallas_call(functools.partial(matrix_kernel, rows, nbr, blk, len(piece...  21.7 us
    pallas_call x4, Pallas kernels, solve_step(): pl.pallas_call(functools.partial(solve_kernel, last), out_shape=tuple(out...  14.1 us
  transfers between devices with their start and end apart: 92, of which 49 were waited for; matrix products, arithmetic and copies ran while one was open for 0% of the time, Pallas kernels for 0%

profile of v4, /device:TPU:0, one launch (start us, length us, event | category | flops | bytes accessed | tf_op | source)
XLA Modules:
  0.0 211.1 jit_solution(8176674120149985467)
XLA Ops:
  1.6 5.1 %collective-permute-start.2 = (bf16[2,64,256]{2,1,0:T(8,128)(2,1)S(1)}, bf16[2,64,256]{2,1,0:T(8,128)(2,1)S(1)}, u32[]{:S(2)}, u32[]{:S(2)}) collective-permute-start(bf16[2,64,256]{2,1,0:T(8,128)(2,1)S(1)} %get-tuple-element.29), channel_id=1, source_target_pairs={{0,24},{1,25},{2,26},{3,27},{4,28},{5,29},{6,30},{7,31},{8,16},{9,... | collective-permute-start | bytes 196616 | tf_op jit(solution)/shard_map/ppermute | solution.py:28
  7.3 3.6 %collective-permute-done = bf16[2,64,256]{2,1,0:T(8,128)(2,1)S(1)} collective-permute-done((bf16[2,64,256]{2,1,0:T(8,128)(2,1)S(1)}, bf16[2,64,256]{2,1,0:T(8,128)(2,1)S(1)}, u32[]{:S(2)}, u32[]{:S(2)}) %collective-permute-start) | collective-permute-done | bytes 65568 | tf_op jit(solution)/shard_map/ppermute | solution.py:28
  29.7 5.4 %matrix.4 = (f32[64,512]{1,0:T(8,128)S(1)}, f32[64,128]{1,0:T(8,128)S(1)}, f32[64,128]{1,0:T(8,128)S(1)}) custom-call(s32[33]{0:T(128)S(1)} %pad_add_fusion.slots, bf16[2,16,256,256]{3,2,1,0:T(8,128)(2,1)S(1)} %copy-done, f32[64,512]{1,0:T(8,128)S(1)} %get-tuple-element.28.vec.res, f32[64,512]{1,0:T(8,128)S(1)} %get-tuple-element.28.vec.res, ...), custom_call_target="tpu_custom_call" | custom-call | tf_op jit(solution)/shard_map/matrix/pallas_call | solution.py:139
  37.4 2.9 %collective-permute-done.18 = f32[64,128]{1,0:T(8,128)S(1)} collective-permute-done((f32[64,128]{1,0:T(8,128)S(1)}, f32[64,128]{1,0:T(8,128)S(1)}, u32[]{:S(2)}, u32[]{:S(2)}) %collective-permute-start.18) | collective-permute-done | bytes 32800 | tf_op jit(solution)/shard_map/ppermute | solution.py:28
  41.0 3.2 %collective-permute-done.19 = f32[64,128]{1,0:T(8,128)S(1)} collective-permute-done((f32[64,128]{1,0:T(8,128)S(1)}, f32[64,128]{1,0:T(8,128)S(1)}, u32[]{:S(2)}, u32[]{:S(2)}) %collective-permute-start.19) | collective-permute-done | bytes 32800 | tf_op jit(solution)/shard_map/ppermute | solution.py:28
  48.5 2.8 %collective-permute-start.21 = (f32[64,128]{1,0:T(8,128)S(1)}, f32[64,128]{1,0:T(8,128)S(1)}, u32[]{:S(2)}, u32[]{:S(2)}) collective-permute-start(f32[64,128]{1,0:T(8,128)S(1)} %add.95), channel_id=1, source_target_pairs={{0,16},{1,17},{2,18},{3,19},{4,20},{5,21},{6,22},{7,23},{8,24},{9,... | collective-permute-start | bytes 98312 | tf_op jit(solution)/shard_map/ppermute | solution.py:28
  54.5 3.7 %small.3 = (f32[64,512]{1,0:T(8,128)S(1)}, f32[64,512]{1,0:T(8,128)S(1)}, f32[64,512]{1,0:T(8,128)S(1)}, bf16[2,64,256]{2,1,0:T(8,128)(2,1)S(1)}) custom-call(s32[1]{0:T(128)} %bitcast.core, f32[64,128]{1,0:T(8,128)S(1)} %add.96.mine, f32[64,128]{1,0:T(8,128)S(1)} %collective-permute-done.22.other, f32[64,512]{1,0:T(8,128)S(1)} %get-tuple-element.28.vec.res, ...), custom_call_target="tpu_custom_call" | custom-call | tf_op jit(solution)/shard_map/small/pallas_call | solution.py:241
  58.2 2.9 %collective-permute-start.25 = (bf16[2,64,256]{2,1,0:T(8,128)(2,1)S(1)}, bf16[2,64,256]{2,1,0:T(8,128)(2,1)S(1)}, u32[]{:S(2)}, u32[]{:S(2)}) collective-permute-start(bf16[2,64,256]{2,1,0:T(8,128)(2,1)S(1)} %get-tuple-element.35), channel_id=1, source_target_pairs={{0,24},{1,25},{2,26},{3,27},{4,28},{5,29},{6,30},{7,31},{8,16},{9,... | collective-permute-start | bytes 196616 | tf_op jit(solution)/shard_map/ppermute | solution.py:28
  62.6 3.5 %collective-permute-done.23 = bf16[2,64,256]{2,1,0:T(8,128)(2,1)S(1)} collective-permute-done((bf16[2,64,256]{2,1,0:T(8,128)(2,1)S(1)}, bf16[2,64,256]{2,1,0:T(8,128)(2,1)S(1)}, u32[]{:S(2)}, u32[]{:S(2)}) %collective-permute-start.23) | collective-permute-done | bytes 65568 | tf_op jit(solution)/shard_map/ppermute | solution.py:28
  80.9 5.4 %matrix.5 = (f32[64,512]{1,0:T(8,128)S(1)}, f32[64,128]{1,0:T(8,128)S(1)}, f32[64,128]{1,0:T(8,128)S(1)}) custom-call(s32[33]{0:T(128)S(1)} %pad_add_fusion.slots, bf16[2,16,256,256]{3,2,1,0:T(8,128)(2,1)S(1)} %copy-done.1, f32[64,512]{1,0:T(8,128)S(1)} %get-tuple-element.33.vec, f32[64,512]{1,0:T(8,128)S(1)} %get-tuple-element.34.res, ...), custom_call_target="tpu_custom_call" | custom-call | tf_op jit(solution)/shard_map/matrix/pallas_call | solution.py:139
  92.4 3.0 %collective-permute-done.42 = f32[64,128]{1,0:T(8,128)S(1)} collective-permute-done((f32[64,128]{1,0:T(8,128)S(1)}, f32[64,128]{1,0:T(8,128)S(1)}, u32[]{:S(2)}, u32[]{:S(2)}) %collective-permute-start.42) | collective-permute-done | bytes 32800 | tf_op jit(solution)/shard_map/ppermute | solution.py:28
  105.6 3.6 %small.4 = (f32[64,512]{1,0:T(8,128)S(1)}, f32[64,512]{1,0:T(8,128)S(1)}, f32[64,512]{1,0:T(8,128)S(1)}, bf16[2,64,256]{2,1,0:T(8,128)(2,1)S(1)}) custom-call(s32[1]{0:T(128)} %bitcast.core, f32[64,128]{1,0:T(8,128)S(1)} %add.101.mine, f32[64,128]{1,0:T(8,128)S(1)} %collective-permute-done.45.other, f32[64,512]{1,0:T(8,128)S(1)} %get-tuple-element.33.vec, ...), custom_call_target="tpu_custom_call" | custom-call | tf_op jit(solution)/shard_map/small/pallas_call | solution.py:241
  109.3 2.8 %collective-permute-start.48 = (bf16[2,64,256]{2,1,0:T(8,128)(2,1)S(1)}, bf16[2,64,256]{2,1,0:T(8,128)(2,1)S(1)}, u32[]{:S(2)}, u32[]{:S(2)}) collective-permute-start(bf16[2,64,256]{2,1,0:T(8,128)(2,1)S(1)} %get-tuple-element.42), channel_id=1, source_target_pairs={{0,24},{1,25},{2,26},{3,27},{4,28},{5,29},{6,30},{7,31},{8,16},{9,... | collective-permute-start | bytes 196616 | tf_op jit(solution)/shard_map/ppermute | solution.py:28
  113.8 3.5 %collective-permute-done.46 = bf16[2,64,256]{2,1,0:T(8,128)(2,1)S(1)} collective-permute-done((bf16[2,64,256]{2,1,0:T(8,128)(2,1)S(1)}, bf16[2,64,256]{2,1,0:T(8,128)(2,1)S(1)}, u32[]{:S(2)}, u32[]{:S(2)}) %collective-permute-start.46) | collective-permute-done | bytes 65568 | tf_op jit(solution)/shard_map/ppermute | solution.py:28
  131.9 5.6 %matrix.6 = (f32[64,512]{1,0:T(8,128)S(1)}, f32[64,128]{1,0:T(8,128)S(1)}, f32[64,128]{1,0:T(8,128)S(1)}) custom-call(s32[33]{0:T(128)S(1)} %pad_add_fusion.slots, bf16[2,16,256,256]{3,2,1,0:T(8,128)(2,1)S(1)} %copy-done.1, f32[64,512]{1,0:T(8,128)S(1)} %get-tuple-element.40.vec, f32[64,512]{1,0:T(8,128)S(1)} %get-tuple-element.41.res, ...), custom_call_target="tpu_custom_call" | custom-call | tf_op jit(solution)/shard_map/matrix/pallas_call | solution.py:139
  139.8 2.8 %collective-permute-done.64 = f32[64,128]{1,0:T(8,128)S(1)} collective-permute-done((f32[64,128]{1,0:T(8,128)S(1)}, f32[64,128]{1,0:T(8,128)S(1)}, u32[]{:S(2)}, u32[]{:S(2)}) %collective-permute-start.64) | collective-permute-done | bytes 32800 | tf_op jit(solution)/shard_map/ppermute | solution.py:28
  152.7 2.7 %collective-permute-done.67 = f32[64,128]{1,0:T(8,128)S(1)} collective-permute-done((f32[64,128]{1,0:T(8,128)S(1)}, f32[64,128]{1,0:T(8,128)S(1)}, u32[]{:S(2)}, u32[]{:S(2)}) %collective-permute-start.67) | collective-permute-done | bytes 32800 | tf_op jit(solution)/shard_map/ppermute | solution.py:28
  156.6 3.6 %small.5 = (f32[64,512]{1,0:T(8,128)S(1)}, f32[64,512]{1,0:T(8,128)S(1)}, f32[64,512]{1,0:T(8,128)S(1)}, bf16[2,64,256]{2,1,0:T(8,128)(2,1)S(1)}) custom-call(s32[1]{0:T(128)} %bitcast.core, f32[64,128]{1,0:T(8,128)S(1)} %add.106.mine, f32[64,128]{1,0:T(8,128)S(1)} %collective-permute-done.68.other, f32[64,512]{1,0:T(8,128)S(1)} %get-tuple-element.40.vec, ...), custom_call_target="tpu_custom_call" | custom-call | tf_op jit(solution)/shard_map/small/pallas_call | solution.py:241
  160.2 3.3 %collective-permute-start.71 = (bf16[2,64,256]{2,1,0:T(8,128)(2,1)S(1)}, bf16[2,64,256]{2,1,0:T(8,128)(2,1)S(1)}, u32[]{:S(2)}, u32[]{:S(2)}) collective-permute-start(bf16[2,64,256]{2,1,0:T(8,128)(2,1)S(1)} %get-tuple-element.49), channel_id=1, source_target_pairs={{0,24},{1,25},{2,26},{3,27},{4,28},{5,29},{6,30},{7,31},{8,16},{9,... | collective-permute-start | bytes 196616 | tf_op jit(solution)/shard_map/ppermute | solution.py:28
  164.7 3.5 %collective-permute-done.69 = bf16[2,64,256]{2,1,0:T(8,128)(2,1)S(1)} collective-permute-done((bf16[2,64,256]{2,1,0:T(8,128)(2,1)S(1)}, bf16[2,64,256]{2,1,0:T(8,128)(2,1)S(1)}, u32[]{:S(2)}, u32[]{:S(2)}) %collective-permute-start.69) | collective-permute-done | bytes 65568 | tf_op jit(solution)/shard_map/ppermute | solution.py:28
  183.1 5.4 %matrix.7 = (f32[64,512]{1,0:T(8,128)S(1)}, f32[64,128]{1,0:T(8,128)S(1)}, f32[64,128]{1,0:T(8,128)S(1)}) custom-call(s32[33]{0:T(128)S(1)} %pad_add_fusion.slots, bf16[2,16,256,256]{3,2,1,0:T(8,128)(2,1)S(1)} %copy-done.1, f32[64,512]{1,0:T(8,128)S(1)} %get-tuple-element.47.vec, f32[64,512]{1,0:T(8,128)S(1)} %get-tuple-element.48.res, ...), custom_call_target="tpu_custom_call" | custom-call | tf_op jit(solution)/shard_map/matrix/pallas_call | solution.py:139
  190.7 2.9 %collective-permute-done.87 = f32[64,128]{1,0:T(8,128)S(1)} collective-permute-done((f32[64,128]{1,0:T(8,128)S(1)}, f32[64,128]{1,0:T(8,128)S(1)}, u32[]{:S(2)}, u32[]{:S(2)}) %collective-permute-start.87) | collective-permute-done | bytes 32800 | tf_op jit(solution)/shard_map/ppermute | solution.py:28
  194.6 3.0 %collective-permute-done.88 = f32[64,128]{1,0:T(8,128)S(1)} collective-permute-done((f32[64,128]{1,0:T(8,128)S(1)}, f32[64,128]{1,0:T(8,128)S(1)}, u32[]{:S(2)}, u32[]{:S(2)}) %collective-permute-start.88) | collective-permute-done | bytes 32800 | tf_op jit(solution)/shard_map/ppermute | solution.py:28
  207.9 3.2 %small_last.1 = (f32[64,512]{1,0:T(8,128)}, f32[64,512]{1,0:T(8,128)}) custom-call(s32[1]{0:T(128)} %bitcast.core, f32[64,128]{1,0:T(8,128)S(1)} %add.111.mine, f32[64,128]{1,0:T(8,128)S(1)} %collective-permute-done.91.other, f32[64,512]{1,0:T(8,128)S(1)} %get-tuple-element.47.vec, f32[64,512]{1,0:T(8,128)S(1)} %get-tuple-element.48.res, ...), custom_call_target="tpu_custom_call" | custom-call | tf_op jit(solution)/shard_map/small_last/pallas_call | solution.py:241
  (219 shorter events, 122.5 us)
Async XLA Ops:
  1.6 12.6 %collective-permute-start.2 = (bf16[2,64,256]{2,1,0:T(8,128)(2,1)S(1)}, bf16[2,64,256]{2,1,0:T(8,128)(2,1)S(1)}, u32[]{:S(2)}, u32[]{:S(2)}) collective-permute-start(bf16[2,64,256]{2,1,0:T(8,128)(2,1)S(1)} %get-tuple-element.29), channel_id=1, source_target_pairs={{0,24},{1,25},{2,26},{3,27},{4,28},{5,29},{6,30},{7,31},{8,16},{9,... | collective-permute-start | bytes 196616 | tf_op jit(solution)/shard_map/ppermute | solution.py:28
  6.7 7.5 %collective-permute-start.1 = (bf16[2,64,256]{2,1,0:T(8,128)(2,1)S(1)}, bf16[2,64,256]{2,1,0:T(8,128)(2,1)S(1)}, u32[]{:S(2)}, u32[]{:S(2)}) collective-permute-start(bf16[2,64,256]{2,1,0:T(8,128)(2,1)S(1)} %get-tuple-element.29), channel_id=1, source_target_pairs={{0,16},{1,17},{2,18},{3,19},{4,20},{5,21},{6,22},{7,23},{8,24},{9,... | collective-permute-start | bytes 196616 | tf_op jit(solution)/shard_map/ppermute | solution.py:28
  14.2 6.4 %collective-permute-start.4 = (bf16[4,64,256]{2,1,0:T(8,128)(2,1)S(1)}, bf16[4,64,256]{2,1,0:T(8,128)(2,1)S(1)}, u32[]{:S(2)}, u32[]{:S(2)}) collective-permute-start(bf16[4,64,256]{2,1,0:T(8,128)(2,1)S(1)} %constant_dynamic-update-slice_fusion.2.refs_1_), channel_id=1, source_target_pairs={{0,2},{1,5},{2,0},{3,7},{4,6},{5,1},{6,4},{7,3},{8,10},{9,13},{10,... | collective-permute-start | bytes 393224 | tf_op jit(solution)/shard_map/ppermute | solution.py:39
  14.8 7.2 %collective-permute-start.10 = (bf16[4,64,256]{2,1,0:T(8,128)(2,1)S(1)}, bf16[4,64,256]{2,1,0:T(8,128)(2,1)S(1)}, u32[]{:S(2)}, u32[]{:S(2)}) collective-permute-start(bf16[4,64,256]{2,1,0:T(8,128)(2,1)S(1)} %constant_dynamic-update-slice_fusion.2.refs_1_), channel_id=1, source_target_pairs={{0,1},{1,0},{2,3},{3,2},{4,5},{5,4},{6,7},{7,6},{8,9},{9,8},{10,11... | collective-permute-start | bytes 393224 | tf_op jit(solution)/shard_map/ppermute | solution.py:28
  14.8 7.2 %collective-permute-start.6 = (bf16[4,64,256]{2,1,0:T(8,128)(2,1)S(1)}, bf16[4,64,256]{2,1,0:T(8,128)(2,1)S(1)}, u32[]{:S(2)}, u32[]{:S(2)}) collective-permute-start(bf16[4,64,256]{2,1,0:T(8,128)(2,1)S(1)} %constant_dynamic-update-slice_fusion.2.refs_1_), channel_id=1, source_target_pairs={{0,4},{1,3},{2,6},{3,1},{4,0},{5,7},{6,2},{7,5},{8,12},{9,11},{10,... | collective-permute-start | bytes 393224 | tf_op jit(solution)/shard_map/ppermute | solution.py:39
  16.6 5.8 %collective-permute-start.13 = (bf16[4,64,256]{2,1,0:T(8,128)(2,1)S(1)}, bf16[4,64,256]{2,1,0:T(8,128)(2,1)S(1)}, u32[]{:S(2)}, u32[]{:S(2)}) collective-permute-start(bf16[4,64,256]{2,1,0:T(8,128)(2,1)S(1)} %collective-permute-done.5.refs_4_), channel_id=1, source_target_pairs={{0,1},{1,0},{2,3},{3,2},{4,5},{5,4},{6,7},{7,6},{8,9},{9,8},{10,11... | collective-permute-start | bytes 393224 | tf_op jit(solution)/shard_map/ppermute | solution.py:28
  58.2 10.3 %collective-permute-start.25 = (bf16[2,64,256]{2,1,0:T(8,128)(2,1)S(1)}, bf16[2,64,256]{2,1,0:T(8,128)(2,1)S(1)}, u32[]{:S(2)}, u32[]{:S(2)}) collective-permute-start(bf16[2,64,256]{2,1,0:T(8,128)(2,1)S(1)} %get-tuple-element.35), channel_id=1, source_target_pairs={{0,24},{1,25},{2,26},{3,27},{4,28},{5,29},{6,30},{7,31},{8,16},{9,... | collective-permute-start | bytes 196616 | tf_op jit(solution)/shard_map/ppermute | solution.py:28
  61.1 7.4 %collective-permute-start.24 = (bf16[2,64,256]{2,1,0:T(8,128)(2,1)S(1)}, bf16[2,64,256]{2,1,0:T(8,128)(2,1)S(1)}, u32[]{:S(2)}, u32[]{:S(2)}) collective-permute-start(bf16[2,64,256]{2,1,0:T(8,128)(2,1)S(1)} %get-tuple-element.35), channel_id=1, source_target_pairs={{0,16},{1,17},{2,18},{3,19},{4,20},{5,21},{6,22},{7,23},{8,24},{9,... | collective-permute-start | bytes 196616 | tf_op jit(solution)/shard_map/ppermute | solution.py:28
  66.2 6.2 %collective-permute-start.28 = (bf16[4,64,256]{2,1,0:T(8,128)(2,1)S(1)}, bf16[4,64,256]{2,1,0:T(8,128)(2,1)S(1)}, u32[]{:S(2)}, u32[]{:S(2)}) collective-permute-start(bf16[4,64,256]{2,1,0:T(8,128)(2,1)S(1)} %constant_dynamic-update-slice_fusion.4.refs_0_), channel_id=1, source_target_pairs={{0,4},{1,3},{2,6},{3,1},{4,0},{5,7},{6,2},{7,5},{8,12},{9,11},{10,... | collective-permute-start | bytes 393224 | tf_op jit(solution)/shard_map/ppermute | solution.py:39
  68.5 6.1 %collective-permute-start.27 = (bf16[4,64,256]{2,1,0:T(8,128)(2,1)S(1)}, bf16[4,64,256]{2,1,0:T(8,128)(2,1)S(1)}, u32[]{:S(2)}, u32[]{:S(2)}) collective-permute-start(bf16[4,64,256]{2,1,0:T(8,128)(2,1)S(1)} %constant_dynamic-update-slice_fusion.6.refs_1_), channel_id=1, source_target_pairs={{0,2},{1,5},{2,0},{3,7},{4,6},{5,1},{6,4},{7,3},{8,10},{9,13},{10,... | collective-permute-start | bytes 393224 | tf_op jit(solution)/shard_map/ppermute | solution.py:39
  69.4 6.2 %collective-permute-start.33 = (bf16[4,64,256]{2,1,0:T(8,128)(2,1)S(1)}, bf16[4,64,256]{2,1,0:T(8,128)(2,1)S(1)}, u32[]{:S(2)}, u32[]{:S(2)}) collective-permute-start(bf16[4,64,256]{2,1,0:T(8,128)(2,1)S(1)} %constant_dynamic-update-slice_fusion.6.refs_1_), channel_id=1, source_target_pairs={{0,1},{1,0},{2,3},{3,2},{4,5},{5,4},{6,7},{7,6},{8,9},{9,8},{10,11... | collective-permute-start | bytes 393224 | tf_op jit(solution)/shard_map/ppermute | solution.py:28
  69.4 6.3 %collective-permute-start.29 = (bf16[4,64,256]{2,1,0:T(8,128)(2,1)S(1)}, bf16[4,64,256]{2,1,0:T(8,128)(2,1)S(1)}, u32[]{:S(2)}, u32[]{:S(2)}) collective-permute-start(bf16[4,64,256]{2,1,0:T(8,128)(2,1)S(1)} %constant_dynamic-update-slice_fusion.6.refs_1_), channel_id=1, source_target_pairs={{0,4},{1,3},{2,6},{3,1},{4,0},{5,7},{6,2},{7,5},{8,12},{9,11},{10,... | collective-permute-start | bytes 393224 | tf_op jit(solution)/shard_map/ppermute | solution.py:39
  109.3 10.1 %collective-permute-start.48 = (bf16[2,64,256]{2,1,0:T(8,128)(2,1)S(1)}, bf16[2,64,256]{2,1,0:T(8,128)(2,1)S(1)}, u32[]{:S(2)}, u32[]{:S(2)}) collective-permute-start(bf16[2,64,256]{2,1,0:T(8,128)(2,1)S(1)} %get-tuple-element.42), channel_id=1, source_target_pairs={{0,24},{1,25},{2,26},{3,27},{4,28},{5,29},{6,30},{7,31},{8,16},{9,... | collective-permute-start | bytes 196616 | tf_op jit(solution)/shard_map/ppermute | solution.py:28
  112.1 7.3 %collective-permute-start.47 = (bf16[2,64,256]{2,1,0:T(8,128)(2,1)S(1)}, bf16[2,64,256]{2,1,0:T(8,128)(2,1)S(1)}, u32[]{:S(2)}, u32[]{:S(2)}) collective-permute-start(bf16[2,64,256]{2,1,0:T(8,128)(2,1)S(1)} %get-tuple-element.42), channel_id=1, source_target_pairs={{0,16},{1,17},{2,18},{3,19},{4,20},{5,21},{6,22},{7,23},{8,24},{9,... | collective-permute-start | bytes 196616 | tf_op jit(solution)/shard_map/ppermute | solution.py:28
  117.3 6.3 %collective-permute-start.51 = (bf16[4,64,256]{2,1,0:T(8,128)(2,1)S(1)}, bf16[4,64,256]{2,1,0:T(8,128)(2,1)S(1)}, u32[]{:S(2)}, u32[]{:S(2)}) collective-permute-start(bf16[4,64,256]{2,1,0:T(8,128)(2,1)S(1)} %constant_dynamic-update-slice_fusion.8.refs_0_), channel_id=1, source_target_pairs={{0,4},{1,3},{2,6},{3,1},{4,0},{5,7},{6,2},{7,5},{8,12},{9,11},{10,... | collective-permute-start | bytes 393224 | tf_op jit(solution)/shard_map/ppermute | solution.py:39
  119.4 6.2 %collective-permute-start.50 = (bf16[4,64,256]{2,1,0:T(8,128)(2,1)S(1)}, bf16[4,64,256]{2,1,0:T(8,128)(2,1)S(1)}, u32[]{:S(2)}, u32[]{:S(2)}) collective-permute-start(bf16[4,64,256]{2,1,0:T(8,128)(2,1)S(1)} %constant_dynamic-update-slice_fusion.10.refs_1_), channel_id=1, source_target_pairs={{0,2},{1,5},{2,0},{3,7},{4,6},{5,1},{6,4},{7,3},{8,10},{9,13},{10,... | collective-permute-start | bytes 393224 | tf_op jit(solution)/shard_map/ppermute | solution.py:39
  120.5 6.4 %collective-permute-start.56 = (bf16[4,64,256]{2,1,0:T(8,128)(2,1)S(1)}, bf16[4,64,256]{2,1,0:T(8,128)(2,1)S(1)}, u32[]{:S(2)}, u32[]{:S(2)}) collective-permute-start(bf16[4,64,256]{2,1,0:T(8,128)(2,1)S(1)} %constant_dynamic-update-slice_fusion.10.refs_1_), channel_id=1, source_target_pairs={{0,1},{1,0},{2,3},{3,2},{4,5},{5,4},{6,7},{7,6},{8,9},{9,8},{10,11... | collective-permute-start | bytes 393224 | tf_op jit(solution)/shard_map/ppermute | solution.py:28
  120.5 6.5 %collective-permute-start.52 = (bf16[4,64,256]{2,1,0:T(8,128)(2,1)S(1)}, bf16[4,64,256]{2,1,0:T(8,128)(2,1)S(1)}, u32[]{:S(2)}, u32[]{:S(2)}) collective-permute-start(bf16[4,64,256]{2,1,0:T(8,128)(2,1)S(1)} %constant_dynamic-update-slice_fusion.10.refs_1_), channel_id=1, source_target_pairs={{0,4},{1,3},{2,6},{3,1},{4,0},{5,7},{6,2},{7,5},{8,12},{9,11},{10,... | collective-permute-start | bytes 393224 | tf_op jit(solution)/shard_map/ppermute | solution.py:39
  160.2 10.1 %collective-permute-start.71 = (bf16[2,64,256]{2,1,0:T(8,128)(2,1)S(1)}, bf16[2,64,256]{2,1,0:T(8,128)(2,1)S(1)}, u32[]{:S(2)}, u32[]{:S(2)}) collective-permute-start(bf16[2,64,256]{2,1,0:T(8,128)(2,1)S(1)} %get-tuple-element.49), channel_id=1, source_target_pairs={{0,24},{1,25},{2,26},{3,27},{4,28},{5,29},{6,30},{7,31},{8,16},{9,... | collective-permute-start | bytes 196616 | tf_op jit(solution)/shard_map/ppermute | solution.py:28
  163.5 6.8 %collective-permute-start.70 = (bf16[2,64,256]{2,1,0:T(8,128)(2,1)S(1)}, bf16[2,64,256]{2,1,0:T(8,128)(2,1)S(1)}, u32[]{:S(2)}, u32[]{:S(2)}) collective-permute-start(bf16[2,64,256]{2,1,0:T(8,128)(2,1)S(1)} %get-tuple-element.49), channel_id=1, source_target_pairs={{0,16},{1,17},{2,18},{3,19},{4,20},{5,21},{6,22},{7,23},{8,24},{9,... | collective-permute-start | bytes 196616 | tf_op jit(solution)/shard_map/ppermute | solution.py:28
  168.2 6.3 %collective-permute-start.74 = (bf16[4,64,256]{2,1,0:T(8,128)(2,1)S(1)}, bf16[4,64,256]{2,1,0:T(8,128)(2,1)S(1)}, u32[]{:S(2)}, u32[]{:S(2)}) collective-permute-start(bf16[4,64,256]{2,1,0:T(8,128)(2,1)S(1)} %constant_dynamic-update-slice_fusion.12.refs_0_), channel_id=1, source_target_pairs={{0,4},{1,3},{2,6},{3,1},{4,0},{5,7},{6,2},{7,5},{8,12},{9,11},{10,... | collective-permute-start | bytes 393224 | tf_op jit(solution)/shard_map/ppermute | solution.py:39
  170.3 6.4 %collective-permute-start.73 = (bf16[4,64,256]{2,1,0:T(8,128)(2,1)S(1)}, bf16[4,64,256]{2,1,0:T(8,128)(2,1)S(1)}, u32[]{:S(2)}, u32[]{:S(2)}) collective-permute-start(bf16[4,64,256]{2,1,0:T(8,128)(2,1)S(1)} %constant_dynamic-update-slice_fusion.14.refs_1_), channel_id=1, source_target_pairs={{0,2},{1,5},{2,0},{3,7},{4,6},{5,1},{6,4},{7,3},{8,10},{9,13},{10,... | collective-permute-start | bytes 393224 | tf_op jit(solution)/shard_map/ppermute | solution.py:39
  171.4 6.2 %collective-permute-start.79 = (bf16[4,64,256]{2,1,0:T(8,128)(2,1)S(1)}, bf16[4,64,256]{2,1,0:T(8,128)(2,1)S(1)}, u32[]{:S(2)}, u32[]{:S(2)}) collective-permute-start(bf16[4,64,256]{2,1,0:T(8,128)(2,1)S(1)} %constant_dynamic-update-slice_fusion.14.refs_1_), channel_id=1, source_target_pairs={{0,1},{1,0},{2,3},{3,2},{4,5},{5,4},{6,7},{7,6},{8,9},{9,8},{10,11... | collective-permute-start | bytes 393224 | tf_op jit(solution)/shard_map/ppermute | solution.py:28
  171.4 6.3 %collective-permute-start.75 = (bf16[4,64,256]{2,1,0:T(8,128)(2,1)S(1)}, bf16[4,64,256]{2,1,0:T(8,128)(2,1)S(1)}, u32[]{:S(2)}, u32[]{:S(2)}) collective-permute-start(bf16[4,64,256]{2,1,0:T(8,128)(2,1)S(1)} %constant_dynamic-update-slice_fusion.14.refs_1_), channel_id=1, source_target_pairs={{0,4},{1,3},{2,6},{3,1},{4,0},{5,7},{6,2},{7,5},{8,12},{9,11},{10,... | collective-permute-start | bytes 393224 | tf_op jit(solution)/shard_map/ppermute | solution.py:39
  (73 other events, 366.2 us)

commit v5 on v4

--- a/solution.py
+++ b/solution.py
@@ -70,17 +70,12 @@
 
 
 def matrix_kernel(rows, nbr, blk, count, slots, tiles, vec, res, diag, *refs):
-    pieces, (image, keep, give, whole, piece_sems) = refs[:count], refs[count:]
+    pieces, (image, keep, give, whole) = refs[:count], refs[count:]
     coef = 1.0 / (nbr * blk)
-    each = whole.shape[0] // count
-    arrivals = [
-        pltpu.make_async_copy(piece, whole.at[pl.ds(i * each, each)], piece_sems.at[i])
-        for i, piece in enumerate(pieces)
-    ]
-    for copy in arrivals:
-        copy.start()
-    for copy in arrivals:
-        copy.wait()
+    first = 0
+    for piece in pieces:
+        whole[first : first + piece.shape[0]] = piece[...]
+        first += piece.shape[0]
     n = vec.shape[0]
     for row in range(rows):
         acc = jnp.zeros((n, blk), jnp.float32)
@@ -133,20 +128,19 @@
     rows, nbr, blk, _ = tiles.shape
     n = vec.shape[0]
     vmem = pl.BlockSpec(memory_space=pltpu.VMEM)
-    anywhere = pl.BlockSpec(memory_space=pl.ANY)
     half = jax.ShapeDtypeStruct((n, 2 * n), jnp.float32)
     blocks = sum(piece.shape[0] for piece in pieces)
+    grant = 2 * blocks * n * blk * 2 + tiles.size * 2 + 2 * 1024 * 1024
     return pl.pallas_call(
         functools.partial(matrix_kernel, rows, nbr, blk, len(pieces)),
         out_shape=(jax.ShapeDtypeStruct(vec.shape, jnp.float32), half, half),
         in_specs=[pl.BlockSpec(memory_space=pltpu.SMEM), vmem, vmem, vmem, vmem]
-        + [anywhere] * len(pieces),
+        + [vmem] * len(pieces),
         out_specs=(vmem, vmem, vmem),
         scratch_shapes=[
             pltpu.VMEM((blocks, n, blk), tiles.dtype),
-            pltpu.SemaphoreType.DMA((len(pieces),)),
         ],
-        compiler_params=pltpu.CompilerParams(vmem_limit_bytes=12 * 1024 * 1024),
+        compiler_params=pltpu.CompilerParams(vmem_limit_bytes=grant),
         name="matrix",
     )(slots, tiles, vec, res, diag, *pieces)
 
@@ -248,7 +242,7 @@
     )(core, mine, other, vec, res, sol, image)
 
 
-def body(groups, crossed, bits, core_bit, count, cols, right_side, diag_vals, tiles, col_ids):
+def body(groups, crossed, stages, core_bit, count, cols, right_side, diag_vals, tiles, col_ids):
     rows, nbr, blk, _ = tiles.shape
     me = lax.axis_index("row") * cols + lax.axis_index("col")
     core = ((me & core_bit) != 0).astype(jnp.int32)[None]
@@ -264,8 +258,8 @@
         pieces = gather_of(rounded, groups, crossed, core_bit, count)
         image, keep, give = apply_matrix(slots, pieces, tiles, vec, res, diag)
         mine = keep + xor_permute(give, core_bit, count)
-        for mask in bits:
-            mine = mine + xor_permute(mine, mask, count)
+        for even, odd in stages:
+            mine = mine + crossed_permute(mine, even, odd, core_bit, count)
         other = xor_permute(mine, core_bit, count)
         outs = solve_step(last, rows, core, mine, other, vec, res, sol, image)
         if last:
@@ -286,11 +280,15 @@
     cols = mesh.shape["col"]
     bits = [1 << i for i in range(1, count.bit_length() - 1)]
     crossed, rest = bits[:2], bits[2:]
+    stages = []
+    for i in range(0, len(bits), 2):
+        pair = bits[i : i + 2]
+        stages += [(pair[0], pair[-1]), (pair[-1], pair[0])][: len(pair)]
     major = [b for b in rest if b >= cols]
     minor = [b for b in rest if b < cols]
     groups = [part[i : i + 2] for part in (major, minor) for i in range(0, len(part), 2)]
     return jax.shard_map(
-        functools.partial(body, groups, crossed, bits, 1, count, cols),
+        functools.partial(body, groups, crossed, stages, 1, count, cols),
         mesh=mesh,
         in_specs=placed,
         out_specs=(P(None, ("row", "col")), P(None, ("row", "col"))),

time: 211 us -> 200 us (0.948)
  Pallas kernels: 35.9 us -> 24.2 us
    ppermute x68 -> x52, waiting for transfers between devices: 69.3 us -> 28.2 us  [xor_permute(): return lax.ppermute(val, AXES, [(i, i ^ mask) for i in range(count)])]
    ppermute x24 -> x40, waiting for transfers between devices: 26 us -> 66.9 us  [crossed_permute(): lax.ppermute(val, AXES, [(i, i ^ (odd if i & core else even)) for i in ra...]
    ppermute x24 -> x40, starting transfers between devices: 24.8 us -> 51.4 us  [crossed_permute(): lax.ppermute(val, AXES, [(i, i ^ (odd if i & core else even)) for i in ra...]
    ppermute x68 -> x52, starting transfers between devices: 49.3 us -> 22.9 us  [xor_permute(): return lax.ppermute(val, AXES, [(i, i ^ mask) for i in range(count)])]
    pallas_call x4, Pallas kernels: 21.7 us -> 10 us  [apply_matrix(): pl.pallas_call(functools.partial(matrix_kernel, rows, nbr, blk, len(piece...]
where the time goes in v5:
time: 200 us; the launch traced here: 199 us
  waiting for transfers between devices  95.1 us (48%)
  starting transfers between devices  74.3 us (37%)
  Pallas kernels  24.2 us (12%)
  local copies, waits for them, and re-layouts  4.63 us (2%)
    ppermute x40, waiting for transfers between devices, crossed_permute(): lax.ppermute(val, AXES, [(i, i ^ (odd if i & core else even)) for i in ra...  66.9 us
    ppermute x40, starting transfers between devices, crossed_permute(): lax.ppermute(val, AXES, [(i, i ^ (odd if i & core else even)) for i in ra...  51.4 us
    ppermute x52, waiting for transfers between devices, xor_permute(): return lax.ppermute(val, AXES, [(i, i ^ mask) for i in range(count)])  28.2 us
    ppermute x52, starting transfers between devices, xor_permute(): return lax.ppermute(val, AXES, [(i, i ^ mask) for i in range(count)])  22.9 us
    pallas_call x4, Pallas kernels, solve_step(): pl.pallas_call(functools.partial(solve_kernel, last), out_shape=tuple(out...  14.1 us
    pallas_call x4, Pallas kernels, apply_matrix(): pl.pallas_call(functools.partial(matrix_kernel, rows, nbr, blk, len(piece...  10 us
  transfers between devices with their start and end apart: 92, of which 49 were waited for; matrix products, arithmetic and copies ran while one was open for 0% of the time, Pallas kernels for 0%

profile of v5, /device:TPU:0, one launch (start us, length us, event | category | flops | bytes accessed | tf_op | source)
XLA Modules:
  0.0 199.4 jit_solution(5999831990559139839)
XLA Ops:
  1.6 5.1 %collective-permute-start.2 = (bf16[2,64,256]{2,1,0:T(8,128)(2,1)S(1)}, bf16[2,64,256]{2,1,0:T(8,128)(2,1)S(1)}, u32[]{:S(2)}, u32[]{:S(2)}) collective-permute-start(bf16[2,64,256]{2,1,0:T(8,128)(2,1)S(1)} %get-tuple-element.29), channel_id=1, source_target_pairs={{0,24},{1,25},{2,26},{3,27},{4,28},{5,29},{6,30},{7,31},{8,16},{9,... | collective-permute-start | bytes 196616 | tf_op jit(solution)/shard_map/ppermute | solution.py:28
  7.3 3.6 %collective-permute-done = bf16[2,64,256]{2,1,0:T(8,128)(2,1)S(1)} collective-permute-done((bf16[2,64,256]{2,1,0:T(8,128)(2,1)S(1)}, bf16[2,64,256]{2,1,0:T(8,128)(2,1)S(1)}, u32[]{:S(2)}, u32[]{:S(2)}) %collective-permute-start) | collective-permute-done | bytes 65568 | tf_op jit(solution)/shard_map/ppermute | solution.py:28
  34.5 2.9 %collective-permute-done.18 = f32[64,128]{1,0:T(8,128)S(1)} collective-permute-done((f32[64,128]{1,0:T(8,128)S(1)}, f32[64,128]{1,0:T(8,128)S(1)}, u32[]{:S(2)}, u32[]{:S(2)}) %collective-permute-start.18) | collective-permute-done | bytes 32800 | tf_op jit(solution)/shard_map/ppermute | solution.py:39
  38.1 3.2 %collective-permute-done.19 = f32[64,128]{1,0:T(8,128)S(1)} collective-permute-done((f32[64,128]{1,0:T(8,128)S(1)}, f32[64,128]{1,0:T(8,128)S(1)}, u32[]{:S(2)}, u32[]{:S(2)}) %collective-permute-start.19) | collective-permute-done | bytes 32800 | tf_op jit(solution)/shard_map/ppermute | solution.py:39
  45.6 2.5 %collective-permute-start.21 = (f32[64,128]{1,0:T(8,128)S(1)}, f32[64,128]{1,0:T(8,128)S(1)}, u32[]{:S(2)}, u32[]{:S(2)}) collective-permute-start(f32[64,128]{1,0:T(8,128)S(1)} %add.95), channel_id=1, source_target_pairs={{0,16},{1,9},{2,18},{3,11},{4,20},{5,13},{6,22},{7,15},{8,24},{9,1... | collective-permute-start | bytes 98312 | tf_op jit(solution)/shard_map/ppermute | solution.py:39
  51.6 3.6 %small.3 = (f32[64,512]{1,0:T(8,128)S(1)}, f32[64,512]{1,0:T(8,128)S(1)}, f32[64,512]{1,0:T(8,128)S(1)}, bf16[2,64,256]{2,1,0:T(8,128)(2,1)S(1)}) custom-call(s32[1]{0:T(128)} %bitcast.core, f32[64,128]{1,0:T(8,128)S(1)} %add.96.mine, f32[64,128]{1,0:T(8,128)S(1)} %collective-permute-done.22.other, f32[64,512]{1,0:T(8,128)S(1)} %get-tuple-element.28.vec.res, ...), custom_call_target="tpu_custom_call" | custom-call | tf_op jit(solution)/shard_map/small/pallas_call | solution.py:235
  55.3 2.9 %collective-permute-start.25 = (bf16[2,64,256]{2,1,0:T(8,128)(2,1)S(1)}, bf16[2,64,256]{2,1,0:T(8,128)(2,1)S(1)}, u32[]{:S(2)}, u32[]{:S(2)}) collective-permute-start(bf16[2,64,256]{2,1,0:T(8,128)(2,1)S(1)} %get-tuple-element.35), channel_id=1, source_target_pairs={{0,24},{1,25},{2,26},{3,27},{4,28},{5,29},{6,30},{7,31},{8,16},{9,... | collective-permute-start | bytes 196616 | tf_op jit(solution)/shard_map/ppermute | solution.py:28
  59.7 3.4 %collective-permute-done.23 = bf16[2,64,256]{2,1,0:T(8,128)(2,1)S(1)} collective-permute-done((bf16[2,64,256]{2,1,0:T(8,128)(2,1)S(1)}, bf16[2,64,256]{2,1,0:T(8,128)(2,1)S(1)}, u32[]{:S(2)}, u32[]{:S(2)}) %collective-permute-start.23) | collective-permute-done | bytes 65568 | tf_op jit(solution)/shard_map/ppermute | solution.py:28
  83.0 2.6 %collective-permute-done.41 = f32[64,128]{1,0:T(8,128)S(1)} collective-permute-done((f32[64,128]{1,0:T(8,128)S(1)}, f32[64,128]{1,0:T(8,128)S(1)}, u32[]{:S(2)}, u32[]{:S(2)}) %collective-permute-start.41) | collective-permute-done | bytes 32800 | tf_op jit(solution)/shard_map/ppermute | solution.py:39
  86.5 3.0 %collective-permute-done.42 = f32[64,128]{1,0:T(8,128)S(1)} collective-permute-done((f32[64,128]{1,0:T(8,128)S(1)}, f32[64,128]{1,0:T(8,128)S(1)}, u32[]{:S(2)}, u32[]{:S(2)}) %collective-permute-start.42) | collective-permute-done | bytes 32800 | tf_op jit(solution)/shard_map/ppermute | solution.py:39
  96.0 2.6 %collective-permute-done.44 = f32[64,128]{1,0:T(8,128)S(1)} collective-permute-done((f32[64,128]{1,0:T(8,128)S(1)}, f32[64,128]{1,0:T(8,128)S(1)}, u32[]{:S(2)}, u32[]{:S(2)}) %collective-permute-start.44) | collective-permute-done | bytes 32800 | tf_op jit(solution)/shard_map/ppermute | solution.py:39
  99.9 3.6 %small.4 = (f32[64,512]{1,0:T(8,128)S(1)}, f32[64,512]{1,0:T(8,128)S(1)}, f32[64,512]{1,0:T(8,128)S(1)}, bf16[2,64,256]{2,1,0:T(8,128)(2,1)S(1)}) custom-call(s32[1]{0:T(128)} %bitcast.core, f32[64,128]{1,0:T(8,128)S(1)} %add.101.mine, f32[64,128]{1,0:T(8,128)S(1)} %collective-permute-done.45.other, f32[64,512]{1,0:T(8,128)S(1)} %get-tuple-element.33.vec, ...), custom_call_target="tpu_custom_call" | custom-call | tf_op jit(solution)/shard_map/small/pallas_call | solution.py:235
  103.5 2.8 %collective-permute-start.48 = (bf16[2,64,256]{2,1,0:T(8,128)(2,1)S(1)}, bf16[2,64,256]{2,1,0:T(8,128)(2,1)S(1)}, u32[]{:S(2)}, u32[]{:S(2)}) collective-permute-start(bf16[2,64,256]{2,1,0:T(8,128)(2,1)S(1)} %get-tuple-element.42), channel_id=1, source_target_pairs={{0,24},{1,25},{2,26},{3,27},{4,28},{5,29},{6,30},{7,31},{8,16},{9,... | collective-permute-start | bytes 196616 | tf_op jit(solution)/shard_map/ppermute | solution.py:28
  108.0 3.4 %collective-permute-done.46 = bf16[2,64,256]{2,1,0:T(8,128)(2,1)S(1)} collective-permute-done((bf16[2,64,256]{2,1,0:T(8,128)(2,1)S(1)}, bf16[2,64,256]{2,1,0:T(8,128)(2,1)S(1)}, u32[]{:S(2)}, u32[]{:S(2)}) %collective-permute-start.46) | collective-permute-done | bytes 65568 | tf_op jit(solution)/shard_map/ppermute | solution.py:28
  130.8 2.8 %collective-permute-done.64 = f32[64,128]{1,0:T(8,128)S(1)} collective-permute-done((f32[64,128]{1,0:T(8,128)S(1)}, f32[64,128]{1,0:T(8,128)S(1)}, u32[]{:S(2)}, u32[]{:S(2)}) %collective-permute-start.64) | collective-permute-done | bytes 32800 | tf_op jit(solution)/shard_map/ppermute | solution.py:39
  134.9 2.7 %collective-permute-done.65 = f32[64,128]{1,0:T(8,128)S(1)} collective-permute-done((f32[64,128]{1,0:T(8,128)S(1)}, f32[64,128]{1,0:T(8,128)S(1)}, u32[]{:S(2)}, u32[]{:S(2)}) %collective-permute-start.65) | collective-permute-done | bytes 32800 | tf_op jit(solution)/shard_map/ppermute | solution.py:39
  143.9 2.6 %collective-permute-done.67 = f32[64,128]{1,0:T(8,128)S(1)} collective-permute-done((f32[64,128]{1,0:T(8,128)S(1)}, f32[64,128]{1,0:T(8,128)S(1)}, u32[]{:S(2)}, u32[]{:S(2)}) %collective-permute-start.67) | collective-permute-done | bytes 32800 | tf_op jit(solution)/shard_map/ppermute | solution.py:39
  147.7 3.6 %small.5 = (f32[64,512]{1,0:T(8,128)S(1)}, f32[64,512]{1,0:T(8,128)S(1)}, f32[64,512]{1,0:T(8,128)S(1)}, bf16[2,64,256]{2,1,0:T(8,128)(2,1)S(1)}) custom-call(s32[1]{0:T(128)} %bitcast.core, f32[64,128]{1,0:T(8,128)S(1)} %add.106.mine, f32[64,128]{1,0:T(8,128)S(1)} %collective-permute-done.68.other, f32[64,512]{1,0:T(8,128)S(1)} %get-tuple-element.40.vec, ...), custom_call_target="tpu_custom_call" | custom-call | tf_op jit(solution)/shard_map/small/pallas_call | solution.py:235
  151.3 3.4 %collective-permute-start.71 = (bf16[2,64,256]{2,1,0:T(8,128)(2,1)S(1)}, bf16[2,64,256]{2,1,0:T(8,128)(2,1)S(1)}, u32[]{:S(2)}, u32[]{:S(2)}) collective-permute-start(bf16[2,64,256]{2,1,0:T(8,128)(2,1)S(1)} %get-tuple-element.49), channel_id=1, source_target_pairs={{0,24},{1,25},{2,26},{3,27},{4,28},{5,29},{6,30},{7,31},{8,16},{9,... | collective-permute-start | bytes 196616 | tf_op jit(solution)/shard_map/ppermute | solution.py:28
  155.8 3.5 %collective-permute-done.69 = bf16[2,64,256]{2,1,0:T(8,128)(2,1)S(1)} collective-permute-done((bf16[2,64,256]{2,1,0:T(8,128)(2,1)S(1)}, bf16[2,64,256]{2,1,0:T(8,128)(2,1)S(1)}, u32[]{:S(2)}, u32[]{:S(2)}) %collective-permute-start.69) | collective-permute-done | bytes 65568 | tf_op jit(solution)/shard_map/ppermute | solution.py:28
  179.0 2.9 %collective-permute-done.87 = f32[64,128]{1,0:T(8,128)S(1)} collective-permute-done((f32[64,128]{1,0:T(8,128)S(1)}, f32[64,128]{1,0:T(8,128)S(1)}, u32[]{:S(2)}, u32[]{:S(2)}) %collective-permute-start.87) | collective-permute-done | bytes 32800 | tf_op jit(solution)/shard_map/ppermute | solution.py:39
  182.8 3.0 %collective-permute-done.88 = f32[64,128]{1,0:T(8,128)S(1)} collective-permute-done((f32[64,128]{1,0:T(8,128)S(1)}, f32[64,128]{1,0:T(8,128)S(1)}, u32[]{:S(2)}, u32[]{:S(2)}) %collective-permute-start.88) | collective-permute-done | bytes 32800 | tf_op jit(solution)/shard_map/ppermute | solution.py:39
  192.4 2.6 %collective-permute-done.90 = f32[64,128]{1,0:T(8,128)S(1)} collective-permute-done((f32[64,128]{1,0:T(8,128)S(1)}, f32[64,128]{1,0:T(8,128)S(1)}, u32[]{:S(2)}, u32[]{:S(2)}) %collective-permute-start.90) | collective-permute-done | bytes 32800 | tf_op jit(solution)/shard_map/ppermute | solution.py:39
  196.2 3.2 %small_last.1 = (f32[64,512]{1,0:T(8,128)}, f32[64,512]{1,0:T(8,128)}) custom-call(s32[1]{0:T(128)} %bitcast.core, f32[64,128]{1,0:T(8,128)S(1)} %add.111.mine, f32[64,128]{1,0:T(8,128)S(1)} %collective-permute-done.91.other, f32[64,512]{1,0:T(8,128)S(1)} %get-tuple-element.47.vec, f32[64,512]{1,0:T(8,128)S(1)} %get-tuple-element.48.res, ...), custom_call_target="tpu_custom_call" | custom-call | tf_op jit(solution)/shard_map/small_last/pallas_call | solution.py:235
  (219 shorter events, 122.7 us)
Async XLA Ops:
  1.6 12.6 %collective-permute-start.2 = (bf16[2,64,256]{2,1,0:T(8,128)(2,1)S(1)}, bf16[2,64,256]{2,1,0:T(8,128)(2,1)S(1)}, u32[]{:S(2)}, u32[]{:S(2)}) collective-permute-start(bf16[2,64,256]{2,1,0:T(8,128)(2,1)S(1)} %get-tuple-element.29), channel_id=1, source_target_pairs={{0,24},{1,25},{2,26},{3,27},{4,28},{5,29},{6,30},{7,31},{8,16},{9,... | collective-permute-start | bytes 196616 | tf_op jit(solution)/shard_map/ppermute | solution.py:28
  6.7 7.5 %collective-permute-start.1 = (bf16[2,64,256]{2,1,0:T(8,128)(2,1)S(1)}, bf16[2,64,256]{2,1,0:T(8,128)(2,1)S(1)}, u32[]{:S(2)}, u32[]{:S(2)}) collective-permute-start(bf16[2,64,256]{2,1,0:T(8,128)(2,1)S(1)} %get-tuple-element.29), channel_id=1, source_target_pairs={{0,16},{1,17},{2,18},{3,19},{4,20},{5,21},{6,22},{7,23},{8,24},{9,... | collective-permute-start | bytes 196616 | tf_op jit(solution)/shard_map/ppermute | solution.py:28
  14.2 6.4 %collective-permute-start.4 = (bf16[4,64,256]{2,1,0:T(8,128)(2,1)S(1)}, bf16[4,64,256]{2,1,0:T(8,128)(2,1)S(1)}, u32[]{:S(2)}, u32[]{:S(2)}) collective-permute-start(bf16[4,64,256]{2,1,0:T(8,128)(2,1)S(1)} %constant_dynamic-update-slice_fusion.2.refs_1_), channel_id=1, source_target_pairs={{0,2},{1,5},{2,0},{3,7},{4,6},{5,1},{6,4},{7,3},{8,10},{9,13},{10,... | collective-permute-start | bytes 393224 | tf_op jit(solution)/shard_map/ppermute | solution.py:39
  14.8 7.2 %collective-permute-start.10 = (bf16[4,64,256]{2,1,0:T(8,128)(2,1)S(1)}, bf16[4,64,256]{2,1,0:T(8,128)(2,1)S(1)}, u32[]{:S(2)}, u32[]{:S(2)}) collective-permute-start(bf16[4,64,256]{2,1,0:T(8,128)(2,1)S(1)} %constant_dynamic-update-slice_fusion.2.refs_1_), channel_id=1, source_target_pairs={{0,1},{1,0},{2,3},{3,2},{4,5},{5,4},{6,7},{7,6},{8,9},{9,8},{10,11... | collective-permute-start | bytes 393224 | tf_op jit(solution)/shard_map/ppermute | solution.py:28
  14.8 7.2 %collective-permute-start.6 = (bf16[4,64,256]{2,1,0:T(8,128)(2,1)S(1)}, bf16[4,64,256]{2,1,0:T(8,128)(2,1)S(1)}, u32[]{:S(2)}, u32[]{:S(2)}) collective-permute-start(bf16[4,64,256]{2,1,0:T(8,128)(2,1)S(1)} %constant_dynamic-update-slice_fusion.2.refs_1_), channel_id=1, source_target_pairs={{0,4},{1,3},{2,6},{3,1},{4,0},{5,7},{6,2},{7,5},{8,12},{9,11},{10,... | collective-permute-start | bytes 393224 | tf_op jit(solution)/shard_map/ppermute | solution.py:39
  16.6 5.8 %collective-permute-start.13 = (bf16[4,64,256]{2,1,0:T(8,128)(2,1)S(1)}, bf16[4,64,256]{2,1,0:T(8,128)(2,1)S(1)}, u32[]{:S(2)}, u32[]{:S(2)}) collective-permute-start(bf16[4,64,256]{2,1,0:T(8,128)(2,1)S(1)} %collective-permute-done.5.refs_4_), channel_id=1, source_target_pairs={{0,1},{1,0},{2,3},{3,2},{4,5},{5,4},{6,7},{7,6},{8,9},{9,8},{10,11... | collective-permute-start | bytes 393224 | tf_op jit(solution)/shard_map/ppermute | solution.py:28
  55.3 10.2 %collective-permute-start.25 = (bf16[2,64,256]{2,1,0:T(8,128)(2,1)S(1)}, bf16[2,64,256]{2,1,0:T(8,128)(2,1)S(1)}, u32[]{:S(2)}, u32[]{:S(2)}) collective-permute-start(bf16[2,64,256]{2,1,0:T(8,128)(2,1)S(1)} %get-tuple-element.35), channel_id=1, source_target_pairs={{0,24},{1,25},{2,26},{3,27},{4,28},{5,29},{6,30},{7,31},{8,16},{9,... | collective-permute-start | bytes 196616 | tf_op jit(solution)/shard_map/ppermute | solution.py:28
  58.2 7.2 %collective-permute-start.24 = (bf16[2,64,256]{2,1,0:T(8,128)(2,1)S(1)}, bf16[2,64,256]{2,1,0:T(8,128)(2,1)S(1)}, u32[]{:S(2)}, u32[]{:S(2)}) collective-permute-start(bf16[2,64,256]{2,1,0:T(8,128)(2,1)S(1)} %get-tuple-element.35), channel_id=1, source_target_pairs={{0,16},{1,17},{2,18},{3,19},{4,20},{5,21},{6,22},{7,23},{8,24},{9,... | collective-permute-start | bytes 196616 | tf_op jit(solution)/shard_map/ppermute | solution.py:28
  63.1 6.2 %collective-permute-start.28 = (bf16[4,64,256]{2,1,0:T(8,128)(2,1)S(1)}, bf16[4,64,256]{2,1,0:T(8,128)(2,1)S(1)}, u32[]{:S(2)}, u32[]{:S(2)}) collective-permute-start(bf16[4,64,256]{2,1,0:T(8,128)(2,1)S(1)} %constant_dynamic-update-slice_fusion.4.refs_0_), channel_id=1, source_target_pairs={{0,4},{1,3},{2,6},{3,1},{4,0},{5,7},{6,2},{7,5},{8,12},{9,11},{10,... | collective-permute-start | bytes 393224 | tf_op jit(solution)/shard_map/ppermute | solution.py:39
  65.4 6.1 %collective-permute-start.27 = (bf16[4,64,256]{2,1,0:T(8,128)(2,1)S(1)}, bf16[4,64,256]{2,1,0:T(8,128)(2,1)S(1)}, u32[]{:S(2)}, u32[]{:S(2)}) collective-permute-start(bf16[4,64,256]{2,1,0:T(8,128)(2,1)S(1)} %constant_dynamic-update-slice_fusion.6.refs_1_), channel_id=1, source_target_pairs={{0,2},{1,5},{2,0},{3,7},{4,6},{5,1},{6,4},{7,3},{8,10},{9,13},{10,... | collective-permute-start | bytes 393224 | tf_op jit(solution)/shard_map/ppermute | solution.py:39
  66.3 6.2 %collective-permute-start.33 = (bf16[4,64,256]{2,1,0:T(8,128)(2,1)S(1)}, bf16[4,64,256]{2,1,0:T(8,128)(2,1)S(1)}, u32[]{:S(2)}, u32[]{:S(2)}) collective-permute-start(bf16[4,64,256]{2,1,0:T(8,128)(2,1)S(1)} %constant_dynamic-update-slice_fusion.6.refs_1_), channel_id=1, source_target_pairs={{0,1},{1,0},{2,3},{3,2},{4,5},{5,4},{6,7},{7,6},{8,9},{9,8},{10,11... | collective-permute-start | bytes 393224 | tf_op jit(solution)/shard_map/ppermute | solution.py:28
  66.3 6.3 %collective-permute-start.29 = (bf16[4,64,256]{2,1,0:T(8,128)(2,1)S(1)}, bf16[4,64,256]{2,1,0:T(8,128)(2,1)S(1)}, u32[]{:S(2)}, u32[]{:S(2)}) collective-permute-start(bf16[4,64,256]{2,1,0:T(8,128)(2,1)S(1)} %constant_dynamic-update-slice_fusion.6.refs_1_), channel_id=1, source_target_pairs={{0,4},{1,3},{2,6},{3,1},{4,0},{5,7},{6,2},{7,5},{8,12},{9,11},{10,... | collective-permute-start | bytes 393224 | tf_op jit(solution)/shard_map/ppermute | solution.py:39
  103.5 9.9 %collective-permute-start.48 = (bf16[2,64,256]{2,1,0:T(8,128)(2,1)S(1)}, bf16[2,64,256]{2,1,0:T(8,128)(2,1)S(1)}, u32[]{:S(2)}, u32[]{:S(2)}) collective-permute-start(bf16[2,64,256]{2,1,0:T(8,128)(2,1)S(1)} %get-tuple-element.42), channel_id=1, source_target_pairs={{0,24},{1,25},{2,26},{3,27},{4,28},{5,29},{6,30},{7,31},{8,16},{9,... | collective-permute-start | bytes 196616 | tf_op jit(solution)/shard_map/ppermute | solution.py:28
  106.3 7.1 %collective-permute-start.47 = (bf16[2,64,256]{2,1,0:T(8,128)(2,1)S(1)}, bf16[2,64,256]{2,1,0:T(8,128)(2,1)S(1)}, u32[]{:S(2)}, u32[]{:S(2)}) collective-permute-start(bf16[2,64,256]{2,1,0:T(8,128)(2,1)S(1)} %get-tuple-element.42), channel_id=1, source_target_pairs={{0,16},{1,17},{2,18},{3,19},{4,20},{5,21},{6,22},{7,23},{8,24},{9,... | collective-permute-start | bytes 196616 | tf_op jit(solution)/shard_map/ppermute | solution.py:28
  111.4 6.3 %collective-permute-start.51 = (bf16[4,64,256]{2,1,0:T(8,128)(2,1)S(1)}, bf16[4,64,256]{2,1,0:T(8,128)(2,1)S(1)}, u32[]{:S(2)}, u32[]{:S(2)}) collective-permute-start(bf16[4,64,256]{2,1,0:T(8,128)(2,1)S(1)} %constant_dynamic-update-slice_fusion.8.refs_0_), channel_id=1, source_target_pairs={{0,4},{1,3},{2,6},{3,1},{4,0},{5,7},{6,2},{7,5},{8,12},{9,11},{10,... | collective-permute-start | bytes 393224 | tf_op jit(solution)/shard_map/ppermute | solution.py:39
  113.4 6.2 %collective-permute-start.50 = (bf16[4,64,256]{2,1,0:T(8,128)(2,1)S(1)}, bf16[4,64,256]{2,1,0:T(8,128)(2,1)S(1)}, u32[]{:S(2)}, u32[]{:S(2)}) collective-permute-start(bf16[4,64,256]{2,1,0:T(8,128)(2,1)S(1)} %constant_dynamic-update-slice_fusion.10.refs_1_), channel_id=1, source_target_pairs={{0,2},{1,5},{2,0},{3,7},{4,6},{5,1},{6,4},{7,3},{8,10},{9,13},{10,... | collective-permute-start | bytes 393224 | tf_op jit(solution)/shard_map/ppermute | solution.py:39
  114.5 6.4 %collective-permute-start.56 = (bf16[4,64,256]{2,1,0:T(8,128)(2,1)S(1)}, bf16[4,64,256]{2,1,0:T(8,128)(2,1)S(1)}, u32[]{:S(2)}, u32[]{:S(2)}) collective-permute-start(bf16[4,64,256]{2,1,0:T(8,128)(2,1)S(1)} %constant_dynamic-update-slice_fusion.10.refs_1_), channel_id=1, source_target_pairs={{0,1},{1,0},{2,3},{3,2},{4,5},{5,4},{6,7},{7,6},{8,9},{9,8},{10,11... | collective-permute-start | bytes 393224 | tf_op jit(solution)/shard_map/ppermute | solution.py:28
  114.5 6.5 %collective-permute-start.52 = (bf16[4,64,256]{2,1,0:T(8,128)(2,1)S(1)}, bf16[4,64,256]{2,1,0:T(8,128)(2,1)S(1)}, u32[]{:S(2)}, u32[]{:S(2)}) collective-permute-start(bf16[4,64,256]{2,1,0:T(8,128)(2,1)S(1)} %constant_dynamic-update-slice_fusion.10.refs_1_), channel_id=1, source_target_pairs={{0,4},{1,3},{2,6},{3,1},{4,0},{5,7},{6,2},{7,5},{8,12},{9,11},{10,... | collective-permute-start | bytes 393224 | tf_op jit(solution)/shard_map/ppermute | solution.py:39
  151.3 10.1 %collective-permute-start.71 = (bf16[2,64,256]{2,1,0:T(8,128)(2,1)S(1)}, bf16[2,64,256]{2,1,0:T(8,128)(2,1)S(1)}, u32[]{:S(2)}, u32[]{:S(2)}) collective-permute-start(bf16[2,64,256]{2,1,0:T(8,128)(2,1)S(1)} %get-tuple-element.49), channel_id=1, source_target_pairs={{0,24},{1,25},{2,26},{3,27},{4,28},{5,29},{6,30},{7,31},{8,16},{9,... | collective-permute-start | bytes 196616 | tf_op jit(solution)/shard_map/ppermute | solution.py:28
  154.7 6.7 %collective-permute-start.70 = (bf16[2,64,256]{2,1,0:T(8,128)(2,1)S(1)}, bf16[2,64,256]{2,1,0:T(8,128)(2,1)S(1)}, u32[]{:S(2)}, u32[]{:S(2)}) collective-permute-start(bf16[2,64,256]{2,1,0:T(8,128)(2,1)S(1)} %get-tuple-element.49), channel_id=1, source_target_pairs={{0,16},{1,17},{2,18},{3,19},{4,20},{5,21},{6,22},{7,23},{8,24},{9,... | collective-permute-start | bytes 196616 | tf_op jit(solution)/shard_map/ppermute | solution.py:28
  159.3 6.3 %collective-permute-start.74 = (bf16[4,64,256]{2,1,0:T(8,128)(2,1)S(1)}, bf16[4,64,256]{2,1,0:T(8,128)(2,1)S(1)}, u32[]{:S(2)}, u32[]{:S(2)}) collective-permute-start(bf16[4,64,256]{2,1,0:T(8,128)(2,1)S(1)} %constant_dynamic-update-slice_fusion.12.refs_0_), channel_id=1, source_target_pairs={{0,4},{1,3},{2,6},{3,1},{4,0},{5,7},{6,2},{7,5},{8,12},{9,11},{10,... | collective-permute-start | bytes 393224 | tf_op jit(solution)/shard_map/ppermute | solution.py:39
  161.4 6.4 %collective-permute-start.73 = (bf16[4,64,256]{2,1,0:T(8,128)(2,1)S(1)}, bf16[4,64,256]{2,1,0:T(8,128)(2,1)S(1)}, u32[]{:S(2)}, u32[]{:S(2)}) collective-permute-start(bf16[4,64,256]{2,1,0:T(8,128)(2,1)S(1)} %constant_dynamic-update-slice_fusion.14.refs_1_), channel_id=1, source_target_pairs={{0,2},{1,5},{2,0},{3,7},{4,6},{5,1},{6,4},{7,3},{8,10},{9,13},{10,... | collective-permute-start | bytes 393224 | tf_op jit(solution)/shard_map/ppermute | solution.py:39
  162.5 6.3 %collective-permute-start.79 = (bf16[4,64,256]{2,1,0:T(8,128)(2,1)S(1)}, bf16[4,64,256]{2,1,0:T(8,128)(2,1)S(1)}, u32[]{:S(2)}, u32[]{:S(2)}) collective-permute-start(bf16[4,64,256]{2,1,0:T(8,128)(2,1)S(1)} %constant_dynamic-update-slice_fusion.14.refs_1_), channel_id=1, source_target_pairs={{0,1},{1,0},{2,3},{3,2},{4,5},{5,4},{6,7},{7,6},{8,9},{9,8},{10,11... | collective-permute-start | bytes 393224 | tf_op jit(solution)/shard_map/ppermute | solution.py:28
  162.5 6.3 %collective-permute-start.75 = (bf16[4,64,256]{2,1,0:T(8,128)(2,1)S(1)}, bf16[4,64,256]{2,1,0:T(8,128)(2,1)S(1)}, u32[]{:S(2)}, u32[]{:S(2)}) collective-permute-start(bf16[4,64,256]{2,1,0:T(8,128)(2,1)S(1)} %constant_dynamic-update-slice_fusion.14.refs_1_), channel_id=1, source_target_pairs={{0,4},{1,3},{2,6},{3,1},{4,0},{5,7},{6,2},{7,5},{8,12},{9,11},{10,... | collective-permute-start | bytes 393224 | tf_op jit(solution)/shard_map/ppermute | solution.py:39
  (73 other events, 360.5 us)

commit v6 on v5

--- a/solution.py
+++ b/solution.py
@@ -258,8 +258,11 @@
         pieces = gather_of(rounded, groups, crossed, core_bit, count)
         image, keep, give = apply_matrix(slots, pieces, tiles, vec, res, diag)
         mine = keep + xor_permute(give, core_bit, count)
-        for even, odd in stages:
-            mine = mine + crossed_permute(mine, even, odd, core_bit, count)
+        for masks in stages:
+            terms = spread(mine, masks, count)
+            while len(terms) > 1:
+                terms = [left + right for left, right in zip(terms[0::2], terms[1::2])]
+            mine = terms[0]
         other = xor_permute(mine, core_bit, count)
         outs = solve_step(last, rows, core, mine, other, vec, res, sol, image)
         if last:
@@ -280,10 +283,7 @@
     cols = mesh.shape["col"]
     bits = [1 << i for i in range(1, count.bit_length() - 1)]
     crossed, rest = bits[:2], bits[2:]
-    stages = []
-    for i in range(0, len(bits), 2):
-        pair = bits[i : i + 2]
-        stages += [(pair[0], pair[-1]), (pair[-1], pair[0])][: len(pair)]
+    stages = [bits[i : i + 2] for i in range(0, len(bits), 2)]
     major = [b for b in rest if b >= cols]
     minor = [b for b in rest if b < cols]
     groups = [part[i : i + 2] for part in (major, minor) for i in range(0, len(part), 2)]

time: 200 us -> 188 us (0.940)
  waiting for transfers between devices: 95.1 us -> 76.9 us
  starting transfers between devices: 74.3 us -> 80.5 us
    ppermute x40 -> x24, waiting for transfers between devices: 66.9 us -> 25.8 us  [crossed_permute(): lax.ppermute(val, AXES, [(i, i ^ (odd if i & core else even)) for i in ra...]
    ppermute x52 -> x76, starting transfers between devices: 22.9 us -> 55.3 us  [xor_permute(): return lax.ppermute(val, AXES, [(i, i ^ mask) for i in range(count)])]
    ppermute x40 -> x24, starting transfers between devices: 51.4 us -> 25.2 us  [crossed_permute(): lax.ppermute(val, AXES, [(i, i ^ (odd if i & core else even)) for i in ra...]
    ppermute x52 -> x76, waiting for transfers between devices: 28.2 us -> 51.2 us  [xor_permute(): return lax.ppermute(val, AXES, [(i, i ^ mask) for i in range(count)])]
  transfers between devices with their start and end apart: 92 -> 100, of which waited for: 49 -> 53; matrix products, arithmetic and copies ran while one was open for 0% -> 1% of each run, Pallas kernels for 0% -> 0%
where the time goes in v6:
time: 188 us; the launch traced here: 187 us
  starting transfers between devices  80.5 us (43%)
  waiting for transfers between devices  76.9 us (41%)
  Pallas kernels  24.1 us (13%)
  local copies, waits for them, and re-layouts  4.63 us (2%)
    ppermute x76, starting transfers between devices, xor_permute(): return lax.ppermute(val, AXES, [(i, i ^ mask) for i in range(count)])  55.3 us
    ppermute x76, waiting for transfers between devices, xor_permute(): return lax.ppermute(val, AXES, [(i, i ^ mask) for i in range(count)])  51.2 us
    ppermute x24, waiting for transfers between devices, crossed_permute(): lax.ppermute(val, AXES, [(i, i ^ (odd if i & core else even)) for i in ra...  25.8 us
    ppermute x24, starting transfers between devices, crossed_permute(): lax.ppermute(val, AXES, [(i, i ^ (odd if i & core else even)) for i in ra...  25.2 us
    pallas_call x4, Pallas kernels, solve_step(): pl.pallas_call(functools.partial(solve_kernel, last), out_shape=tuple(out...  14.1 us
    pallas_call x4, Pallas kernels, apply_matrix(): pl.pallas_call(functools.partial(matrix_kernel, rows, nbr, blk, len(piece...  10 us
    unnamed x18, local copies, waits for them, and re-layouts  3.82 us
  transfers between devices with their start and end apart: 100, of which 53 were waited for; matrix products, arithmetic and copies ran while one was open for 1% of the time, Pallas kernels for 0%

profile of v6, /device:TPU:0, one launch (start us, length us, event | category | flops | bytes accessed | tf_op | source)
XLA Modules:
  0.0 187.5 jit_solution(189740138152859002)
XLA Ops:
  1.6 5.1 %collective-permute-start.2 = (bf16[2,64,256]{2,1,0:T(8,128)(2,1)S(1)}, bf16[2,64,256]{2,1,0:T(8,128)(2,1)S(1)}, u32[]{:S(2)}, u32[]{:S(2)}) collective-permute-start(bf16[2,64,256]{2,1,0:T(8,128)(2,1)S(1)} %get-tuple-element.29), channel_id=1, source_target_pairs={{0,24},{1,25},{2,26},{3,27},{4,28},{5,29},{6,30},{7,31},{8,16},{9,... | collective-permute-start | bytes 196616 | tf_op jit(solution)/shard_map/ppermute | solution.py:28
  7.3 3.6 %collective-permute-done = bf16[2,64,256]{2,1,0:T(8,128)(2,1)S(1)} collective-permute-done((bf16[2,64,256]{2,1,0:T(8,128)(2,1)S(1)}, bf16[2,64,256]{2,1,0:T(8,128)(2,1)S(1)}, u32[]{:S(2)}, u32[]{:S(2)}) %collective-permute-start) | collective-permute-done | bytes 65568 | tf_op jit(solution)/shard_map/ppermute | solution.py:28
  23.0 2.5 %collective-permute-done.8.refs_7_ = bf16[4,64,256]{2,1,0:T(8,128)(2,1)S(1)} collective-permute-done((bf16[4,64,256]{2,1,0:T(8,128)(2,1)S(1)}, bf16[4,64,256]{2,1,0:T(8,128)(2,1)S(1)}, u32[]{:S(2)}, u32[]{:S(2)}) %collective-permute-start.8) | collective-permute-done | bytes 131104 | tf_op jit(solution)/shard_map/ppermute | solution.py:39
  26.9 2.2 %copy-done = bf16[2,16,256,256]{3,2,1,0:T(8,128)(2,1)S(1)} copy-done((bf16[2,16,256,256]{3,2,1,0:T(8,128)(2,1)S(1)}, bf16[2,16,256,256]{3,2,1,0:T(8,128)(2,1)}, u32[]{:S(2)}) %copy-start) | copy-done | bytes 4194328
  29.7 2.5 %matrix.4 = (f32[64,512]{1,0:T(8,128)S(1)}, f32[64,128]{1,0:T(8,128)S(1)}, f32[64,128]{1,0:T(8,128)S(1)}) custom-call(s32[33]{0:T(128)S(1)} %pad_add_fusion.slots, bf16[2,16,256,256]{3,2,1,0:T(8,128)(2,1)S(1)} %copy-done, f32[64,512]{1,0:T(8,128)S(1)} %get-tuple-element.28.vec.res, f32[64,512]{1,0:T(8,128)S(1)} %get-tuple-element.28.vec.res, ...), custom_call_target="tpu_custom_call" | custom-call | tf_op jit(solution)/shard_map/matrix/pallas_call | solution.py:134
  39.9 3.2 %collective-permute-start.23 = (f32[64,128]{1,0:T(8,128)S(1)}, f32[64,128]{1,0:T(8,128)S(1)}, u32[]{:S(2)}, u32[]{:S(2)}) collective-permute-start(f32[64,128]{1,0:T(8,128)S(1)} %add_add_fusion.7), channel_id=1, source_target_pairs={{0,24},{1,25},{2,26},{3,27},{4,28},{5,29},{6,30},{7,31},{8,16},{9,... | collective-permute-start | bytes 98312 | tf_op jit(solution)/shard_map/ppermute | solution.py:28
  45.8 2.2 %collective-permute-done.22 = f32[64,128]{1,0:T(8,128)S(1)} collective-permute-done((f32[64,128]{1,0:T(8,128)S(1)}, f32[64,128]{1,0:T(8,128)S(1)}, u32[]{:S(2)}, u32[]{:S(2)}) %collective-permute-start.22) | collective-permute-done | bytes 32800 | tf_op jit(solution)/shard_map/ppermute | solution.py:28
  49.3 3.6 %small.3 = (f32[64,512]{1,0:T(8,128)S(1)}, f32[64,512]{1,0:T(8,128)S(1)}, f32[64,512]{1,0:T(8,128)S(1)}, bf16[2,64,256]{2,1,0:T(8,128)(2,1)S(1)}) custom-call(s32[1]{0:T(128)} %bitcast.core, f32[64,128]{1,0:T(8,128)S(1)} %add_add_fusion.6.mine, f32[64,128]{1,0:T(8,128)S(1)} %collective-permute-done.24.other, f32[64,512]{1,0:T(8,128)S(1)} %get-tuple-element.28.vec.res, ...), custom_call_target="tpu_custom_call" | custom-call | tf_op jit(solution)/shard_map/small/pallas_call | solution.py:235
  55.1 2.4 %collective-permute-start.25 = (bf16[2,64,256]{2,1,0:T(8,128)(2,1)S(1)}, bf16[2,64,256]{2,1,0:T(8,128)(2,1)S(1)}, u32[]{:S(2)}, u32[]{:S(2)}) collective-permute-start(bf16[2,64,256]{2,1,0:T(8,128)(2,1)S(1)} %get-tuple-element.35), channel_id=1, source_target_pairs={{0,8},{1,9},{2,10},{3,11},{4,12},{5,13},{6,14},{7,15},{8,0},{9,1},... | collective-permute-start | bytes 196616 | tf_op jit(solution)/shard_map/ppermute | solution.py:28
  57.5 3.7 %collective-permute-done.25 = bf16[2,64,256]{2,1,0:T(8,128)(2,1)S(1)} collective-permute-done((bf16[2,64,256]{2,1,0:T(8,128)(2,1)S(1)}, bf16[2,64,256]{2,1,0:T(8,128)(2,1)S(1)}, u32[]{:S(2)}, u32[]{:S(2)}) %collective-permute-start.25) | collective-permute-done | bytes 65568 | tf_op jit(solution)/shard_map/ppermute | solution.py:28
  72.4 2.5 %collective-permute-done.33.refs_7_ = bf16[4,64,256]{2,1,0:T(8,128)(2,1)S(1)} collective-permute-done((bf16[4,64,256]{2,1,0:T(8,128)(2,1)S(1)}, bf16[4,64,256]{2,1,0:T(8,128)(2,1)S(1)}, u32[]{:S(2)}, u32[]{:S(2)}) %collective-permute-start.33) | collective-permute-done | bytes 131104 | tf_op jit(solution)/shard_map/ppermute | solution.py:39
  76.3 2.5 %matrix.5 = (f32[64,512]{1,0:T(8,128)S(1)}, f32[64,128]{1,0:T(8,128)S(1)}, f32[64,128]{1,0:T(8,128)S(1)}) custom-call(s32[33]{0:T(128)S(1)} %pad_add_fusion.slots, bf16[2,16,256,256]{3,2,1,0:T(8,128)(2,1)S(1)} %copy-done.1, f32[64,512]{1,0:T(8,128)S(1)} %get-tuple-element.33.vec, f32[64,512]{1,0:T(8,128)S(1)} %get-tuple-element.34.res, ...), custom_call_target="tpu_custom_call" | custom-call | tf_op jit(solution)/shard_map/matrix/pallas_call | solution.py:134
  88.5 2.4 %collective-permute-start.46 = (f32[64,128]{1,0:T(8,128)S(1)}, f32[64,128]{1,0:T(8,128)S(1)}, u32[]{:S(2)}, u32[]{:S(2)}) collective-permute-start(f32[64,128]{1,0:T(8,128)S(1)} %add_add_fusion.5), channel_id=1, source_target_pairs={{0,8},{1,9},{2,10},{3,11},{4,12},{5,13},{6,14},{7,15},{8,0},{9,1},... | collective-permute-start | bytes 98312 | tf_op jit(solution)/shard_map/ppermute | solution.py:28
  94.4 3.6 %small.4 = (f32[64,512]{1,0:T(8,128)S(1)}, f32[64,512]{1,0:T(8,128)S(1)}, f32[64,512]{1,0:T(8,128)S(1)}, bf16[2,64,256]{2,1,0:T(8,128)(2,1)S(1)}) custom-call(s32[1]{0:T(128)} %bitcast.core, f32[64,128]{1,0:T(8,128)S(1)} %add_add_fusion.4.mine, f32[64,128]{1,0:T(8,128)S(1)} %collective-permute-done.49.other, f32[64,512]{1,0:T(8,128)S(1)} %get-tuple-element.33.vec, ...), custom_call_target="tpu_custom_call" | custom-call | tf_op jit(solution)/shard_map/small/pallas_call | solution.py:235
  98.1 2.1 %collective-permute-start.52 = (bf16[2,64,256]{2,1,0:T(8,128)(2,1)S(1)}, bf16[2,64,256]{2,1,0:T(8,128)(2,1)S(1)}, u32[]{:S(2)}, u32[]{:S(2)}) collective-permute-start(bf16[2,64,256]{2,1,0:T(8,128)(2,1)S(1)} %get-tuple-element.42), channel_id=1, source_target_pairs={{0,24},{1,25},{2,26},{3,27},{4,28},{5,29},{6,30},{7,31},{8,16},{9,... | collective-permute-start | bytes 196616 | tf_op jit(solution)/shard_map/ppermute | solution.py:28
  102.5 3.3 %collective-permute-done.50 = bf16[2,64,256]{2,1,0:T(8,128)(2,1)S(1)} collective-permute-done((bf16[2,64,256]{2,1,0:T(8,128)(2,1)S(1)}, bf16[2,64,256]{2,1,0:T(8,128)(2,1)S(1)}, u32[]{:S(2)}, u32[]{:S(2)}) %collective-permute-start.50) | collective-permute-done | bytes 65568 | tf_op jit(solution)/shard_map/ppermute | solution.py:28
  117.1 2.2 %collective-permute-done.58.refs_7_ = bf16[4,64,256]{2,1,0:T(8,128)(2,1)S(1)} collective-permute-done((bf16[4,64,256]{2,1,0:T(8,128)(2,1)S(1)}, bf16[4,64,256]{2,1,0:T(8,128)(2,1)S(1)}, u32[]{:S(2)}, u32[]{:S(2)}) %collective-permute-start.58) | collective-permute-done | bytes 131104 | tf_op jit(solution)/shard_map/ppermute | solution.py:39
  120.7 2.5 %matrix.6 = (f32[64,512]{1,0:T(8,128)S(1)}, f32[64,128]{1,0:T(8,128)S(1)}, f32[64,128]{1,0:T(8,128)S(1)}) custom-call(s32[33]{0:T(128)S(1)} %pad_add_fusion.slots, bf16[2,16,256,256]{3,2,1,0:T(8,128)(2,1)S(1)} %copy-done.1, f32[64,512]{1,0:T(8,128)S(1)} %get-tuple-element.40.vec, f32[64,512]{1,0:T(8,128)S(1)} %get-tuple-element.41.res, ...), custom_call_target="tpu_custom_call" | custom-call | tf_op jit(solution)/shard_map/matrix/pallas_call | solution.py:134
  130.8 2.5 %collective-permute-start.73 = (f32[64,128]{1,0:T(8,128)S(1)}, f32[64,128]{1,0:T(8,128)S(1)}, u32[]{:S(2)}, u32[]{:S(2)}) collective-permute-start(f32[64,128]{1,0:T(8,128)S(1)} %add_add_fusion.3), channel_id=1, source_target_pairs={{0,24},{1,25},{2,26},{3,27},{4,28},{5,29},{6,30},{7,31},{8,16},{9,... | collective-permute-start | bytes 98312 | tf_op jit(solution)/shard_map/ppermute | solution.py:28
  139.4 3.6 %small.5 = (f32[64,512]{1,0:T(8,128)S(1)}, f32[64,512]{1,0:T(8,128)S(1)}, f32[64,512]{1,0:T(8,128)S(1)}, bf16[2,64,256]{2,1,0:T(8,128)(2,1)S(1)}) custom-call(s32[1]{0:T(128)} %bitcast.core, f32[64,128]{1,0:T(8,128)S(1)} %add_add_fusion.2.mine, f32[64,128]{1,0:T(8,128)S(1)} %collective-permute-done.74.other, f32[64,512]{1,0:T(8,128)S(1)} %get-tuple-element.40.vec, ...), custom_call_target="tpu_custom_call" | custom-call | tf_op jit(solution)/shard_map/small/pallas_call | solution.py:235
  147.5 3.6 %collective-permute-done.75 = bf16[2,64,256]{2,1,0:T(8,128)(2,1)S(1)} collective-permute-done((bf16[2,64,256]{2,1,0:T(8,128)(2,1)S(1)}, bf16[2,64,256]{2,1,0:T(8,128)(2,1)S(1)}, u32[]{:S(2)}, u32[]{:S(2)}) %collective-permute-start.75) | collective-permute-done | bytes 65568 | tf_op jit(solution)/shard_map/ppermute | solution.py:28
  162.3 2.4 %collective-permute-done.83.refs_7_ = bf16[4,64,256]{2,1,0:T(8,128)(2,1)S(1)} collective-permute-done((bf16[4,64,256]{2,1,0:T(8,128)(2,1)S(1)}, bf16[4,64,256]{2,1,0:T(8,128)(2,1)S(1)}, u32[]{:S(2)}, u32[]{:S(2)}) %collective-permute-start.83) | collective-permute-done | bytes 131104 | tf_op jit(solution)/shard_map/ppermute | solution.py:39
  166.1 2.5 %matrix.7 = (f32[64,512]{1,0:T(8,128)S(1)}, f32[64,128]{1,0:T(8,128)S(1)}, f32[64,128]{1,0:T(8,128)S(1)}) custom-call(s32[33]{0:T(128)S(1)} %pad_add_fusion.slots, bf16[2,16,256,256]{3,2,1,0:T(8,128)(2,1)S(1)} %copy-done.1, f32[64,512]{1,0:T(8,128)S(1)} %get-tuple-element.47.vec, f32[64,512]{1,0:T(8,128)S(1)} %get-tuple-element.48.res, ...), custom_call_target="tpu_custom_call" | custom-call | tf_op jit(solution)/shard_map/matrix/pallas_call | solution.py:134
  184.3 3.2 %small_last.1 = (f32[64,512]{1,0:T(8,128)}, f32[64,512]{1,0:T(8,128)}) custom-call(s32[1]{0:T(128)} %bitcast.core, f32[64,128]{1,0:T(8,128)S(1)} %add_add_fusion.mine, f32[64,128]{1,0:T(8,128)S(1)} %collective-permute-done.99.other, f32[64,512]{1,0:T(8,128)S(1)} %get-tuple-element.47.vec, f32[64,512]{1,0:T(8,128)S(1)} %get-tuple-element.48.res, ...), custom_call_target="tpu_custom_call" | custom-call | tf_op jit(solution)/shard_map/small_last/pallas_call | solution.py:235
  (227 shorter events, 116.3 us)
Async XLA Ops:
  1.6 12.6 %collective-permute-start.2 = (bf16[2,64,256]{2,1,0:T(8,128)(2,1)S(1)}, bf16[2,64,256]{2,1,0:T(8,128)(2,1)S(1)}, u32[]{:S(2)}, u32[]{:S(2)}) collective-permute-start(bf16[2,64,256]{2,1,0:T(8,128)(2,1)S(1)} %get-tuple-element.29), channel_id=1, source_target_pairs={{0,24},{1,25},{2,26},{3,27},{4,28},{5,29},{6,30},{7,31},{8,16},{9,... | collective-permute-start | bytes 196616 | tf_op jit(solution)/shard_map/ppermute | solution.py:28
  6.7 7.5 %collective-permute-start.1 = (bf16[2,64,256]{2,1,0:T(8,128)(2,1)S(1)}, bf16[2,64,256]{2,1,0:T(8,128)(2,1)S(1)}, u32[]{:S(2)}, u32[]{:S(2)}) collective-permute-start(bf16[2,64,256]{2,1,0:T(8,128)(2,1)S(1)} %get-tuple-element.29), channel_id=1, source_target_pairs={{0,16},{1,17},{2,18},{3,19},{4,20},{5,21},{6,22},{7,23},{8,24},{9,... | collective-permute-start | bytes 196616 | tf_op jit(solution)/shard_map/ppermute | solution.py:28
  14.2 6.4 %collective-permute-start.4 = (bf16[4,64,256]{2,1,0:T(8,128)(2,1)S(1)}, bf16[4,64,256]{2,1,0:T(8,128)(2,1)S(1)}, u32[]{:S(2)}, u32[]{:S(2)}) collective-permute-start(bf16[4,64,256]{2,1,0:T(8,128)(2,1)S(1)} %constant_dynamic-update-slice_fusion.2.refs_1_), channel_id=1, source_target_pairs={{0,2},{1,5},{2,0},{3,7},{4,6},{5,1},{6,4},{7,3},{8,10},{9,13},{10,... | collective-permute-start | bytes 393224 | tf_op jit(solution)/shard_map/ppermute | solution.py:39
  14.8 7.2 %collective-permute-start.10 = (bf16[4,64,256]{2,1,0:T(8,128)(2,1)S(1)}, bf16[4,64,256]{2,1,0:T(8,128)(2,1)S(1)}, u32[]{:S(2)}, u32[]{:S(2)}) collective-permute-start(bf16[4,64,256]{2,1,0:T(8,128)(2,1)S(1)} %constant_dynamic-update-slice_fusion.2.refs_1_), channel_id=1, source_target_pairs={{0,1},{1,0},{2,3},{3,2},{4,5},{5,4},{6,7},{7,6},{8,9},{9,8},{10,11... | collective-permute-start | bytes 393224 | tf_op jit(solution)/shard_map/ppermute | solution.py:28
  14.8 7.2 %collective-permute-start.6 = (bf16[4,64,256]{2,1,0:T(8,128)(2,1)S(1)}, bf16[4,64,256]{2,1,0:T(8,128)(2,1)S(1)}, u32[]{:S(2)}, u32[]{:S(2)}) collective-permute-start(bf16[4,64,256]{2,1,0:T(8,128)(2,1)S(1)} %constant_dynamic-update-slice_fusion.2.refs_1_), channel_id=1, source_target_pairs={{0,4},{1,3},{2,6},{3,1},{4,0},{5,7},{6,2},{7,5},{8,12},{9,11},{10,... | collective-permute-start | bytes 393224 | tf_op jit(solution)/shard_map/ppermute | solution.py:39
  53.0 10.0 %collective-permute-start.27 = (bf16[2,64,256]{2,1,0:T(8,128)(2,1)S(1)}, bf16[2,64,256]{2,1,0:T(8,128)(2,1)S(1)}, u32[]{:S(2)}, u32[]{:S(2)}) collective-permute-start(bf16[2,64,256]{2,1,0:T(8,128)(2,1)S(1)} %get-tuple-element.35), channel_id=1, source_target_pairs={{0,24},{1,25},{2,26},{3,27},{4,28},{5,29},{6,30},{7,31},{8,16},{9,... | collective-permute-start | bytes 196616 | tf_op jit(solution)/shard_map/ppermute | solution.py:28
  54.7 8.3 %collective-permute-start.26 = (bf16[2,64,256]{2,1,0:T(8,128)(2,1)S(1)}, bf16[2,64,256]{2,1,0:T(8,128)(2,1)S(1)}, u32[]{:S(2)}, u32[]{:S(2)}) collective-permute-start(bf16[2,64,256]{2,1,0:T(8,128)(2,1)S(1)} %get-tuple-element.35), channel_id=1, source_target_pairs={{0,16},{1,17},{2,18},{3,19},{4,20},{5,21},{6,22},{7,23},{8,24},{9,... | collective-permute-start | bytes 196616 | tf_op jit(solution)/shard_map/ppermute | solution.py:28
  55.1 6.1 %collective-permute-start.25 = (bf16[2,64,256]{2,1,0:T(8,128)(2,1)S(1)}, bf16[2,64,256]{2,1,0:T(8,128)(2,1)S(1)}, u32[]{:S(2)}, u32[]{:S(2)}) collective-permute-start(bf16[2,64,256]{2,1,0:T(8,128)(2,1)S(1)} %get-tuple-element.35), channel_id=1, source_target_pairs={{0,8},{1,9},{2,10},{3,11},{4,12},{5,13},{6,14},{7,15},{8,0},{9,1},... | collective-permute-start | bytes 196616 | tf_op jit(solution)/shard_map/ppermute | solution.py:28
  61.2 6.2 %collective-permute-start.30 = (bf16[4,64,256]{2,1,0:T(8,128)(2,1)S(1)}, bf16[4,64,256]{2,1,0:T(8,128)(2,1)S(1)}, u32[]{:S(2)}, u32[]{:S(2)}) collective-permute-start(bf16[4,64,256]{2,1,0:T(8,128)(2,1)S(1)} %constant_dynamic-update-slice_fusion.4.refs_0_), channel_id=1, source_target_pairs={{0,4},{1,3},{2,6},{3,1},{4,0},{5,7},{6,2},{7,5},{8,12},{9,11},{10,... | collective-permute-start | bytes 393224 | tf_op jit(solution)/shard_map/ppermute | solution.py:39
  63.0 6.9 %collective-permute-start.29 = (bf16[4,64,256]{2,1,0:T(8,128)(2,1)S(1)}, bf16[4,64,256]{2,1,0:T(8,128)(2,1)S(1)}, u32[]{:S(2)}, u32[]{:S(2)}) collective-permute-start(bf16[4,64,256]{2,1,0:T(8,128)(2,1)S(1)} %constant_dynamic-update-slice_fusion.6.refs_1_), channel_id=1, source_target_pairs={{0,2},{1,5},{2,0},{3,7},{4,6},{5,1},{6,4},{7,3},{8,10},{9,13},{10,... | collective-permute-start | bytes 393224 | tf_op jit(solution)/shard_map/ppermute | solution.py:39
  64.6 6.2 %collective-permute-start.35 = (bf16[4,64,256]{2,1,0:T(8,128)(2,1)S(1)}, bf16[4,64,256]{2,1,0:T(8,128)(2,1)S(1)}, u32[]{:S(2)}, u32[]{:S(2)}) collective-permute-start(bf16[4,64,256]{2,1,0:T(8,128)(2,1)S(1)} %constant_dynamic-update-slice_fusion.6.refs_1_), channel_id=1, source_target_pairs={{0,1},{1,0},{2,3},{3,2},{4,5},{5,4},{6,7},{7,6},{8,9},{9,8},{10,11... | collective-permute-start | bytes 393224 | tf_op jit(solution)/shard_map/ppermute | solution.py:28
  64.6 6.6 %collective-permute-start.31 = (bf16[4,64,256]{2,1,0:T(8,128)(2,1)S(1)}, bf16[4,64,256]{2,1,0:T(8,128)(2,1)S(1)}, u32[]{:S(2)}, u32[]{:S(2)}) collective-permute-start(bf16[4,64,256]{2,1,0:T(8,128)(2,1)S(1)} %constant_dynamic-update-slice_fusion.6.refs_1_), channel_id=1, source_target_pairs={{0,4},{1,3},{2,6},{3,1},{4,0},{5,7},{6,2},{7,5},{8,12},{9,11},{10,... | collective-permute-start | bytes 393224 | tf_op jit(solution)/shard_map/ppermute | solution.py:39
  98.1 9.8 %collective-permute-start.52 = (bf16[2,64,256]{2,1,0:T(8,128)(2,1)S(1)}, bf16[2,64,256]{2,1,0:T(8,128)(2,1)S(1)}, u32[]{:S(2)}, u32[]{:S(2)}) collective-permute-start(bf16[2,64,256]{2,1,0:T(8,128)(2,1)S(1)} %get-tuple-element.42), channel_id=1, source_target_pairs={{0,24},{1,25},{2,26},{3,27},{4,28},{5,29},{6,30},{7,31},{8,16},{9,... | collective-permute-start | bytes 196616 | tf_op jit(solution)/shard_map/ppermute | solution.py:28
  100.2 7.7 %collective-permute-start.51 = (bf16[2,64,256]{2,1,0:T(8,128)(2,1)S(1)}, bf16[2,64,256]{2,1,0:T(8,128)(2,1)S(1)}, u32[]{:S(2)}, u32[]{:S(2)}) collective-permute-start(bf16[2,64,256]{2,1,0:T(8,128)(2,1)S(1)} %get-tuple-element.42), channel_id=1, source_target_pairs={{0,16},{1,17},{2,18},{3,19},{4,20},{5,21},{6,22},{7,23},{8,24},{9,... | collective-permute-start | bytes 196616 | tf_op jit(solution)/shard_map/ppermute | solution.py:28
  105.9 6.3 %collective-permute-start.55 = (bf16[4,64,256]{2,1,0:T(8,128)(2,1)S(1)}, bf16[4,64,256]{2,1,0:T(8,128)(2,1)S(1)}, u32[]{:S(2)}, u32[]{:S(2)}) collective-permute-start(bf16[4,64,256]{2,1,0:T(8,128)(2,1)S(1)} %constant_dynamic-update-slice_fusion.8.refs_0_), channel_id=1, source_target_pairs={{0,4},{1,3},{2,6},{3,1},{4,0},{5,7},{6,2},{7,5},{8,12},{9,11},{10,... | collective-permute-start | bytes 393224 | tf_op jit(solution)/shard_map/ppermute | solution.py:39
  107.9 6.4 %collective-permute-start.54 = (bf16[4,64,256]{2,1,0:T(8,128)(2,1)S(1)}, bf16[4,64,256]{2,1,0:T(8,128)(2,1)S(1)}, u32[]{:S(2)}, u32[]{:S(2)}) collective-permute-start(bf16[4,64,256]{2,1,0:T(8,128)(2,1)S(1)} %constant_dynamic-update-slice_fusion.10.refs_1_), channel_id=1, source_target_pairs={{0,2},{1,5},{2,0},{3,7},{4,6},{5,1},{6,4},{7,3},{8,10},{9,13},{10,... | collective-permute-start | bytes 393224 | tf_op jit(solution)/shard_map/ppermute | solution.py:39
  108.9 6.6 %collective-permute-start.60 = (bf16[4,64,256]{2,1,0:T(8,128)(2,1)S(1)}, bf16[4,64,256]{2,1,0:T(8,128)(2,1)S(1)}, u32[]{:S(2)}, u32[]{:S(2)}) collective-permute-start(bf16[4,64,256]{2,1,0:T(8,128)(2,1)S(1)} %constant_dynamic-update-slice_fusion.10.refs_1_), channel_id=1, source_target_pairs={{0,1},{1,0},{2,3},{3,2},{4,5},{5,4},{6,7},{7,6},{8,9},{9,8},{10,11... | collective-permute-start | bytes 393224 | tf_op jit(solution)/shard_map/ppermute | solution.py:28
  108.9 6.8 %collective-permute-start.56 = (bf16[4,64,256]{2,1,0:T(8,128)(2,1)S(1)}, bf16[4,64,256]{2,1,0:T(8,128)(2,1)S(1)}, u32[]{:S(2)}, u32[]{:S(2)}) collective-permute-start(bf16[4,64,256]{2,1,0:T(8,128)(2,1)S(1)} %constant_dynamic-update-slice_fusion.10.refs_1_), channel_id=1, source_target_pairs={{0,4},{1,3},{2,6},{3,1},{4,0},{5,7},{6,2},{7,5},{8,12},{9,11},{10,... | collective-permute-start | bytes 393224 | tf_op jit(solution)/shard_map/ppermute | solution.py:39
  143.1 10.3 %collective-permute-start.77 = (bf16[2,64,256]{2,1,0:T(8,128)(2,1)S(1)}, bf16[2,64,256]{2,1,0:T(8,128)(2,1)S(1)}, u32[]{:S(2)}, u32[]{:S(2)}) collective-permute-start(bf16[2,64,256]{2,1,0:T(8,128)(2,1)S(1)} %get-tuple-element.49), channel_id=1, source_target_pairs={{0,24},{1,25},{2,26},{3,27},{4,28},{5,29},{6,30},{7,31},{8,16},{9,... | collective-permute-start | bytes 196616 | tf_op jit(solution)/shard_map/ppermute | solution.py:28
  145.0 8.4 %collective-permute-start.76 = (bf16[2,64,256]{2,1,0:T(8,128)(2,1)S(1)}, bf16[2,64,256]{2,1,0:T(8,128)(2,1)S(1)}, u32[]{:S(2)}, u32[]{:S(2)}) collective-permute-start(bf16[2,64,256]{2,1,0:T(8,128)(2,1)S(1)} %get-tuple-element.49), channel_id=1, source_target_pairs={{0,16},{1,17},{2,18},{3,19},{4,20},{5,21},{6,22},{7,23},{8,24},{9,... | collective-permute-start | bytes 196616 | tf_op jit(solution)/shard_map/ppermute | solution.py:28
  151.2 6.2 %collective-permute-start.80 = (bf16[4,64,256]{2,1,0:T(8,128)(2,1)S(1)}, bf16[4,64,256]{2,1,0:T(8,128)(2,1)S(1)}, u32[]{:S(2)}, u32[]{:S(2)}) collective-permute-start(bf16[4,64,256]{2,1,0:T(8,128)(2,1)S(1)} %constant_dynamic-update-slice_fusion.12.refs_0_), channel_id=1, source_target_pairs={{0,4},{1,3},{2,6},{3,1},{4,0},{5,7},{6,2},{7,5},{8,12},{9,11},{10,... | collective-permute-start | bytes 393224 | tf_op jit(solution)/shard_map/ppermute | solution.py:39
  153.4 6.4 %collective-permute-start.79 = (bf16[4,64,256]{2,1,0:T(8,128)(2,1)S(1)}, bf16[4,64,256]{2,1,0:T(8,128)(2,1)S(1)}, u32[]{:S(2)}, u32[]{:S(2)}) collective-permute-start(bf16[4,64,256]{2,1,0:T(8,128)(2,1)S(1)} %constant_dynamic-update-slice_fusion.14.refs_1_), channel_id=1, source_target_pairs={{0,2},{1,5},{2,0},{3,7},{4,6},{5,1},{6,4},{7,3},{8,10},{9,13},{10,... | collective-permute-start | bytes 393224 | tf_op jit(solution)/shard_map/ppermute | solution.py:39
  154.5 6.2 %collective-permute-start.85 = (bf16[4,64,256]{2,1,0:T(8,128)(2,1)S(1)}, bf16[4,64,256]{2,1,0:T(8,128)(2,1)S(1)}, u32[]{:S(2)}, u32[]{:S(2)}) collective-permute-start(bf16[4,64,256]{2,1,0:T(8,128)(2,1)S(1)} %constant_dynamic-update-slice_fusion.14.refs_1_), channel_id=1, source_target_pairs={{0,1},{1,0},{2,3},{3,2},{4,5},{5,4},{6,7},{7,6},{8,9},{9,8},{10,11... | collective-permute-start | bytes 393224 | tf_op jit(solution)/shard_map/ppermute | solution.py:28
  154.5 6.4 %collective-permute-start.81 = (bf16[4,64,256]{2,1,0:T(8,128)(2,1)S(1)}, bf16[4,64,256]{2,1,0:T(8,128)(2,1)S(1)}, u32[]{:S(2)}, u32[]{:S(2)}) collective-permute-start(bf16[4,64,256]{2,1,0:T(8,128)(2,1)S(1)} %constant_dynamic-update-slice_fusion.14.refs_1_), channel_id=1, source_target_pairs={{0,4},{1,3},{2,6},{3,1},{4,0},{5,7},{6,2},{7,5},{8,12},{9,11},{10,... | collective-permute-start | bytes 393224 | tf_op jit(solution)/shard_map/ppermute | solution.py:39
  (81 other events, 405.5 us)

commit v7 on v6

--- a/solution.py
+++ b/solution.py
@@ -50,7 +50,7 @@
     far = [crossed_permute(part, two, one, core, count) for part in halves]
     both = [crossed_permute(part, two, one, core, count) for part in near]
     pieces = halves + near + far + both
-    return pieces + [xor_permute(piece, core, count) for piece in pieces]
+    return pieces
 
 
 def slot_of(me, other, groups, crossed, core):
@@ -69,13 +69,13 @@
     return slot + jnp.where((diff & core) != 0, 4 * place, 0)
 
 
-def matrix_kernel(rows, nbr, blk, count, slots, tiles, vec, res, diag, *refs):
+def matrix_kernel(rows, nbr, blk, count, last, slots, tiles, vec, res, diag, *refs):
     pieces, (image, keep, give, whole) = refs[:count], refs[count:]
     coef = 1.0 / (nbr * blk)
-    first = 0
+    at = 0
     for piece in pieces:
-        whole[first : first + piece.shape[0]] = piece[...]
-        first += piece.shape[0]
+        whole[at : at + piece.shape[0]] = piece[...]
+        at += piece.shape[0]
     n = vec.shape[0]
     for row in range(rows):
         acc = jnp.zeros((n, blk), jnp.float32)
@@ -91,12 +91,15 @@
         image[:, cols] = diag[:, cols] * vec[:, cols] + coef * acc
     img = image[...]
     old = res[...]
-    both = nt(jnp.concatenate([old, img], axis=0), jnp.concatenate([old, img], axis=0))
     curv = nt(vec[...], img)
-    first = jnp.concatenate([both[0:n, 0:n], curv], axis=1)
-    second = both[:, n : 2 * n]
-    second = jnp.concatenate([second[0:n], second[n : 2 * n]], axis=1)
     core = slots[rows * nbr]
+    if last:
+        both = jnp.concatenate([nt(old, old), curv], axis=1)
+        first, second = both[0 : n // 2], both[n // 2 : n]
+    else:
+        both = nt(jnp.concatenate([old, img], axis=0), jnp.concatenate([old, img], axis=0))
+        first = jnp.concatenate([both[0:n, 0:n], curv], axis=1)
+        second = jnp.concatenate([both[0:n, n : 2 * n], both[n : 2 * n, n : 2 * n]], axis=1)
     keep[...] = jnp.where(core == 0, first, second)
     give[...] = jnp.where(core == 0, second, first)
 
@@ -124,22 +127,59 @@
     )(source)
 
 
-def apply_matrix(slots, pieces, tiles, vec, res, diag):
+def load_kernel(parts, source, diag, after, target, diag_target, token, sems):
+    del after
+    rows = source.shape[0] // parts
+    copies = [pltpu.make_async_copy(diag, diag_target, sems.at[parts])]
+    for part in range(parts):
+        span = pl.ds(part * rows, rows)
+        copies.append(pltpu.make_async_copy(source.at[span], target.at[span], sems.at[part]))
+    for copy in copies:
+        copy.start()
+    token[...] = jnp.zeros_like(token)
+    for copy in copies:
+        copy.wait()
+
+
+def load(source, diag, after):
+    anywhere = pl.BlockSpec(memory_space=pl.ANY)
+    vmem = pl.BlockSpec(memory_space=pltpu.VMEM)
+    parts = source.shape[0]
+    return pl.pallas_call(
+        functools.partial(load_kernel, parts),
+        out_shape=(
+            jax.ShapeDtypeStruct(source.shape, source.dtype),
+            jax.ShapeDtypeStruct(diag.shape, diag.dtype),
+            jax.ShapeDtypeStruct((8, 128), jnp.float32),
+        ),
+        in_specs=[anywhere] * 3,
+        out_specs=(vmem, vmem, vmem),
+        scratch_shapes=[pltpu.SemaphoreType.DMA((parts + 1,))],
+        compiler_params=pltpu.CompilerParams(vmem_limit_bytes=6 * 1024 * 1024),
+        name="load",
+    )(
+        pltpu.with_memory_space_constraint(source, pltpu.HBM),
+        pltpu.with_memory_space_constraint(diag, pltpu.HBM),
+        after,
+    )
+
+
+def apply_matrix(last, slots, pieces, tiles, vec, res, diag):
     rows, nbr, blk, _ = tiles.shape
     n = vec.shape[0]
     vmem = pl.BlockSpec(memory_space=pltpu.VMEM)
-    half = jax.ShapeDtypeStruct((n, 2 * n), jnp.float32)
     blocks = sum(piece.shape[0] for piece in pieces)
     grant = 2 * blocks * n * blk * 2 + tiles.size * 2 + 2 * 1024 * 1024
+    half = jax.ShapeDtypeStruct((n // 2 if last else n, 2 * n), jnp.float32)
+    outs = [jax.ShapeDtypeStruct(vec.shape, jnp.float32), half, half]
+    scratch = [pltpu.VMEM((blocks, n, blk), tiles.dtype)]
     return pl.pallas_call(
-        functools.partial(matrix_kernel, rows, nbr, blk, len(pieces)),
-        out_shape=(jax.ShapeDtypeStruct(vec.shape, jnp.float32), half, half),
+        functools.partial(matrix_kernel, rows, nbr, blk, len(pieces), last),
+        out_shape=tuple(outs),
         in_specs=[pl.BlockSpec(memory_space=pltpu.SMEM), vmem, vmem, vmem, vmem]
         + [vmem] * len(pieces),
-        out_specs=(vmem, vmem, vmem),
-        scratch_shapes=[
-            pltpu.VMEM((blocks, n, blk), tiles.dtype),
-        ],
+        out_specs=tuple([vmem] * len(outs)),
+        scratch_shapes=scratch,
         compiler_params=pltpu.CompilerParams(vmem_limit_bytes=grant),
         name="matrix",
     )(slots, tiles, vec, res, diag, *pieces)
@@ -205,6 +245,8 @@
     n = vec.shape[0]
     at_zero = core[0] == 0
     first = jnp.where(at_zero, mine[...], other[...])
+    if last:
+        first = jnp.concatenate([first, jnp.where(at_zero, other[...], mine[...])], axis=0)
     gram, curv = first[:, 0:n], first[:, n : 2 * n]
     inverses = invert_pair(jnp.concatenate([curv, gram], axis=1), n)
     alpha_t = nn(gram, inverses[:, 0:n])
@@ -256,7 +298,11 @@
     for step in range(ITERS):
         last = step + 1 == ITERS
         pieces = gather_of(rounded, groups, crossed, core_bit, count)
-        image, keep, give = apply_matrix(slots, pieces, tiles, vec, res, diag)
+        if step == 0:
+            tiles, diag, token = load(tiles, diag, pieces[3])
+            pieces[5], _ = lax.optimization_barrier((pieces[5], token))
+        pieces += [xor_permute(piece, core_bit, count) for piece in pieces]
+        image, keep, give = apply_matrix(last, slots, pieces, tiles, vec, res, diag)
         mine = keep + xor_permute(give, core_bit, count)
         for masks in stages:
             terms = spread(mine, masks, count)

time: 188 us -> 186 us (0.989)
  Pallas kernels: 24.1 us -> 27.1 us
  waiting for transfers between devices: 76.9 us -> 73.9 us
  local copies, waits for them, and re-layouts: 4.63 us -> 1.76 us
    ppermute x76, waiting for transfers between devices: 51.2 us -> 47.8 us  [xor_permute(): return lax.ppermute(val, AXES, [(i, i ^ mask) for i in range(count)])]
    unnamed x18 -> x10, local copies, waits for them, and re-layouts: 3.82 us -> 0.94 us
    pallas_call x0 -> x1, Pallas kernels: none -> 2.86 us  [load(): pl.pallas_call(functools.partial(load_kernel, parts), out_shape=(jax.Shap...]
  transfers between devices with their start and end apart: 100 -> 100, of which waited for: 53 -> 51; matrix products, arithmetic and copies ran while one was open for 1% -> 1% of each run, Pallas kernels for 0% -> 2%
where the time goes in v7:
time: 186 us
  starting transfers between devices  81.9 us (44%)
  waiting for transfers between devices  73.9 us (40%)
  Pallas kernels  27.1 us (15%)
    ppermute x76, starting transfers between devices, xor_permute(): return lax.ppermute(val, AXES, [(i, i ^ mask) for i in range(count)])  55.2 us
    ppermute x76, waiting for transfers between devices, xor_permute(): return lax.ppermute(val, AXES, [(i, i ^ mask) for i in range(count)])  47.8 us
    ppermute x24, starting transfers between devices, crossed_permute(): lax.ppermute(val, AXES, [(i, i ^ (odd if i & core else even)) for i in ra...  26.6 us
    ppermute x24, waiting for transfers between devices, crossed_permute(): lax.ppermute(val, AXES, [(i, i ^ (odd if i & core else even)) for i in ra...  26.1 us
    pallas_call x4, Pallas kernels, solve_step(): pl.pallas_call(functools.partial(solve_kernel, last), out_shape=tuple(out...  14.1 us
    pallas_call x4, Pallas kernels, apply_matrix(): pl.pallas_call(functools.partial(matrix_kernel, rows, nbr, blk, len(piece...  10.1 us
  transfers between devices with their start and end apart: 100, of which 51 were waited for; matrix products, arithmetic and copies ran while one was open for 1% of the time, Pallas kernels for 2%

profile of v7, /device:TPU:0, one launch (start us, length us, event | category | flops | bytes accessed | tf_op | source)
XLA Modules:
  0.0 185.9 jit_solution(2107589150160923816)
XLA Ops:
  1.6 3.1 %collective-permute-start.3 = (bf16[2,64,256]{2,1,0:T(8,128)(2,1)S(1)}, bf16[2,64,256]{2,1,0:T(8,128)(2,1)S(1)}, u32[]{:S(2)}, u32[]{:S(2)}) collective-permute-start(bf16[2,64,256]{2,1,0:T(8,128)(2,1)S(1)} %get-tuple-element.30), channel_id=1, source_target_pairs={{0,8},{1,9},{2,10},{3,11},{4,12},{5,13},{6,14},{7,15},{8,0},{9,1},... | collective-permute-start | bytes 196616 | tf_op jit(solution)/shard_map/ppermute | solution.py:28
  4.6 2.5 %collective-permute-start.1 = (bf16[2,64,256]{2,1,0:T(8,128)(2,1)S(1)}, bf16[2,64,256]{2,1,0:T(8,128)(2,1)S(1)}, u32[]{:S(2)}, u32[]{:S(2)}) collective-permute-start(bf16[2,64,256]{2,1,0:T(8,128)(2,1)S(1)} %get-tuple-element.30), channel_id=1, source_target_pairs={{0,24},{1,25},{2,26},{3,27},{4,28},{5,29},{6,30},{7,31},{8,16},{9,... | collective-permute-start | bytes 196616 | tf_op jit(solution)/shard_map/ppermute | solution.py:28
  10.4 3.2 %collective-permute-done = bf16[2,64,256]{2,1,0:T(8,128)(2,1)S(1)} collective-permute-done((bf16[2,64,256]{2,1,0:T(8,128)(2,1)S(1)}, bf16[2,64,256]{2,1,0:T(8,128)(2,1)S(1)}, u32[]{:S(2)}, u32[]{:S(2)}) %collective-permute-start) | collective-permute-done | bytes 65568 | tf_op jit(solution)/shard_map/ppermute | solution.py:28
  17.3 2.5 %collective-permute-done.6.refs_5_ = bf16[4,64,256]{2,1,0:T(8,128)(2,1)S(1)} collective-permute-done((bf16[4,64,256]{2,1,0:T(8,128)(2,1)S(1)}, bf16[4,64,256]{2,1,0:T(8,128)(2,1)S(1)}, u32[]{:S(2)}, u32[]{:S(2)}) %collective-permute-start.6) | collective-permute-done | bytes 131104 | tf_op jit(solution)/shard_map/ppermute | solution.py:39
  26.4 2.9 %load.1 = (bf16[2,16,256,256]{3,2,1,0:T(8,128)(2,1)S(1)}, f32[1,512]{1,0:T(1,128)S(1)}, f32[8,128]{1,0:T(8,128)}) custom-call(bf16[2,16,256,256]{3,2,1,0:T(8,128)(2,1)} %source.3, f32[1,512]{1,0:T(1,128)} %bitcast.2, bf16[4,64,256]{2,1,0:T(8,128)(2,1)S(1)} %collective-permute-done.2.after.refs_3_), custom_call_target="tpu_custom_call" | custom-call | tf_op jit(solution)/shard_map/load/pallas_call | solution.py:148
  29.3 2.6 %matrix.4 = (f32[64,512]{1,0:T(8,128)S(1)}, f32[64,128]{1,0:T(8,128)S(1)}, f32[64,128]{1,0:T(8,128)S(1)}) custom-call(s32[33]{0:T(128)S(1)} %pad_add_fusion.slots, bf16[2,16,256,256]{3,2,1,0:T(8,128)(2,1)S(1)} %get-tuple-element.31.tiles, f32[64,512]{1,0:T(8,128)S(1)} %get-tuple-element.32.vec.res, f32[64,512]{1,0:T(8,128)S(1)} %get-tuple-element.32.vec.res, ...), custom_call_target="tpu_custom_call" | custom-call | tf_op jit(solution)/shard_map/matrix/pallas_call | solution.py:176
  39.7 2.7 %collective-permute-start.23 = (f32[64,128]{1,0:T(8,128)S(1)}, f32[64,128]{1,0:T(8,128)S(1)}, u32[]{:S(2)}, u32[]{:S(2)}) collective-permute-start(f32[64,128]{1,0:T(8,128)S(1)} %add_add_fusion.5), channel_id=1, source_target_pairs={{0,24},{1,25},{2,26},{3,27},{4,28},{5,29},{6,30},{7,31},{8,16},{9,... | collective-permute-start | bytes 98312 | tf_op jit(solution)/shard_map/ppermute | solution.py:28
  48.5 3.6 %small.3 = (f32[64,512]{1,0:T(8,128)S(1)}, f32[64,512]{1,0:T(8,128)S(1)}, f32[64,512]{1,0:T(8,128)S(1)}, bf16[2,64,256]{2,1,0:T(8,128)(2,1)S(1)}) custom-call(s32[1]{0:T(128)} %bitcast.core, f32[64,128]{1,0:T(8,128)S(1)} %add_add_fusion.4.mine, f32[64,128]{1,0:T(8,128)S(1)} %collective-permute-done.24.other, f32[64,512]{1,0:T(8,128)S(1)} %get-tuple-element.32.vec.res, ...), custom_call_target="tpu_custom_call" | custom-call | tf_op jit(solution)/shard_map/small/pallas_call | solution.py:277
  54.6 2.0 %collective-permute-start.25 = (bf16[2,64,256]{2,1,0:T(8,128)(2,1)S(1)}, bf16[2,64,256]{2,1,0:T(8,128)(2,1)S(1)}, u32[]{:S(2)}, u32[]{:S(2)}) collective-permute-start(bf16[2,64,256]{2,1,0:T(8,128)(2,1)S(1)} %get-tuple-element.39), channel_id=1, source_target_pairs={{0,8},{1,9},{2,10},{3,11},{4,12},{5,13},{6,14},{7,15},{8,0},{9,1},... | collective-permute-start | bytes 196616 | tf_op jit(solution)/shard_map/ppermute | solution.py:28
  56.6 3.7 %collective-permute-done.25 = bf16[2,64,256]{2,1,0:T(8,128)(2,1)S(1)} collective-permute-done((bf16[2,64,256]{2,1,0:T(8,128)(2,1)S(1)}, bf16[2,64,256]{2,1,0:T(8,128)(2,1)S(1)}, u32[]{:S(2)}, u32[]{:S(2)}) %collective-permute-start.25) | collective-permute-done | bytes 65568 | tf_op jit(solution)/shard_map/ppermute | solution.py:28
  64.6 2.1 %collective-permute-done.30.refs_4_ = bf16[4,64,256]{2,1,0:T(8,128)(2,1)S(1)} collective-permute-done((bf16[4,64,256]{2,1,0:T(8,128)(2,1)S(1)}, bf16[4,64,256]{2,1,0:T(8,128)(2,1)S(1)}, u32[]{:S(2)}, u32[]{:S(2)}) %collective-permute-start.30) | collective-permute-done | bytes 131104 | tf_op jit(solution)/shard_map/ppermute | solution.py:39
  71.7 2.3 %collective-permute-done.33.refs_7_ = bf16[4,64,256]{2,1,0:T(8,128)(2,1)S(1)} collective-permute-done((bf16[4,64,256]{2,1,0:T(8,128)(2,1)S(1)}, bf16[4,64,256]{2,1,0:T(8,128)(2,1)S(1)}, u32[]{:S(2)}, u32[]{:S(2)}) %collective-permute-start.33) | collective-permute-done | bytes 131104 | tf_op jit(solution)/shard_map/ppermute | solution.py:39
  75.4 2.6 %matrix.5 = (f32[64,512]{1,0:T(8,128)S(1)}, f32[64,128]{1,0:T(8,128)S(1)}, f32[64,128]{1,0:T(8,128)S(1)}) custom-call(s32[33]{0:T(128)S(1)} %pad_add_fusion.slots, bf16[2,16,256,256]{3,2,1,0:T(8,128)(2,1)S(1)} %get-tuple-element.31.tiles, f32[64,512]{1,0:T(8,128)S(1)} %get-tuple-element.37.vec, f32[64,512]{1,0:T(8,128)S(1)} %get-tuple-element.38.res, ...), custom_call_target="tpu_custom_call" | custom-call | tf_op jit(solution)/shard_map/matrix/pallas_call | solution.py:176
  93.2 3.6 %small.4 = (f32[64,512]{1,0:T(8,128)S(1)}, f32[64,512]{1,0:T(8,128)S(1)}, f32[64,512]{1,0:T(8,128)S(1)}, bf16[2,64,256]{2,1,0:T(8,128)(2,1)S(1)}) custom-call(s32[1]{0:T(128)} %bitcast.core, f32[64,128]{1,0:T(8,128)S(1)} %add_add_fusion.2.mine, f32[64,128]{1,0:T(8,128)S(1)} %collective-permute-done.49.other, f32[64,512]{1,0:T(8,128)S(1)} %get-tuple-element.37.vec, ...), custom_call_target="tpu_custom_call" | custom-call | tf_op jit(solution)/shard_map/small/pallas_call | solution.py:277
  101.3 3.3 %collective-permute-done.50 = bf16[2,64,256]{2,1,0:T(8,128)(2,1)S(1)} collective-permute-done((bf16[2,64,256]{2,1,0:T(8,128)(2,1)S(1)}, bf16[2,64,256]{2,1,0:T(8,128)(2,1)S(1)}, u32[]{:S(2)}, u32[]{:S(2)}) %collective-permute-start.50) | collective-permute-done | bytes 65568 | tf_op jit(solution)/shard_map/ppermute | solution.py:28
  115.8 2.5 %collective-permute-done.58.refs_7_ = bf16[4,64,256]{2,1,0:T(8,128)(2,1)S(1)} collective-permute-done((bf16[4,64,256]{2,1,0:T(8,128)(2,1)S(1)}, bf16[4,64,256]{2,1,0:T(8,128)(2,1)S(1)}, u32[]{:S(2)}, u32[]{:S(2)}) %collective-permute-start.58) | collective-permute-done | bytes 131104 | tf_op jit(solution)/shard_map/ppermute | solution.py:39
  119.6 2.6 %matrix.6 = (f32[64,512]{1,0:T(8,128)S(1)}, f32[64,128]{1,0:T(8,128)S(1)}, f32[64,128]{1,0:T(8,128)S(1)}) custom-call(s32[33]{0:T(128)S(1)} %pad_add_fusion.slots, bf16[2,16,256,256]{3,2,1,0:T(8,128)(2,1)S(1)} %get-tuple-element.31.tiles, f32[64,512]{1,0:T(8,128)S(1)} %get-tuple-element.44.vec, f32[64,512]{1,0:T(8,128)S(1)} %get-tuple-element.45.res, ...), custom_call_target="tpu_custom_call" | custom-call | tf_op jit(solution)/shard_map/matrix/pallas_call | solution.py:176
  130.1 2.7 %collective-permute-start.73 = (f32[64,128]{1,0:T(8,128)S(1)}, f32[64,128]{1,0:T(8,128)S(1)}, u32[]{:S(2)}, u32[]{:S(2)}) collective-permute-start(f32[64,128]{1,0:T(8,128)S(1)} %add_add_fusion.1), channel_id=1, source_target_pairs={{0,24},{1,25},{2,26},{3,27},{4,28},{5,29},{6,30},{7,31},{8,16},{9,... | collective-permute-start | bytes 98312 | tf_op jit(solution)/shard_map/ppermute | solution.py:28
  138.8 3.6 %small.5 = (f32[64,512]{1,0:T(8,128)S(1)}, f32[64,512]{1,0:T(8,128)S(1)}, f32[64,512]{1,0:T(8,128)S(1)}, bf16[2,64,256]{2,1,0:T(8,128)(2,1)S(1)}) custom-call(s32[1]{0:T(128)} %bitcast.core, f32[64,128]{1,0:T(8,128)S(1)} %add_add_fusion.mine, f32[64,128]{1,0:T(8,128)S(1)} %collective-permute-done.74.other, f32[64,512]{1,0:T(8,128)S(1)} %get-tuple-element.44.vec, ...), custom_call_target="tpu_custom_call" | custom-call | tf_op jit(solution)/shard_map/small/pallas_call | solution.py:277
  147.0 3.7 %collective-permute-done.75 = bf16[2,64,256]{2,1,0:T(8,128)(2,1)S(1)} collective-permute-done((bf16[2,64,256]{2,1,0:T(8,128)(2,1)S(1)}, bf16[2,64,256]{2,1,0:T(8,128)(2,1)S(1)}, u32[]{:S(2)}, u32[]{:S(2)}) %collective-permute-start.75) | collective-permute-done | bytes 65568 | tf_op jit(solution)/shard_map/ppermute | solution.py:28
  154.9 2.1 %collective-permute-done.80.refs_4_ = bf16[4,64,256]{2,1,0:T(8,128)(2,1)S(1)} collective-permute-done((bf16[4,64,256]{2,1,0:T(8,128)(2,1)S(1)}, bf16[4,64,256]{2,1,0:T(8,128)(2,1)S(1)}, u32[]{:S(2)}, u32[]{:S(2)}) %collective-permute-start.80) | collective-permute-done | bytes 131104 | tf_op jit(solution)/shard_map/ppermute | solution.py:39
  162.1 2.0 %collective-permute-done.83.refs_7_ = bf16[4,64,256]{2,1,0:T(8,128)(2,1)S(1)} collective-permute-done((bf16[4,64,256]{2,1,0:T(8,128)(2,1)S(1)}, bf16[4,64,256]{2,1,0:T(8,128)(2,1)S(1)}, u32[]{:S(2)}, u32[]{:S(2)}) %collective-permute-start.83) | collective-permute-done | bytes 131104 | tf_op jit(solution)/shard_map/ppermute | solution.py:39
  165.5 2.4 %matrix.7 = (f32[64,512]{1,0:T(8,128)S(1)}, f32[32,128]{1,0:T(8,128)S(1)}, f32[32,128]{1,0:T(8,128)S(1)}) custom-call(s32[33]{0:T(128)S(1)} %pad_add_fusion.slots, bf16[2,16,256,256]{3,2,1,0:T(8,128)(2,1)S(1)} %get-tuple-element.31.tiles, f32[64,512]{1,0:T(8,128)S(1)} %get-tuple-element.51.vec, f32[64,512]{1,0:T(8,128)S(1)} %get-tuple-element.52.res, ...), custom_call_target="tpu_custom_call" | custom-call | tf_op jit(solution)/shard_map/matrix/pallas_call | solution.py:176
  182.7 3.2 %small_last.1 = (f32[64,512]{1,0:T(8,128)}, f32[64,512]{1,0:T(8,128)}) custom-call(s32[1]{0:T(128)} %bitcast.core, f32[32,128]{1,0:T(8,128)S(1)} %add_add_fusion.6.mine, f32[32,128]{1,0:T(8,128)S(1)} %collective-permute-done.99.other, f32[64,512]{1,0:T(8,128)S(1)} %get-tuple-element.51.vec, f32[64,512]{1,0:T(8,128)S(1)} %get-tuple-element.52.res, ...), custom_call_target="tpu_custom_call" | custom-call | tf_op jit(solution)/shard_map/small_last/pallas_call | solution.py:277
  (220 shorter events, 117.1 us)
Async XLA Ops:
  4.6 8.9 %collective-permute-start.1 = (bf16[2,64,256]{2,1,0:T(8,128)(2,1)S(1)}, bf16[2,64,256]{2,1,0:T(8,128)(2,1)S(1)}, u32[]{:S(2)}, u32[]{:S(2)}) collective-permute-start(bf16[2,64,256]{2,1,0:T(8,128)(2,1)S(1)} %get-tuple-element.30), channel_id=1, source_target_pairs={{0,24},{1,25},{2,26},{3,27},{4,28},{5,29},{6,30},{7,31},{8,16},{9,... | collective-permute-start | bytes 196616 | tf_op jit(solution)/shard_map/ppermute | solution.py:28
  7.1 6.4 %collective-permute-start = (bf16[2,64,256]{2,1,0:T(8,128)(2,1)S(1)}, bf16[2,64,256]{2,1,0:T(8,128)(2,1)S(1)}, u32[]{:S(2)}, u32[]{:S(2)}) collective-permute-start(bf16[2,64,256]{2,1,0:T(8,128)(2,1)S(1)} %get-tuple-element.30), channel_id=1, source_target_pairs={{0,16},{1,17},{2,18},{3,19},{4,20},{5,21},{6,22},{7,23},{8,24},{9,... | collective-permute-start | bytes 196616 | tf_op jit(solution)/shard_map/ppermute | solution.py:28
  7.3 9.4 %collective-permute-start.5 = (bf16[4,64,256]{2,1,0:T(8,128)(2,1)S(1)}, bf16[4,64,256]{2,1,0:T(8,128)(2,1)S(1)}, u32[]{:S(2)}, u32[]{:S(2)}) collective-permute-start(bf16[4,64,256]{2,1,0:T(8,128)(2,1)S(1)} %constant_dynamic-update-slice_fusion.2.refs_0_), channel_id=1, source_target_pairs={{0,4},{1,3},{2,6},{3,1},{4,0},{5,7},{6,2},{7,5},{8,12},{9,11},{10,... | collective-permute-start | bytes 393224 | tf_op jit(solution)/shard_map/ppermute | solution.py:39
  8.9 8.3 %collective-permute-start.4 = (bf16[4,64,256]{2,1,0:T(8,128)(2,1)S(1)}, bf16[4,64,256]{2,1,0:T(8,128)(2,1)S(1)}, u32[]{:S(2)}, u32[]{:S(2)}) collective-permute-start(bf16[4,64,256]{2,1,0:T(8,128)(2,1)S(1)} %constant_dynamic-update-slice_fusion.2.refs_0_), channel_id=1, source_target_pairs={{0,2},{1,5},{2,0},{3,7},{4,6},{5,1},{6,4},{7,3},{8,10},{9,13},{10,... | collective-permute-start | bytes 393224 | tf_op jit(solution)/shard_map/ppermute | solution.py:39
  13.6 6.2 %collective-permute-start.6 = (bf16[4,64,256]{2,1,0:T(8,128)(2,1)S(1)}, bf16[4,64,256]{2,1,0:T(8,128)(2,1)S(1)}, u32[]{:S(2)}, u32[]{:S(2)}) collective-permute-start(bf16[4,64,256]{2,1,0:T(8,128)(2,1)S(1)} %constant_dynamic-update-slice_fusion.refs_1_), channel_id=1, source_target_pairs={{0,4},{1,3},{2,6},{3,1},{4,0},{5,7},{6,2},{7,5},{8,12},{9,11},{10,... | collective-permute-start | bytes 393224 | tf_op jit(solution)/shard_map/ppermute | solution.py:39
  22.6 6.7 %collective-permute-start.14 = (bf16[4,64,256]{2,1,0:T(8,128)(2,1)S(1)}, bf16[4,64,256]{2,1,0:T(8,128)(2,1)S(1)}, u32[]{:S(2)}, u32[]{:S(2)}) collective-permute-start(bf16[4,64,256]{2,1,0:T(8,128)(2,1)S(1)} %collective-permute-done.6.refs_5_), channel_id=1, source_target_pairs={{0,1},{1,0},{2,3},{3,2},{4,5},{5,4},{6,7},{7,6},{8,9},{9,8},{10,11... | collective-permute-start | bytes 393224 | tf_op jit(solution)/shard_map/ppermute | solution.py:28
  22.6 6.7 %collective-permute-start.11 = (bf16[4,64,256]{2,1,0:T(8,128)(2,1)S(1)}, bf16[4,64,256]{2,1,0:T(8,128)(2,1)S(1)}, u32[]{:S(2)}, u32[]{:S(2)}) collective-permute-start(bf16[4,64,256]{2,1,0:T(8,128)(2,1)S(1)} %collective-permute-done.4.refs_2_), channel_id=1, source_target_pairs={{0,1},{1,0},{2,3},{3,2},{4,5},{5,4},{6,7},{7,6},{8,9},{9,8},{10,11... | collective-permute-start | bytes 393224 | tf_op jit(solution)/shard_map/ppermute | solution.py:28
  52.2 9.6 %collective-permute-start.27 = (bf16[2,64,256]{2,1,0:T(8,128)(2,1)S(1)}, bf16[2,64,256]{2,1,0:T(8,128)(2,1)S(1)}, u32[]{:S(2)}, u32[]{:S(2)}) collective-permute-start(bf16[2,64,256]{2,1,0:T(8,128)(2,1)S(1)} %get-tuple-element.39), channel_id=1, source_target_pairs={{0,24},{1,25},{2,26},{3,27},{4,28},{5,29},{6,30},{7,31},{8,16},{9,... | collective-permute-start | bytes 196616 | tf_op jit(solution)/shard_map/ppermute | solution.py:28
  54.0 7.8 %collective-permute-start.26 = (bf16[2,64,256]{2,1,0:T(8,128)(2,1)S(1)}, bf16[2,64,256]{2,1,0:T(8,128)(2,1)S(1)}, u32[]{:S(2)}, u32[]{:S(2)}) collective-permute-start(bf16[2,64,256]{2,1,0:T(8,128)(2,1)S(1)} %get-tuple-element.39), channel_id=1, source_target_pairs={{0,16},{1,17},{2,18},{3,19},{4,20},{5,21},{6,22},{7,23},{8,24},{9,... | collective-permute-start | bytes 196616 | tf_op jit(solution)/shard_map/ppermute | solution.py:28
  60.4 6.4 %collective-permute-start.30 = (bf16[4,64,256]{2,1,0:T(8,128)(2,1)S(1)}, bf16[4,64,256]{2,1,0:T(8,128)(2,1)S(1)}, u32[]{:S(2)}, u32[]{:S(2)}) collective-permute-start(bf16[4,64,256]{2,1,0:T(8,128)(2,1)S(1)} %constant_dynamic-update-slice_fusion.4.refs_0_), channel_id=1, source_target_pairs={{0,4},{1,3},{2,6},{3,1},{4,0},{5,7},{6,2},{7,5},{8,12},{9,11},{10,... | collective-permute-start | bytes 393224 | tf_op jit(solution)/shard_map/ppermute | solution.py:39
  61.8 7.3 %collective-permute-start.29 = (bf16[4,64,256]{2,1,0:T(8,128)(2,1)S(1)}, bf16[4,64,256]{2,1,0:T(8,128)(2,1)S(1)}, u32[]{:S(2)}, u32[]{:S(2)}) collective-permute-start(bf16[4,64,256]{2,1,0:T(8,128)(2,1)S(1)} %constant_dynamic-update-slice_fusion.6.refs_1_), channel_id=1, source_target_pairs={{0,2},{1,5},{2,0},{3,7},{4,6},{5,1},{6,4},{7,3},{8,10},{9,13},{10,... | collective-permute-start | bytes 393224 | tf_op jit(solution)/shard_map/ppermute | solution.py:39
  62.7 7.2 %collective-permute-start.35 = (bf16[4,64,256]{2,1,0:T(8,128)(2,1)S(1)}, bf16[4,64,256]{2,1,0:T(8,128)(2,1)S(1)}, u32[]{:S(2)}, u32[]{:S(2)}) collective-permute-start(bf16[4,64,256]{2,1,0:T(8,128)(2,1)S(1)} %constant_dynamic-update-slice_fusion.6.refs_1_), channel_id=1, source_target_pairs={{0,1},{1,0},{2,3},{3,2},{4,5},{5,4},{6,7},{7,6},{8,9},{9,8},{10,11... | collective-permute-start | bytes 393224 | tf_op jit(solution)/shard_map/ppermute | solution.py:28
  62.7 7.2 %collective-permute-start.31 = (bf16[4,64,256]{2,1,0:T(8,128)(2,1)S(1)}, bf16[4,64,256]{2,1,0:T(8,128)(2,1)S(1)}, u32[]{:S(2)}, u32[]{:S(2)}) collective-permute-start(bf16[4,64,256]{2,1,0:T(8,128)(2,1)S(1)} %constant_dynamic-update-slice_fusion.6.refs_1_), channel_id=1, source_target_pairs={{0,4},{1,3},{2,6},{3,1},{4,0},{5,7},{6,2},{7,5},{8,12},{9,11},{10,... | collective-permute-start | bytes 393224 | tf_op jit(solution)/shard_map/ppermute | solution.py:39
  96.8 10.2 %collective-permute-start.52 = (bf16[2,64,256]{2,1,0:T(8,128)(2,1)S(1)}, bf16[2,64,256]{2,1,0:T(8,128)(2,1)S(1)}, u32[]{:S(2)}, u32[]{:S(2)}) collective-permute-start(bf16[2,64,256]{2,1,0:T(8,128)(2,1)S(1)} %get-tuple-element.46), channel_id=1, source_target_pairs={{0,24},{1,25},{2,26},{3,27},{4,28},{5,29},{6,30},{7,31},{8,16},{9,... | collective-permute-start | bytes 196616 | tf_op jit(solution)/shard_map/ppermute | solution.py:28
  98.8 8.2 %collective-permute-start.51 = (bf16[2,64,256]{2,1,0:T(8,128)(2,1)S(1)}, bf16[2,64,256]{2,1,0:T(8,128)(2,1)S(1)}, u32[]{:S(2)}, u32[]{:S(2)}) collective-permute-start(bf16[2,64,256]{2,1,0:T(8,128)(2,1)S(1)} %get-tuple-element.46), channel_id=1, source_target_pairs={{0,16},{1,17},{2,18},{3,19},{4,20},{5,21},{6,22},{7,23},{8,24},{9,... | collective-permute-start | bytes 196616 | tf_op jit(solution)/shard_map/ppermute | solution.py:28
  107.0 6.3 %collective-permute-start.54 = (bf16[4,64,256]{2,1,0:T(8,128)(2,1)S(1)}, bf16[4,64,256]{2,1,0:T(8,128)(2,1)S(1)}, u32[]{:S(2)}, u32[]{:S(2)}) collective-permute-start(bf16[4,64,256]{2,1,0:T(8,128)(2,1)S(1)} %constant_dynamic-update-slice_fusion.10.refs_1_), channel_id=1, source_target_pairs={{0,2},{1,5},{2,0},{3,7},{4,6},{5,1},{6,4},{7,3},{8,10},{9,13},{10,... | collective-permute-start | bytes 393224 | tf_op jit(solution)/shard_map/ppermute | solution.py:39
  108.0 6.6 %collective-permute-start.60 = (bf16[4,64,256]{2,1,0:T(8,128)(2,1)S(1)}, bf16[4,64,256]{2,1,0:T(8,128)(2,1)S(1)}, u32[]{:S(2)}, u32[]{:S(2)}) collective-permute-start(bf16[4,64,256]{2,1,0:T(8,128)(2,1)S(1)} %constant_dynamic-update-slice_fusion.10.refs_1_), channel_id=1, source_target_pairs={{0,1},{1,0},{2,3},{3,2},{4,5},{5,4},{6,7},{7,6},{8,9},{9,8},{10,11... | collective-permute-start | bytes 393224 | tf_op jit(solution)/shard_map/ppermute | solution.py:28
  108.0 6.6 %collective-permute-start.56 = (bf16[4,64,256]{2,1,0:T(8,128)(2,1)S(1)}, bf16[4,64,256]{2,1,0:T(8,128)(2,1)S(1)}, u32[]{:S(2)}, u32[]{:S(2)}) collective-permute-start(bf16[4,64,256]{2,1,0:T(8,128)(2,1)S(1)} %constant_dynamic-update-slice_fusion.10.refs_1_), channel_id=1, source_target_pairs={{0,4},{1,3},{2,6},{3,1},{4,0},{5,7},{6,2},{7,5},{8,12},{9,11},{10,... | collective-permute-start | bytes 393224 | tf_op jit(solution)/shard_map/ppermute | solution.py:39
  142.5 9.8 %collective-permute-start.77 = (bf16[2,64,256]{2,1,0:T(8,128)(2,1)S(1)}, bf16[2,64,256]{2,1,0:T(8,128)(2,1)S(1)}, u32[]{:S(2)}, u32[]{:S(2)}) collective-permute-start(bf16[2,64,256]{2,1,0:T(8,128)(2,1)S(1)} %get-tuple-element.53), channel_id=1, source_target_pairs={{0,24},{1,25},{2,26},{3,27},{4,28},{5,29},{6,30},{7,31},{8,16},{9,... | collective-permute-start | bytes 196616 | tf_op jit(solution)/shard_map/ppermute | solution.py:28
  144.3 7.9 %collective-permute-start.76 = (bf16[2,64,256]{2,1,0:T(8,128)(2,1)S(1)}, bf16[2,64,256]{2,1,0:T(8,128)(2,1)S(1)}, u32[]{:S(2)}, u32[]{:S(2)}) collective-permute-start(bf16[2,64,256]{2,1,0:T(8,128)(2,1)S(1)} %get-tuple-element.53), channel_id=1, source_target_pairs={{0,16},{1,17},{2,18},{3,19},{4,20},{5,21},{6,22},{7,23},{8,24},{9,... | collective-permute-start | bytes 196616 | tf_op jit(solution)/shard_map/ppermute | solution.py:28
  150.7 6.4 %collective-permute-start.80 = (bf16[4,64,256]{2,1,0:T(8,128)(2,1)S(1)}, bf16[4,64,256]{2,1,0:T(8,128)(2,1)S(1)}, u32[]{:S(2)}, u32[]{:S(2)}) collective-permute-start(bf16[4,64,256]{2,1,0:T(8,128)(2,1)S(1)} %constant_dynamic-update-slice_fusion.12.refs_0_), channel_id=1, source_target_pairs={{0,4},{1,3},{2,6},{3,1},{4,0},{5,7},{6,2},{7,5},{8,12},{9,11},{10,... | collective-permute-start | bytes 393224 | tf_op jit(solution)/shard_map/ppermute | solution.py:39
  152.3 6.8 %collective-permute-start.79 = (bf16[4,64,256]{2,1,0:T(8,128)(2,1)S(1)}, bf16[4,64,256]{2,1,0:T(8,128)(2,1)S(1)}, u32[]{:S(2)}, u32[]{:S(2)}) collective-permute-start(bf16[4,64,256]{2,1,0:T(8,128)(2,1)S(1)} %constant_dynamic-update-slice_fusion.14.refs_1_), channel_id=1, source_target_pairs={{0,2},{1,5},{2,0},{3,7},{4,6},{5,1},{6,4},{7,3},{8,10},{9,13},{10,... | collective-permute-start | bytes 393224 | tf_op jit(solution)/shard_map/ppermute | solution.py:39
  153.7 6.5 %collective-permute-start.85 = (bf16[4,64,256]{2,1,0:T(8,128)(2,1)S(1)}, bf16[4,64,256]{2,1,0:T(8,128)(2,1)S(1)}, u32[]{:S(2)}, u32[]{:S(2)}) collective-permute-start(bf16[4,64,256]{2,1,0:T(8,128)(2,1)S(1)} %constant_dynamic-update-slice_fusion.14.refs_1_), channel_id=1, source_target_pairs={{0,1},{1,0},{2,3},{3,2},{4,5},{5,4},{6,7},{7,6},{8,9},{9,8},{10,11... | collective-permute-start | bytes 393224 | tf_op jit(solution)/shard_map/ppermute | solution.py:28
  153.7 6.5 %collective-permute-start.81 = (bf16[4,64,256]{2,1,0:T(8,128)(2,1)S(1)}, bf16[4,64,256]{2,1,0:T(8,128)(2,1)S(1)}, u32[]{:S(2)}, u32[]{:S(2)}) collective-permute-start(bf16[4,64,256]{2,1,0:T(8,128)(2,1)S(1)} %constant_dynamic-update-slice_fusion.14.refs_1_), channel_id=1, source_target_pairs={{0,4},{1,3},{2,6},{3,1},{4,0},{5,7},{6,2},{7,5},{8,12},{9,11},{10,... | collective-permute-start | bytes 393224 | tf_op jit(solution)/shard_map/ppermute | solution.py:39
  (77 other events, 309.0 us)

commit v8 on v7

--- a/solution.py
+++ b/solution.py
@@ -104,11 +104,19 @@
     give[...] = jnp.where(core == 0, second, first)
 
 
-def round_kernel(source, target, same):
+def round_kernel(source, target, same, sems):
     blk = target.shape[2]
-    for row in range(target.shape[0]):
-        target[row] = source[:, row * blk : (row + 1) * blk].astype(jnp.bfloat16)
-    same[...] = source[...]
+    rows = target.shape[0]
+    spans = [pl.ds(row * blk, blk) for row in range(rows)]
+    copies = [
+        pltpu.make_async_copy(source.at[:, span], same.at[:, span], sems.at[row])
+        for row, span in enumerate(spans)
+    ]
+    for copy in copies:
+        copy.start()
+    for row in range(rows):
+        copies[row].wait()
+        target[row] = same[:, spans[row]].astype(jnp.bfloat16)
 
 
 def round_blocks(source, rows):
@@ -120,20 +128,25 @@
             jax.ShapeDtypeStruct((rows, n, width // rows), jnp.bfloat16),
             jax.ShapeDtypeStruct(source.shape, source.dtype),
         ),
-        in_specs=[vmem],
+        in_specs=[pl.BlockSpec(memory_space=pl.ANY)],
+        scratch_shapes=[pltpu.SemaphoreType.DMA((rows,))],
         out_specs=(vmem, vmem),
         compiler_params=pltpu.CompilerParams(vmem_limit_bytes=4 * 1024 * 1024),
         name="round",
-    )(source)
+    )(pltpu.with_memory_space_constraint(source, pltpu.HBM))
 
 
 def load_kernel(parts, source, diag, after, target, diag_target, token, sems):
     del after
-    rows = source.shape[0] // parts
+    rows, nbr = source.shape[:2]
+    each = rows * nbr // parts
     copies = [pltpu.make_async_copy(diag, diag_target, sems.at[parts])]
     for part in range(parts):
-        span = pl.ds(part * rows, rows)
-        copies.append(pltpu.make_async_copy(source.at[span], target.at[span], sems.at[part]))
+        row, at = divmod(part * each, nbr)
+        span = pl.ds(at, each)
+        copies.append(
+            pltpu.make_async_copy(source.at[row, span], target.at[row, span], sems.at[part])
+        )
     for copy in copies:
         copy.start()
     token[...] = jnp.zeros_like(token)
@@ -144,7 +157,7 @@
 def load(source, diag, after):
     anywhere = pl.BlockSpec(memory_space=pl.ANY)
     vmem = pl.BlockSpec(memory_space=pltpu.VMEM)
-    parts = source.shape[0]
+    parts = 16
     return pl.pallas_call(
         functools.partial(load_kernel, parts),
         out_shape=(
@@ -252,7 +265,7 @@
     alpha_t = nn(gram, inverses[:, 0:n])
     old = vec[...]
     new = res[...] - nn(alpha_t, image[...])
-    outs[0][...] = sol[...] + nn(alpha_t, old)
+    outs[0][...] = sol[...] + nn(alpha_t, old) if last else alpha_t
     outs[1][...] = new
     if not last:
         second = jnp.where(at_zero, other[...], mine[...])
@@ -273,6 +286,7 @@
     space = pl.BlockSpec(memory_space=pltpu.VMEM)
     outs = [shape, shape]
     if not last:
+        outs[0] = jax.ShapeDtypeStruct((n, n), jnp.float32)
         outs += [shape, jax.ShapeDtypeStruct((rows, n, width // rows), jnp.bfloat16)]
     return pl.pallas_call(
         functools.partial(solve_kernel, last),
@@ -282,6 +296,22 @@
         compiler_params=pltpu.CompilerParams(vmem_limit_bytes=8 * 1024 * 1024),
         name="small_last" if last else "small",
     )(core, mine, other, vec, res, sol, image)
+
+
+def grow_kernel(sol, alpha_t, vec, out):
+    out[...] = sol[...] + nn(alpha_t[...], vec[...])
+
+
+def grow(sol, alpha_t, vec):
+    space = pl.BlockSpec(memory_space=pltpu.VMEM)
+    return pl.pallas_call(
+        grow_kernel,
+        out_shape=jax.ShapeDtypeStruct(vec.shape, jnp.float32),
+        in_specs=[space] * 3,
+        out_specs=space,
+        compiler_params=pltpu.CompilerParams(vmem_limit_bytes=4 * 1024 * 1024),
+        name="grow",
+    )(sol, alpha_t, vec)
 
 
 def body(groups, crossed, stages, core_bit, count, cols, right_side, diag_vals, tiles, col_ids):
@@ -314,7 +344,9 @@
         if last:
             sol, res = outs
         else:
-            sol, res, vec, rounded = outs
+            alpha_t, res, step_vec, rounded = outs
+            sol = grow(sol, alpha_t, vec)
+            vec = step_vec
     return (sol, res)
 
 

time: 186 us -> 185 us (level)
  no operation moved by 1% of the time
where the time goes in v8:
time: 185 us
  starting transfers between devices  81.9 us (44%)
  waiting for transfers between devices  73 us (39%)
  Pallas kernels  27.9 us (15%)
    ppermute x76, starting transfers between devices, xor_permute(): return lax.ppermute(val, AXES, [(i, i ^ mask) for i in range(count)])  55.2 us
    ppermute x76, waiting for transfers between devices, xor_permute(): return lax.ppermute(val, AXES, [(i, i ^ mask) for i in range(count)])  47.1 us
    ppermute x24, starting transfers between devices, crossed_permute(): lax.ppermute(val, AXES, [(i, i ^ (odd if i & core else even)) for i in ra...  26.7 us
    ppermute x24, waiting for transfers between devices, crossed_permute(): lax.ppermute(val, AXES, [(i, i ^ (odd if i & core else even)) for i in ra...  25.9 us
    pallas_call x4, Pallas kernels, solve_step(): pl.pallas_call(functools.partial(solve_kernel, last), out_shape=tuple(out...  13.2 us
    pallas_call x4, Pallas kernels, apply_matrix(): pl.pallas_call(functools.partial(matrix_kernel, rows, nbr, blk, len(piece...  10.1 us
  transfers between devices with their start and end apart: 100, of which 51 were waited for; matrix products, arithmetic and copies ran while one was open for 1% of the time, Pallas kernels for 2%

profile of v8, /device:TPU:0, one launch (start us, length us, event | category | flops | bytes accessed | tf_op | source)
XLA Modules:
  0.0 185.0 jit_solution(14485876355430885848)
XLA Ops:
  1.5 3.1 %collective-permute-start.3 = (bf16[2,64,256]{2,1,0:T(8,128)(2,1)S(1)}, bf16[2,64,256]{2,1,0:T(8,128)(2,1)S(1)}, u32[]{:S(2)}, u32[]{:S(2)}) collective-permute-start(bf16[2,64,256]{2,1,0:T(8,128)(2,1)S(1)} %get-tuple-element.30), channel_id=1, source_target_pairs={{0,8},{1,9},{2,10},{3,11},{4,12},{5,13},{6,14},{7,15},{8,0},{9,1},... | collective-permute-start | bytes 196616 | tf_op jit(solution)/shard_map/ppermute | solution.py:28
  4.6 2.5 %collective-permute-start.1 = (bf16[2,64,256]{2,1,0:T(8,128)(2,1)S(1)}, bf16[2,64,256]{2,1,0:T(8,128)(2,1)S(1)}, u32[]{:S(2)}, u32[]{:S(2)}) collective-permute-start(bf16[2,64,256]{2,1,0:T(8,128)(2,1)S(1)} %get-tuple-element.30), channel_id=1, source_target_pairs={{0,24},{1,25},{2,26},{3,27},{4,28},{5,29},{6,30},{7,31},{8,16},{9,... | collective-permute-start | bytes 196616 | tf_op jit(solution)/shard_map/ppermute | solution.py:28
  10.3 3.2 %collective-permute-done = bf16[2,64,256]{2,1,0:T(8,128)(2,1)S(1)} collective-permute-done((bf16[2,64,256]{2,1,0:T(8,128)(2,1)S(1)}, bf16[2,64,256]{2,1,0:T(8,128)(2,1)S(1)}, u32[]{:S(2)}, u32[]{:S(2)}) %collective-permute-start) | collective-permute-done | bytes 65568 | tf_op jit(solution)/shard_map/ppermute | solution.py:28
  17.2 2.5 %collective-permute-done.6.refs_5_ = bf16[4,64,256]{2,1,0:T(8,128)(2,1)S(1)} collective-permute-done((bf16[4,64,256]{2,1,0:T(8,128)(2,1)S(1)}, bf16[4,64,256]{2,1,0:T(8,128)(2,1)S(1)}, u32[]{:S(2)}, u32[]{:S(2)}) %collective-permute-start.6) | collective-permute-done | bytes 131104 | tf_op jit(solution)/shard_map/ppermute | solution.py:39
  26.4 2.9 %load.1 = (bf16[2,16,256,256]{3,2,1,0:T(8,128)(2,1)S(1)}, f32[1,512]{1,0:T(1,128)S(1)}, f32[8,128]{1,0:T(8,128)}) custom-call(bf16[2,16,256,256]{3,2,1,0:T(8,128)(2,1)} %source.3, f32[1,512]{1,0:T(1,128)} %bitcast.2, bf16[4,64,256]{2,1,0:T(8,128)(2,1)S(1)} %collective-permute-done.2.after.refs_3_), custom_call_target="tpu_custom_call" | custom-call | tf_op jit(solution)/shard_map/load/pallas_call | solution.py:161
  29.3 2.6 %matrix.4 = (f32[64,512]{1,0:T(8,128)S(1)}, f32[64,128]{1,0:T(8,128)S(1)}, f32[64,128]{1,0:T(8,128)S(1)}) custom-call(s32[33]{0:T(128)S(1)} %pad_add_fusion.slots, bf16[2,16,256,256]{3,2,1,0:T(8,128)(2,1)S(1)} %get-tuple-element.31.tiles, f32[64,512]{1,0:T(8,128)S(1)} %get-tuple-element.32.vec.res, f32[64,512]{1,0:T(8,128)S(1)} %get-tuple-element.32.vec.res, ...), custom_call_target="tpu_custom_call" | custom-call | tf_op jit(solution)/shard_map/matrix/pallas_call | solution.py:189
  39.7 2.7 %collective-permute-start.23 = (f32[64,128]{1,0:T(8,128)S(1)}, f32[64,128]{1,0:T(8,128)S(1)}, u32[]{:S(2)}, u32[]{:S(2)}) collective-permute-start(f32[64,128]{1,0:T(8,128)S(1)} %add_add_fusion.5), channel_id=1, source_target_pairs={{0,24},{1,25},{2,26},{3,27},{4,28},{5,29},{6,30},{7,31},{8,16},{9,... | collective-permute-start | bytes 98312 | tf_op jit(solution)/shard_map/ppermute | solution.py:28
  48.5 3.4 %small.3 = (f32[64,64]{1,0:T(8,128)S(1)}, f32[64,512]{1,0:T(8,128)S(1)}, f32[64,512]{1,0:T(8,128)S(1)}, bf16[2,64,256]{2,1,0:T(8,128)(2,1)S(1)}) custom-call(s32[1]{0:T(128)} %bitcast.core, f32[64,128]{1,0:T(8,128)S(1)} %add_add_fusion.4.mine, f32[64,128]{1,0:T(8,128)S(1)} %collective-permute-done.24.other, f32[64,512]{1,0:T(8,128)S(1)} %get-tuple-element.32.vec.res, ...), custom_call_target="tpu_custom_call" | custom-call | tf_op jit(solution)/shard_map/small/pallas_call | solution.py:291
  54.3 2.1 %collective-permute-start.25 = (bf16[2,64,256]{2,1,0:T(8,128)(2,1)S(1)}, bf16[2,64,256]{2,1,0:T(8,128)(2,1)S(1)}, u32[]{:S(2)}, u32[]{:S(2)}) collective-permute-start(bf16[2,64,256]{2,1,0:T(8,128)(2,1)S(1)} %get-tuple-element.39), channel_id=1, source_target_pairs={{0,8},{1,9},{2,10},{3,11},{4,12},{5,13},{6,14},{7,15},{8,0},{9,1},... | collective-permute-start | bytes 196616 | tf_op jit(solution)/shard_map/ppermute | solution.py:28
  56.4 3.7 %collective-permute-done.25 = bf16[2,64,256]{2,1,0:T(8,128)(2,1)S(1)} collective-permute-done((bf16[2,64,256]{2,1,0:T(8,128)(2,1)S(1)}, bf16[2,64,256]{2,1,0:T(8,128)(2,1)S(1)}, u32[]{:S(2)}, u32[]{:S(2)}) %collective-permute-start.25) | collective-permute-done | bytes 65568 | tf_op jit(solution)/shard_map/ppermute | solution.py:28
  64.3 2.1 %collective-permute-done.30.refs_4_ = bf16[4,64,256]{2,1,0:T(8,128)(2,1)S(1)} collective-permute-done((bf16[4,64,256]{2,1,0:T(8,128)(2,1)S(1)}, bf16[4,64,256]{2,1,0:T(8,128)(2,1)S(1)}, u32[]{:S(2)}, u32[]{:S(2)}) %collective-permute-start.30) | collective-permute-done | bytes 131104 | tf_op jit(solution)/shard_map/ppermute | solution.py:39
  71.5 2.3 %collective-permute-done.33.refs_7_ = bf16[4,64,256]{2,1,0:T(8,128)(2,1)S(1)} collective-permute-done((bf16[4,64,256]{2,1,0:T(8,128)(2,1)S(1)}, bf16[4,64,256]{2,1,0:T(8,128)(2,1)S(1)}, u32[]{:S(2)}, u32[]{:S(2)}) %collective-permute-start.33) | collective-permute-done | bytes 131104 | tf_op jit(solution)/shard_map/ppermute | solution.py:39
  75.1 2.6 %matrix.5 = (f32[64,512]{1,0:T(8,128)S(1)}, f32[64,128]{1,0:T(8,128)S(1)}, f32[64,128]{1,0:T(8,128)S(1)}) custom-call(s32[33]{0:T(128)S(1)} %pad_add_fusion.slots, bf16[2,16,256,256]{3,2,1,0:T(8,128)(2,1)S(1)} %get-tuple-element.31.tiles, f32[64,512]{1,0:T(8,128)S(1)} %get-tuple-element.37.vec, f32[64,512]{1,0:T(8,128)S(1)} %get-tuple-element.38.res, ...), custom_call_target="tpu_custom_call" | custom-call | tf_op jit(solution)/shard_map/matrix/pallas_call | solution.py:189
  92.9 3.3 %small.4 = (f32[64,64]{1,0:T(8,128)S(1)}, f32[64,512]{1,0:T(8,128)S(1)}, f32[64,512]{1,0:T(8,128)S(1)}, bf16[2,64,256]{2,1,0:T(8,128)(2,1)S(1)}) custom-call(s32[1]{0:T(128)} %bitcast.core, f32[64,128]{1,0:T(8,128)S(1)} %add_add_fusion.2.mine, f32[64,128]{1,0:T(8,128)S(1)} %collective-permute-done.49.other, f32[64,512]{1,0:T(8,128)S(1)} %get-tuple-element.37.vec, ...), custom_call_target="tpu_custom_call" | custom-call | tf_op jit(solution)/shard_map/small/pallas_call | solution.py:291
  100.7 3.3 %collective-permute-done.50 = bf16[2,64,256]{2,1,0:T(8,128)(2,1)S(1)} collective-permute-done((bf16[2,64,256]{2,1,0:T(8,128)(2,1)S(1)}, bf16[2,64,256]{2,1,0:T(8,128)(2,1)S(1)}, u32[]{:S(2)}, u32[]{:S(2)}) %collective-permute-start.50) | collective-permute-done | bytes 65568 | tf_op jit(solution)/shard_map/ppermute | solution.py:28
  115.2 2.5 %collective-permute-done.58.refs_7_ = bf16[4,64,256]{2,1,0:T(8,128)(2,1)S(1)} collective-permute-done((bf16[4,64,256]{2,1,0:T(8,128)(2,1)S(1)}, bf16[4,64,256]{2,1,0:T(8,128)(2,1)S(1)}, u32[]{:S(2)}, u32[]{:S(2)}) %collective-permute-start.58) | collective-permute-done | bytes 131104 | tf_op jit(solution)/shard_map/ppermute | solution.py:39
  119.0 2.6 %matrix.6 = (f32[64,512]{1,0:T(8,128)S(1)}, f32[64,128]{1,0:T(8,128)S(1)}, f32[64,128]{1,0:T(8,128)S(1)}) custom-call(s32[33]{0:T(128)S(1)} %pad_add_fusion.slots, bf16[2,16,256,256]{3,2,1,0:T(8,128)(2,1)S(1)} %get-tuple-element.31.tiles, f32[64,512]{1,0:T(8,128)S(1)} %get-tuple-element.44.vec, f32[64,512]{1,0:T(8,128)S(1)} %get-tuple-element.45.res, ...), custom_call_target="tpu_custom_call" | custom-call | tf_op jit(solution)/shard_map/matrix/pallas_call | solution.py:189
  129.5 2.7 %collective-permute-start.73 = (f32[64,128]{1,0:T(8,128)S(1)}, f32[64,128]{1,0:T(8,128)S(1)}, u32[]{:S(2)}, u32[]{:S(2)}) collective-permute-start(f32[64,128]{1,0:T(8,128)S(1)} %add_add_fusion.1), channel_id=1, source_target_pairs={{0,24},{1,25},{2,26},{3,27},{4,28},{5,29},{6,30},{7,31},{8,16},{9,... | collective-permute-start | bytes 98312 | tf_op jit(solution)/shard_map/ppermute | solution.py:28
  138.3 3.3 %small.5 = (f32[64,64]{1,0:T(8,128)S(1)}, f32[64,512]{1,0:T(8,128)S(1)}, f32[64,512]{1,0:T(8,128)S(1)}, bf16[2,64,256]{2,1,0:T(8,128)(2,1)S(1)}) custom-call(s32[1]{0:T(128)} %bitcast.core, f32[64,128]{1,0:T(8,128)S(1)} %add_add_fusion.mine, f32[64,128]{1,0:T(8,128)S(1)} %collective-permute-done.74.other, f32[64,512]{1,0:T(8,128)S(1)} %get-tuple-element.44.vec, ...), custom_call_target="tpu_custom_call" | custom-call | tf_op jit(solution)/shard_map/small/pallas_call | solution.py:291
  146.1 3.7 %collective-permute-done.75 = bf16[2,64,256]{2,1,0:T(8,128)(2,1)S(1)} collective-permute-done((bf16[2,64,256]{2,1,0:T(8,128)(2,1)S(1)}, bf16[2,64,256]{2,1,0:T(8,128)(2,1)S(1)}, u32[]{:S(2)}, u32[]{:S(2)}) %collective-permute-start.75) | collective-permute-done | bytes 65568 | tf_op jit(solution)/shard_map/ppermute | solution.py:28
  154.1 2.1 %collective-permute-done.80.refs_4_ = bf16[4,64,256]{2,1,0:T(8,128)(2,1)S(1)} collective-permute-done((bf16[4,64,256]{2,1,0:T(8,128)(2,1)S(1)}, bf16[4,64,256]{2,1,0:T(8,128)(2,1)S(1)}, u32[]{:S(2)}, u32[]{:S(2)}) %collective-permute-start.80) | collective-permute-done | bytes 131104 | tf_op jit(solution)/shard_map/ppermute | solution.py:39
  164.5 2.4 %matrix.7 = (f32[64,512]{1,0:T(8,128)S(1)}, f32[32,128]{1,0:T(8,128)S(1)}, f32[32,128]{1,0:T(8,128)S(1)}) custom-call(s32[33]{0:T(128)S(1)} %pad_add_fusion.slots, bf16[2,16,256,256]{3,2,1,0:T(8,128)(2,1)S(1)} %get-tuple-element.31.tiles, f32[64,512]{1,0:T(8,128)S(1)} %get-tuple-element.51.vec, f32[64,512]{1,0:T(8,128)S(1)} %get-tuple-element.52.res, ...), custom_call_target="tpu_custom_call" | custom-call | tf_op jit(solution)/shard_map/matrix/pallas_call | solution.py:189
  176.6 2.1 %collective-permute-start.96 = (f32[32,128]{1,0:T(8,128)S(1)}, f32[32,128]{1,0:T(8,128)S(1)}, u32[]{:S(2)}, u32[]{:S(2)}) collective-permute-start(f32[32,128]{1,0:T(8,128)S(1)} %add_add_fusion.7), channel_id=1, source_target_pairs={{0,8},{1,9},{2,10},{3,11},{4,12},{5,13},{6,14},{7,15},{8,0},{9,1},... | collective-permute-start | bytes 49160 | tf_op jit(solution)/shard_map/ppermute | solution.py:28
  181.9 3.2 %small_last.1 = (f32[64,512]{1,0:T(8,128)}, f32[64,512]{1,0:T(8,128)}) custom-call(s32[1]{0:T(128)} %bitcast.core, f32[32,128]{1,0:T(8,128)S(1)} %add_add_fusion.6.mine, f32[32,128]{1,0:T(8,128)S(1)} %collective-permute-done.99.other, f32[64,512]{1,0:T(8,128)S(1)} %get-tuple-element.51.vec, f32[64,512]{1,0:T(8,128)S(1)} %get-tuple-element.52.res, ...), custom_call_target="tpu_custom_call" | custom-call | tf_op jit(solution)/shard_map/small_last/pallas_call | solution.py:291
  (221 shorter events, 117.0 us)
Async XLA Ops:
  4.6 8.9 %collective-permute-start.1 = (bf16[2,64,256]{2,1,0:T(8,128)(2,1)S(1)}, bf16[2,64,256]{2,1,0:T(8,128)(2,1)S(1)}, u32[]{:S(2)}, u32[]{:S(2)}) collective-permute-start(bf16[2,64,256]{2,1,0:T(8,128)(2,1)S(1)} %get-tuple-element.30), channel_id=1, source_target_pairs={{0,24},{1,25},{2,26},{3,27},{4,28},{5,29},{6,30},{7,31},{8,16},{9,... | collective-permute-start | bytes 196616 | tf_op jit(solution)/shard_map/ppermute | solution.py:28
  7.1 6.4 %collective-permute-start = (bf16[2,64,256]{2,1,0:T(8,128)(2,1)S(1)}, bf16[2,64,256]{2,1,0:T(8,128)(2,1)S(1)}, u32[]{:S(2)}, u32[]{:S(2)}) collective-permute-start(bf16[2,64,256]{2,1,0:T(8,128)(2,1)S(1)} %get-tuple-element.30), channel_id=1, source_target_pairs={{0,16},{1,17},{2,18},{3,19},{4,20},{5,21},{6,22},{7,23},{8,24},{9,... | collective-permute-start | bytes 196616 | tf_op jit(solution)/shard_map/ppermute | solution.py:28
  7.2 9.4 %collective-permute-start.5 = (bf16[4,64,256]{2,1,0:T(8,128)(2,1)S(1)}, bf16[4,64,256]{2,1,0:T(8,128)(2,1)S(1)}, u32[]{:S(2)}, u32[]{:S(2)}) collective-permute-start(bf16[4,64,256]{2,1,0:T(8,128)(2,1)S(1)} %constant_dynamic-update-slice_fusion.2.refs_0_), channel_id=1, source_target_pairs={{0,4},{1,3},{2,6},{3,1},{4,0},{5,7},{6,2},{7,5},{8,12},{9,11},{10,... | collective-permute-start | bytes 393224 | tf_op jit(solution)/shard_map/ppermute | solution.py:39
  8.8 8.3 %collective-permute-start.4 = (bf16[4,64,256]{2,1,0:T(8,128)(2,1)S(1)}, bf16[4,64,256]{2,1,0:T(8,128)(2,1)S(1)}, u32[]{:S(2)}, u32[]{:S(2)}) collective-permute-start(bf16[4,64,256]{2,1,0:T(8,128)(2,1)S(1)} %constant_dynamic-update-slice_fusion.2.refs_0_), channel_id=1, source_target_pairs={{0,2},{1,5},{2,0},{3,7},{4,6},{5,1},{6,4},{7,3},{8,10},{9,13},{10,... | collective-permute-start | bytes 393224 | tf_op jit(solution)/shard_map/ppermute | solution.py:39
  13.6 6.2 %collective-permute-start.6 = (bf16[4,64,256]{2,1,0:T(8,128)(2,1)S(1)}, bf16[4,64,256]{2,1,0:T(8,128)(2,1)S(1)}, u32[]{:S(2)}, u32[]{:S(2)}) collective-permute-start(bf16[4,64,256]{2,1,0:T(8,128)(2,1)S(1)} %constant_dynamic-update-slice_fusion.refs_1_), channel_id=1, source_target_pairs={{0,4},{1,3},{2,6},{3,1},{4,0},{5,7},{6,2},{7,5},{8,12},{9,11},{10,... | collective-permute-start | bytes 393224 | tf_op jit(solution)/shard_map/ppermute | solution.py:39
  22.6 6.7 %collective-permute-start.14 = (bf16[4,64,256]{2,1,0:T(8,128)(2,1)S(1)}, bf16[4,64,256]{2,1,0:T(8,128)(2,1)S(1)}, u32[]{:S(2)}, u32[]{:S(2)}) collective-permute-start(bf16[4,64,256]{2,1,0:T(8,128)(2,1)S(1)} %collective-permute-done.6.refs_5_), channel_id=1, source_target_pairs={{0,1},{1,0},{2,3},{3,2},{4,5},{5,4},{6,7},{7,6},{8,9},{9,8},{10,11... | collective-permute-start | bytes 393224 | tf_op jit(solution)/shard_map/ppermute | solution.py:28
  22.6 6.7 %collective-permute-start.11 = (bf16[4,64,256]{2,1,0:T(8,128)(2,1)S(1)}, bf16[4,64,256]{2,1,0:T(8,128)(2,1)S(1)}, u32[]{:S(2)}, u32[]{:S(2)}) collective-permute-start(bf16[4,64,256]{2,1,0:T(8,128)(2,1)S(1)} %collective-permute-done.4.refs_2_), channel_id=1, source_target_pairs={{0,1},{1,0},{2,3},{3,2},{4,5},{5,4},{6,7},{7,6},{8,9},{9,8},{10,11... | collective-permute-start | bytes 393224 | tf_op jit(solution)/shard_map/ppermute | solution.py:28
  51.9 9.6 %collective-permute-start.27 = (bf16[2,64,256]{2,1,0:T(8,128)(2,1)S(1)}, bf16[2,64,256]{2,1,0:T(8,128)(2,1)S(1)}, u32[]{:S(2)}, u32[]{:S(2)}) collective-permute-start(bf16[2,64,256]{2,1,0:T(8,128)(2,1)S(1)} %get-tuple-element.39), channel_id=1, source_target_pairs={{0,24},{1,25},{2,26},{3,27},{4,28},{5,29},{6,30},{7,31},{8,16},{9,... | collective-permute-start | bytes 196616 | tf_op jit(solution)/shard_map/ppermute | solution.py:28
  53.7 7.8 %collective-permute-start.26 = (bf16[2,64,256]{2,1,0:T(8,128)(2,1)S(1)}, bf16[2,64,256]{2,1,0:T(8,128)(2,1)S(1)}, u32[]{:S(2)}, u32[]{:S(2)}) collective-permute-start(bf16[2,64,256]{2,1,0:T(8,128)(2,1)S(1)} %get-tuple-element.39), channel_id=1, source_target_pairs={{0,16},{1,17},{2,18},{3,19},{4,20},{5,21},{6,22},{7,23},{8,24},{9,... | collective-permute-start | bytes 196616 | tf_op jit(solution)/shard_map/ppermute | solution.py:28
  60.1 6.4 %collective-permute-start.30 = (bf16[4,64,256]{2,1,0:T(8,128)(2,1)S(1)}, bf16[4,64,256]{2,1,0:T(8,128)(2,1)S(1)}, u32[]{:S(2)}, u32[]{:S(2)}) collective-permute-start(bf16[4,64,256]{2,1,0:T(8,128)(2,1)S(1)} %constant_dynamic-update-slice_fusion.4.refs_0_), channel_id=1, source_target_pairs={{0,4},{1,3},{2,6},{3,1},{4,0},{5,7},{6,2},{7,5},{8,12},{9,11},{10,... | collective-permute-start | bytes 393224 | tf_op jit(solution)/shard_map/ppermute | solution.py:39
  61.6 7.3 %collective-permute-start.29 = (bf16[4,64,256]{2,1,0:T(8,128)(2,1)S(1)}, bf16[4,64,256]{2,1,0:T(8,128)(2,1)S(1)}, u32[]{:S(2)}, u32[]{:S(2)}) collective-permute-start(bf16[4,64,256]{2,1,0:T(8,128)(2,1)S(1)} %constant_dynamic-update-slice_fusion.6.refs_1_), channel_id=1, source_target_pairs={{0,2},{1,5},{2,0},{3,7},{4,6},{5,1},{6,4},{7,3},{8,10},{9,13},{10,... | collective-permute-start | bytes 393224 | tf_op jit(solution)/shard_map/ppermute | solution.py:39
  62.5 7.2 %collective-permute-start.35 = (bf16[4,64,256]{2,1,0:T(8,128)(2,1)S(1)}, bf16[4,64,256]{2,1,0:T(8,128)(2,1)S(1)}, u32[]{:S(2)}, u32[]{:S(2)}) collective-permute-start(bf16[4,64,256]{2,1,0:T(8,128)(2,1)S(1)} %constant_dynamic-update-slice_fusion.6.refs_1_), channel_id=1, source_target_pairs={{0,1},{1,0},{2,3},{3,2},{4,5},{5,4},{6,7},{7,6},{8,9},{9,8},{10,11... | collective-permute-start | bytes 393224 | tf_op jit(solution)/shard_map/ppermute | solution.py:28
  62.5 7.2 %collective-permute-start.31 = (bf16[4,64,256]{2,1,0:T(8,128)(2,1)S(1)}, bf16[4,64,256]{2,1,0:T(8,128)(2,1)S(1)}, u32[]{:S(2)}, u32[]{:S(2)}) collective-permute-start(bf16[4,64,256]{2,1,0:T(8,128)(2,1)S(1)} %constant_dynamic-update-slice_fusion.6.refs_1_), channel_id=1, source_target_pairs={{0,4},{1,3},{2,6},{3,1},{4,0},{5,7},{6,2},{7,5},{8,12},{9,11},{10,... | collective-permute-start | bytes 393224 | tf_op jit(solution)/shard_map/ppermute | solution.py:39
  96.2 10.2 %collective-permute-start.52 = (bf16[2,64,256]{2,1,0:T(8,128)(2,1)S(1)}, bf16[2,64,256]{2,1,0:T(8,128)(2,1)S(1)}, u32[]{:S(2)}, u32[]{:S(2)}) collective-permute-start(bf16[2,64,256]{2,1,0:T(8,128)(2,1)S(1)} %get-tuple-element.46), channel_id=1, source_target_pairs={{0,24},{1,25},{2,26},{3,27},{4,28},{5,29},{6,30},{7,31},{8,16},{9,... | collective-permute-start | bytes 196616 | tf_op jit(solution)/shard_map/ppermute | solution.py:28
  98.2 8.2 %collective-permute-start.51 = (bf16[2,64,256]{2,1,0:T(8,128)(2,1)S(1)}, bf16[2,64,256]{2,1,0:T(8,128)(2,1)S(1)}, u32[]{:S(2)}, u32[]{:S(2)}) collective-permute-start(bf16[2,64,256]{2,1,0:T(8,128)(2,1)S(1)} %get-tuple-element.46), channel_id=1, source_target_pairs={{0,16},{1,17},{2,18},{3,19},{4,20},{5,21},{6,22},{7,23},{8,24},{9,... | collective-permute-start | bytes 196616 | tf_op jit(solution)/shard_map/ppermute | solution.py:28
  106.5 6.3 %collective-permute-start.54 = (bf16[4,64,256]{2,1,0:T(8,128)(2,1)S(1)}, bf16[4,64,256]{2,1,0:T(8,128)(2,1)S(1)}, u32[]{:S(2)}, u32[]{:S(2)}) collective-permute-start(bf16[4,64,256]{2,1,0:T(8,128)(2,1)S(1)} %constant_dynamic-update-slice_fusion.10.refs_1_), channel_id=1, source_target_pairs={{0,2},{1,5},{2,0},{3,7},{4,6},{5,1},{6,4},{7,3},{8,10},{9,13},{10,... | collective-permute-start | bytes 393224 | tf_op jit(solution)/shard_map/ppermute | solution.py:39
  107.4 6.6 %collective-permute-start.60 = (bf16[4,64,256]{2,1,0:T(8,128)(2,1)S(1)}, bf16[4,64,256]{2,1,0:T(8,128)(2,1)S(1)}, u32[]{:S(2)}, u32[]{:S(2)}) collective-permute-start(bf16[4,64,256]{2,1,0:T(8,128)(2,1)S(1)} %constant_dynamic-update-slice_fusion.10.refs_1_), channel_id=1, source_target_pairs={{0,1},{1,0},{2,3},{3,2},{4,5},{5,4},{6,7},{7,6},{8,9},{9,8},{10,11... | collective-permute-start | bytes 393224 | tf_op jit(solution)/shard_map/ppermute | solution.py:28
  107.4 6.6 %collective-permute-start.56 = (bf16[4,64,256]{2,1,0:T(8,128)(2,1)S(1)}, bf16[4,64,256]{2,1,0:T(8,128)(2,1)S(1)}, u32[]{:S(2)}, u32[]{:S(2)}) collective-permute-start(bf16[4,64,256]{2,1,0:T(8,128)(2,1)S(1)} %constant_dynamic-update-slice_fusion.10.refs_1_), channel_id=1, source_target_pairs={{0,4},{1,3},{2,6},{3,1},{4,0},{5,7},{6,2},{7,5},{8,12},{9,11},{10,... | collective-permute-start | bytes 393224 | tf_op jit(solution)/shard_map/ppermute | solution.py:39
  141.6 9.8 %collective-permute-start.77 = (bf16[2,64,256]{2,1,0:T(8,128)(2,1)S(1)}, bf16[2,64,256]{2,1,0:T(8,128)(2,1)S(1)}, u32[]{:S(2)}, u32[]{:S(2)}) collective-permute-start(bf16[2,64,256]{2,1,0:T(8,128)(2,1)S(1)} %get-tuple-element.53), channel_id=1, source_target_pairs={{0,24},{1,25},{2,26},{3,27},{4,28},{5,29},{6,30},{7,31},{8,16},{9,... | collective-permute-start | bytes 196616 | tf_op jit(solution)/shard_map/ppermute | solution.py:28
  143.5 7.9 %collective-permute-start.76 = (bf16[2,64,256]{2,1,0:T(8,128)(2,1)S(1)}, bf16[2,64,256]{2,1,0:T(8,128)(2,1)S(1)}, u32[]{:S(2)}, u32[]{:S(2)}) collective-permute-start(bf16[2,64,256]{2,1,0:T(8,128)(2,1)S(1)} %get-tuple-element.53), channel_id=1, source_target_pairs={{0,16},{1,17},{2,18},{3,19},{4,20},{5,21},{6,22},{7,23},{8,24},{9,... | collective-permute-start | bytes 196616 | tf_op jit(solution)/shard_map/ppermute | solution.py:28
  149.8 6.4 %collective-permute-start.80 = (bf16[4,64,256]{2,1,0:T(8,128)(2,1)S(1)}, bf16[4,64,256]{2,1,0:T(8,128)(2,1)S(1)}, u32[]{:S(2)}, u32[]{:S(2)}) collective-permute-start(bf16[4,64,256]{2,1,0:T(8,128)(2,1)S(1)} %constant_dynamic-update-slice_fusion.12.refs_0_), channel_id=1, source_target_pairs={{0,4},{1,3},{2,6},{3,1},{4,0},{5,7},{6,2},{7,5},{8,12},{9,11},{10,... | collective-permute-start | bytes 393224 | tf_op jit(solution)/shard_map/ppermute | solution.py:39
  151.5 6.8 %collective-permute-start.79 = (bf16[4,64,256]{2,1,0:T(8,128)(2,1)S(1)}, bf16[4,64,256]{2,1,0:T(8,128)(2,1)S(1)}, u32[]{:S(2)}, u32[]{:S(2)}) collective-permute-start(bf16[4,64,256]{2,1,0:T(8,128)(2,1)S(1)} %constant_dynamic-update-slice_fusion.14.refs_1_), channel_id=1, source_target_pairs={{0,2},{1,5},{2,0},{3,7},{4,6},{5,1},{6,4},{7,3},{8,10},{9,13},{10,... | collective-permute-start | bytes 393224 | tf_op jit(solution)/shard_map/ppermute | solution.py:39
  152.9 6.5 %collective-permute-start.85 = (bf16[4,64,256]{2,1,0:T(8,128)(2,1)S(1)}, bf16[4,64,256]{2,1,0:T(8,128)(2,1)S(1)}, u32[]{:S(2)}, u32[]{:S(2)}) collective-permute-start(bf16[4,64,256]{2,1,0:T(8,128)(2,1)S(1)} %constant_dynamic-update-slice_fusion.14.refs_1_), channel_id=1, source_target_pairs={{0,1},{1,0},{2,3},{3,2},{4,5},{5,4},{6,7},{7,6},{8,9},{9,8},{10,11... | collective-permute-start | bytes 393224 | tf_op jit(solution)/shard_map/ppermute | solution.py:28
  152.9 6.5 %collective-permute-start.81 = (bf16[4,64,256]{2,1,0:T(8,128)(2,1)S(1)}, bf16[4,64,256]{2,1,0:T(8,128)(2,1)S(1)}, u32[]{:S(2)}, u32[]{:S(2)}) collective-permute-start(bf16[4,64,256]{2,1,0:T(8,128)(2,1)S(1)} %constant_dynamic-update-slice_fusion.14.refs_1_), channel_id=1, source_target_pairs={{0,4},{1,3},{2,6},{3,1},{4,0},{5,7},{6,2},{7,5},{8,12},{9,11},{10,... | collective-permute-start | bytes 393224 | tf_op jit(solution)/shard_map/ppermute | solution.py:39
  (76 other events, 308.1 us)
